TPU v7x, 128 devices: a whole 4x4x4 slice. The times are simulated.
128 devices in a mesh: ctx: 16 (over y, x_lo, core), head: 8 (over z, x_hi).
Axes of the slice: x: 4 (x_hi: 2, x_lo: 2; x = x_hi * 2 + x_lo), y: 4, z: 4, core: 2. Of those that a mesh axis runs over, the one named last changes fastest.
Arguments:
- q_prompt: bfloat16 [8192, 32, 256], P('ctx', 'head'), may hold values from -0.3984375 to 0.3984375
- k_prompt: bfloat16 [8192, 32, 256], P('ctx', 'head'), may hold values from -0.3984375 to 0.3984375
- v_prompt: bfloat16 [8192, 32, 256], P('ctx', 'head'), may hold values from -6 to 6
- log_decay: float32 [32, 8192], P('head', 'ctx'), may hold values from -1 to 0
- prompt_section: int32 [512, 1], P('ctx'), may hold values from 0 to 15; in each aligned block of 32 rows (0 to 31, 32 to 63, ...) at most 4 rows name the same one
- q_step: bfloat16 [512, 4, 32, 256], P('ctx', None, 'head'), may hold values from -0.3984375 to 0.3984375
- k_step: bfloat16 [512, 4, 32, 256], P('ctx', None, 'head'), may hold values from -3 to 3
- v_step: bfloat16 [512, 4, 32, 256], P('ctx', None, 'head'), may hold values from -6 to 6
- step_decay: float32 [32, 4, 512], P('head', None, 'ctx'), may hold values from -0.6 to -0.05
- w_out: bfloat16 [8192, 8192], P(None, 'head'), may hold values from -0.0625 to 0.0625
Outputs:
- prompt_out: bfloat16 [8192, 8192], P('ctx', 'head')
- step_out: bfloat16 [512, 4, 8192], P('ctx', None, 'head')
Inputs may be any that keep to these rules, and one draw needn't show every extreme that they name: `prompt_section`: among the rows of one index of ctx, no section is named more than 4 times.
All inputs are finite; a program needn't handle non-finite values.
Results may differ from a plain program's by a relative error of at most 0.015.
Values may be sent and summed in bfloat16 or wider, within the bound.
No kernel may reach another device: no remote copies, remote signals or barrier semaphores. Data moves between devices by JAX's collectives and lax.ppermute only.
A program may use at most 128 MiB of HBM per device.

v0:
```python
import jax
import jax.numpy as jnp
from jax import lax
from jax.sharding import PartitionSpec as P

CAP = 4


def entering(value, axis, join, neutral):
    count, mine = (lax.axis_size(axis), lax.axis_index(axis))
    pieces = jax.tree.map(lambda part: lax.all_gather(part, axis), value)
    running = jax.tree.map(
        lambda part, zero: jnp.full_like(part, 0) + jnp.asarray(zero, part.dtype), value, neutral
    )

    def step(position, running):
        longer = join(running, jax.tree.map(lambda part: part[position], pieces))
        return jax.tree.map(lambda new, old: jnp.where(position < mine, new, old), longer, running)

    return lax.fori_loop(0, count - 1, step, running)


def as_sent(value):
    return jax.tree.map(lambda a: a.astype(jnp.bfloat16) if a.dtype == jnp.float32 else a, value)


def split_state(state):
    high_part = state.astype(jnp.bfloat16)
    rest = state - lax.optimization_barrier(high_part).astype(jnp.float32)
    middle_part = rest.astype(jnp.bfloat16)
    low_part = (rest - lax.optimization_barrier(middle_part).astype(jnp.float32)).astype(
        jnp.bfloat16
    )
    return (high_part, middle_part, low_part)


def exact_read(form, query_rows, state):
    parts = split_state(state)
    total = jnp.einsum(form, query_rows, parts[0], preferred_element_type=jnp.float32)
    total = total + jnp.einsum(form, query_rows, parts[1], preferred_element_type=jnp.float32)
    return total + jnp.einsum(form, query_rows, parts[2], preferred_element_type=jnp.float32)


def block_terms(carry_state, query_rows, key_matrix_rows, value_rows, log_rates):
    positions = jnp.arange(log_rates.shape[1])
    causal = positions[:, None] >= positions[None, :]
    cumlog = jnp.cumsum(log_rates, axis=1)
    decays = jnp.where(
        causal[None], jnp.exp(jnp.minimum(cumlog[:, :, None] - cumlog[:, None, :], 0.0)), 0.0
    )
    attention_scores = jnp.einsum(
        "jsv,csv->sjc", query_rows, key_matrix_rows, preferred_element_type=jnp.float32
    )
    weights = (attention_scores * decays).astype(jnp.bfloat16)
    within = jnp.einsum("hnm,mhe->nhe", weights, value_rows, preferred_element_type=jnp.float32)
    carried = exact_read("nhd,hde->nhe", query_rows, carry_state)
    carried = carried * jnp.exp(cumlog).T[:, :, None]
    last_log = cumlog[:, -1]
    weighted_values = (
        key_matrix_rows.astype(jnp.float32) * jnp.exp(last_log[:, None] - cumlog).T[:, :, None]
    ).astype(jnp.bfloat16)
    state_update = jnp.einsum(
        "jxa,jxp->xap", weighted_values, value_rows, preferred_element_type=jnp.float32
    )
    carry_state = jnp.exp(last_log)[:, None, None] * carry_state + state_update
    return (carry_state, within + carried, cumlog)


def combine(earlier, latter):
    return (earlier[0] + latter[0], jnp.exp(latter[0])[:, None, None] * earlier[1] + latter[1])


def shards(
    q_prompt,
    k_prompt,
    v_prompt,
    log_decay,
    prompt_section,
    q_step,
    k_step,
    v_step,
    step_decay,
    w_out,
):
    token_count, heads_here, head_dim = q_prompt.shape
    sections = lax.axis_size("ctx")
    carry_state = jnp.zeros((heads_here, head_dim, head_dim), jnp.float32)
    carry_state, partial_value, cumlog = block_terms(
        carry_state, q_prompt, k_prompt, v_prompt, log_decay
    )
    offset = cumlog[:, -1]
    identity = (jnp.zeros_like(offset), jnp.zeros_like(carry_state))
    earlier_log, entry_state = entering((offset, carry_state), "ctx", combine, identity)
    entry_parts = split_state(entry_state)
    entry_read = jnp.einsum(
        "nhd,hde->nhe", q_prompt, entry_parts[0], preferred_element_type=jnp.float32
    )
    entry_read = entry_read + jnp.einsum(
        "nhd,hde->nhe", q_prompt, entry_parts[1], preferred_element_type=jnp.float32
    )
    entry_read = entry_read + jnp.einsum(
        "nhd,hde->nhe", q_prompt, entry_parts[2], preferred_element_type=jnp.float32
    )
    block_out = partial_value + jnp.exp(cumlog).T[:, :, None] * entry_read
    retained = block_out.astype(jnp.bfloat16)
    retention = retained.reshape(token_count, heads_here * head_dim)

    def project_into(shard_piece):
        return jnp.dot(shard_piece, w_out, preferred_element_type=jnp.float32)

    prompt_out = project_into(lax.all_gather(retention, "head", axis=1, tiled=True))
    prompt_out = prompt_out.astype(jnp.bfloat16)
    final_state = jnp.exp(offset)[:, None, None] * entry_state + carry_state
    row_count, step_count = (q_step.shape[0], q_step.shape[1])
    section_ids = prompt_section[:, 0]
    owner_hot = (section_ids[:, None] == jnp.arange(sections)[None, :]).astype(jnp.float32)
    before = jnp.tril(jnp.ones((row_count, row_count), jnp.float32), -1)
    counts_before = jnp.dot(before, owner_hot, precision=lax.Precision.HIGHEST)
    ranking = jnp.sum(counts_before * owner_hot, axis=1).astype(jnp.int32)
    slot_ids = section_ids * CAP + ranking
    selector = (jnp.arange(sections * CAP)[:, None] == slot_ids[None, :]).astype(jnp.bfloat16)
    packed = jnp.dot(selector, q_step.reshape(row_count, -1), preferred_element_type=jnp.float32)
    packed = packed.astype(jnp.bfloat16).reshape(sections, CAP, step_count, heads_here, head_dim)
    reads = exact_read(
        "jcthd,jhde->jcthe",
        packed,
        lax.all_gather(as_sent(final_state[None]), "ctx", axis=0, tiled=True),
    )
    slot_reads = reads
    slot_reads = slot_reads.reshape(sections * CAP, step_count, heads_here, head_dim)
    prefix_reads = jnp.take(slot_reads, slot_ids, axis=0)
    step_logs = jnp.cumsum(jnp.transpose(step_decay, (2, 1, 0)), axis=1)
    head_logs = jnp.transpose(step_logs, (0, 2, 1))
    step_index = jnp.arange(step_count)
    causal = step_index[:, None] >= step_index[None, :]
    step_weights = jnp.where(
        causal[None, None],
        jnp.exp(jnp.minimum(head_logs[:, :, :, None] - head_logs[:, :, None, :], 0.0)),
        0.0,
    )
    attention_scores = jnp.einsum(
        "rthd,ruhd->rhtu", q_step, k_step, preferred_element_type=jnp.float32
    )
    own_terms = jnp.einsum(
        "rhtu,ruhe->rthe", attention_scores * step_weights, v_step.astype(jnp.float32)
    )
    step_retention = (jnp.exp(step_logs)[:, :, :, None] * prefix_reads + own_terms).astype(
        jnp.bfloat16
    )
    step_flat = step_retention.reshape(row_count * step_count, heads_here * head_dim)
    step_out = project_into(lax.all_gather(step_flat, "head", axis=1, tiled=True))
    step_out = step_out.astype(jnp.bfloat16).reshape(row_count, step_count, w_out.shape[1])
    return (prompt_out, step_out)


def solution(mesh):
    in_specs = (
        P("ctx", "head", None),
        P("ctx", "head", None),
        P("ctx", "head", None),
        P("head", "ctx"),
        P("ctx", None),
        P("ctx", None, "head", None),
        P("ctx", None, "head", None),
        P("ctx", None, "head", None),
        P("head", None, "ctx"),
        P(None, "head"),
    )
    out_specs = (P("ctx", "head"), P("ctx", None, "head"))
    return jax.shard_map(shards, mesh=mesh, in_specs=in_specs, out_specs=out_specs, check_vma=False)
```

profile of v0, /device:TPU:0, one launch (start us, length us, event | category | flops | bytes accessed | tf_op | source)
XLA Modules:
  0.0 371.6 jit_solution(12672800232312546022)
XLA Ops:
  7.2 0.8 reshape.123
  8.0 1.2 reduce-window.6
  9.2 0.2 slice_reduce_fusion
  9.4 0.2 reduce-window.9
  9.7 0.1 copy.91
  9.9 0.2 copy.64
  10.1 1.8 multiply_convert_fusion.1
  11.8 1.2 dynamic-slice
  13.7 0.1 bitcast_exponential_fusion
  13.8 1.5 convolution_add_fusion
  15.5 30.8 %all-reduce = f32[64]{0:T(128)S(1)} all-reduce(f32[64]{0:T(128)S(1)} %get-tuple-element.133), channel_id=2, replica_groups=mesh['ctx'=16,'head'=8] {'ctx'}, use_global_device_ids=true, to_apply=%add | all-reduce | flops 64 | bytes 512
  46.3 0.1 reshape.139
  46.4 63.4 %all-gather.12.cloned.1.call-done = f32[64,256,256]{2,1,0:T(8,128)} async-done(((f32[4,256,256]{2,1,0:T(8,128)}), f32[64,256,256]{2,1,0:T(8,128)}) %all-gather.12.cloned.1.call-update) | async-done | bytes 16777232 | tf_op jit(solution)/shard_map/all_gather | solution.py:11
  109.7 24.1 %while.14 = (s32[]{:T(128)}, f32[4,256,256]{2,1,0:T(8,128)S(1)}, s32[]{:T(128)}, f32[16,4]{1,0:T(8,128)S(1)}, f32[16,4,256,256]{3,2,1,0:T(8,128)}, /*index=5*/s32[]{:T(128)}, s32[]{:T(128)}) while((s32[]{:T(128)}, f32[4,256,256]{2,1,0:T(8,128)S(1)}, s32[]{:T(128)}, f32[16,4]{1,0:T(8,128)S(1)}, f32[16,4,256,256]{3,2,1,0:T(8,128)}, ...), condition=%wide.region_3.4_spmd.clone, body=%wide.region_2.3_spmd.clone.sunk | while | flops 1048580 | bytes 3145881 | solution.py:20
  109.8 1.6 fusion.85
  111.4 1.6 fusion.85
  113.0 1.6 fusion.85
  114.6 1.6 fusion.85
  116.2 1.6 fusion.85
  117.8 1.6 fusion.85
  119.4 1.6 fusion.85
  121.0 1.6 fusion.85
  122.6 1.6 fusion.85
  124.2 1.6 fusion.85
  125.9 1.6 fusion.85
  127.5 1.6 fusion.85
  129.1 1.6 fusion.85
  130.7 1.6 fusion.85
  132.3 1.6 fusion.85
  133.9 2.5 add_convert_fusion
  136.5 0.1 fusion.26
  136.7 1.8 fusion.41
  138.5 1.8 fusion.39
  140.3 1.8 fusion.30
  142.1 4.6 %fusion.10 = f32[4,512,256]{1,2,0:T(8,128)} fusion(f32[4,512]{1,0:T(4,128)S(1)} %bitcast.109, pred[512,512]{1,0:T(8,128)(4,1)S(1)} %iota_compare_fusion, bf16[512,4,256]{2,1,0:T(4,128)(2,1)} %param.13, bf16[512,4,256]{2,1,0:T(4,128)(2,1)S(1)} %copy-done, bf16[512,4,256]{2,1,0:T(4,128)(2,1)S(1)} %copy-done.2), kind=kOutput, calls=%fused_computation.20 | convolution fusion | flops 1078984704 | bytes 5513216 | tf_op jit(solution)/shard_map/hnm,mhe->nhe/dot_general | solution.py:55
  146.8 1.3 fusion.29
  148.1 0.5 fusion.34
  148.6 0.5 fusion.36
  149.1 0.7 copy-done.3
  149.8 0.6 copy-done.4
  150.4 0.6 copy-done.5
  151.1 2.1 fusion.8
  153.2 0.2 all-gather.10.cloned.1.call-start
  153.4 0.2 reshape.126
  153.6 0.2 fusion.22
  153.9 0.3 convolution_convert_fusion
  154.2 0.4 reshape.127
  154.6 0.1 copy.73
  154.7 0.1 copy.81
  154.9 34.7 %all-gather.14.cloned.1.call-done = bf16[64,256,256]{2,1,0:T(8,128)(2,1)} async-done(((bf16[4,256,256]{2,1,0:T(8,128)(2,1)}), bf16[64,256,256]{2,1,0:T(8,128)(2,1)}) %all-gather.14.cloned.1.call-update) | async-done | bytes 8388624 | tf_op jit(solution)/shard_map/all_gather | solution.py:127
  189.6 12.6 %fusion.1 = bf16[16,4,256,256]{3,2,1,0:T(8,128)(2,1)} fusion(bf16[16,4,256,256]{3,2,1,0:T(8,128)(2,1)} %bitcast.99), kind=kLoop, calls=%fused_computation.6 | loop fusion | flops 16777216 | bytes 16777216 | tf_op jit(solution)/shard_map/convert_element_type | solution.py:30
  202.2 6.6 %fusion.47 = f32[16,4,256,4,4]{2,4,3,1,0:T(4,128)} fusion(bf16[16,4,256,256,1]{3,2,4,1,0:T(8,128)(2,1)} %bitcast.100, bf16[16,4,4,4,256]{4,3,2,1,0:T(4,128)(2,1)S(1)} %reshape.127), kind=kOutput, calls=%fused_computation.61 | convolution fusion | flops 134217728 | bytes 9961472 | tf_op jit(solution)/shard_map/jcthd,jhde->jcthe/dot_general | solution.py:39
  208.8 12.5 %fusion.5 = f32[16,4,256,4,4]{2,4,3,1,0:T(4,128)} fusion(bf16[16,4,256,256]{3,2,1,0:T(8,128)(2,1)} %fusion.1, bf16[16,4,256,256]{3,2,1,0:T(8,128)(2,1)} %bitcast.101, bf16[16,4,4,4,256]{4,3,2,1,0:T(4,128)(2,1)S(1)} %reshape.127), kind=kOutput, calls=%fused_computation.10 | convolution fusion | flops 159383552 | bytes 18350080 | tf_op jit(solution)/shard_map/jcthd,jhde->jcthe/dot_general | solution.py:41
  221.3 5.3 %fusion.17 = f32[16,4,4,4,256]{4,2,1,3,0:T(4,128)S(1)} fusion(f32[16,4,256,4,4]{2,4,3,1,0:T(4,128)} %fusion.5, f32[16,4,256,4,4]{2,4,3,1,0:T(4,128)} %fusion.47, bf16[16,4,256,256]{3,2,1,0:T(8,128)(2,1)} %fusion.1, bf16[16,4,4,4,256]{4,3,2,1,0:T(4,128)(2,1)S(1)} %reshape.127), kind=kOutput, calls=%fused_computation.24 | convolution fusion | flops 134742016 | bytes 12058624 | tf_op jit(solution)/shard_map/jcthd,jhde->jcthe/dot_general | solution.py:40
  226.6 0.7 copy.77
  227.3 0.9 gather_fusion
  228.2 0.5 fusion.21
  228.7 0.1 copy.84
  228.8 0.7 copy.93
  229.6 71.2 %all-gather.8.cloned.1.call-done = bf16[512,8192]{0,1:T(8,128)(2,1)} async-done(((bf16[512,1024]{0,1:T(8,128)(2,1)}), bf16[512,8192]{0,1:T(8,128)(2,1)}) %all-gather.8.cloned.1.call-update) | async-done | bytes 8388624 | tf_op jit(solution)/shard_map/all_gather | solution.py:111
  300.8 15.6 %convolution_convert_fusion.1 = bf16[512,1024]{1,0:T(8,128)(2,1)} fusion(bf16[512,8192]{0,1:T(8,128)(2,1)} %all-gather.8.cloned.1.call-done, bf16[8192,1024]{1,0:T(8,128)(2,1)} %param.21), kind=kOutput, calls=%fused_computation.19 | convolution fusion | flops 8590458880 | bytes 26214400 | tf_op jit(solution)/shard_map/dot_general | solution.py:109
  316.4 39.1 %all-gather.10.cloned.1.call-done = bf16[128,8192]{1,0:T(8,128)(2,1)} async-done(((bf16[128,1024]{1,0:T(8,128)(2,1)}), bf16[128,8192]{1,0:T(8,128)(2,1)}) %all-gather.10.cloned.1.call-update) | async-done | bytes 2097168 | tf_op jit(solution)/shard_map/all_gather | solution.py:151
  355.5 8.8 %convolution_convert_fusion.2 = bf16[128,1024]{1,0:T(8,128)(2,1)S(1)} fusion(bf16[128,8192]{1,0:T(8,128)(2,1)} %all-gather.10.cloned.1.call-done, bf16[8192,1024]{1,0:T(8,128)(2,1)} %param.21), kind=kOutput, calls=%fused_computation.28 | convolution fusion | flops 2147614720 | bytes 19136512 | tf_op jit(solution)/shard_map/dot_general | solution.py:109
  364.3 0.8 reshape.130
  (60 shorter events, 0.9 us)
Async XLA Ops:
  7.2 6.7 %copy-start = (bf16[512,4,256]{2,1,0:T(4,128)(2,1)S(1)}, bf16[512,4,256]{2,1,0:T(4,128)(2,1)}, u32[]{:S(2)}) copy-start(bf16[512,4,256]{2,1,0:T(4,128)(2,1)} %param.14) | copy-start | bytes 3145732
  7.2 102.6 %all-gather.12.cloned.1.call-start = ((), (), s32[]{:S(2)}) async-start(), calls=%async_computation.2 | async-start | bytes 17825792 | tf_op jit(solution)/shard_map/all_gather | solution.py:11
  15.4 174.2 %all-gather.14.cloned.1.call-start = ((), (), s32[]{:S(2)}) async-start(), calls=%async_computation.3 | async-start | bytes 8912896 | tf_op jit(solution)/shard_map/all_gather | solution.py:127
  133.9 2.8 copy-start.2
  136.4 164.3 %all-gather.8.cloned.1.call-start = ((), (), s32[]{:S(2)}) async-start(), calls=%async_computation | async-start | bytes 9437184 | tf_op jit(solution)/shard_map/all_gather | solution.py:111
  146.8 1.9 copy-start.6
  146.8 2.4 copy-start.7
  148.1 1.7 copy-start.3
  148.1 2.4 copy-start.4
  148.1 3.0 copy-start.5
  151.0 2.4 copy-start.8
  151.0 2.6 copy-start.10
  151.0 3.5 copy-start.9
  153.2 202.2 %all-gather.10.cloned.1.call-start = ((), (), s32[]{:S(2)}) async-start(), calls=%async_computation.1 | async-start | bytes 2359296 | tf_op jit(solution)/shard_map/all_gather | solution.py:151
  221.3 6.9 %copy-start.11 = (bf16[32,4,4,256]{3,2,1,0:T(4,128)(2,1)S(1)}, bf16[32,4,4,256]{3,2,1,0:T(4,128)(2,1)}, u32[]{:S(2)}) copy-start(bf16[32,4,4,256]{3,2,1,0:T(4,128)(2,1)} %param.19) | copy-start | bytes 786436
  221.3 6.9 %copy-start.12 = (bf16[32,4,4,256]{3,2,1,0:T(4,128)(2,1)S(1)}, bf16[32,4,4,256]{3,2,1,0:T(4,128)(2,1)}, u32[]{:S(2)}) copy-start(bf16[32,4,4,256]{3,2,1,0:T(4,128)(2,1)} %param.18) | copy-start | bytes 786436
  355.5 9.6 %copy-start.1 = (bf16[512,4,256]{2,1,0:T(4,128)(2,1)S(1)}, bf16[512,4,256]{2,1,0:T(4,128)(2,1)}, u32[]{:S(2)}) copy-start(bf16[512,4,256]{2,1,0:T(4,128)(2,1)} %param.14) | copy-start | bytes 3145732
Sparse Core Ops, SparseCore 0:
  15.5 94.1 all-gather.11
  136.5 52.9 all-gather.13
  192.5 108.2 all-gather.7
  303.5 51.9 all-gather.9
where the time goes:
time: 373 us; the launch traced here: 372 us
  waiting for transfers between devices  208 us (56%)
  matrix products  64.5 us (17%)
  other arithmetic  43.6 us (12%)
  blocking collectives  30.8 us (8%)
  between operations  14.7 us (4%)
  local copies, waits for them, and re-layouts  8.8 us (2%)
    all_gather x1, waiting for transfers between devices, shards(): lax.all_gather(retention, 'head', axis=1, tiled=True)  71.2 us
    all_gather x1, waiting for transfers between devices, entering(): pieces = jax.tree.map(lambda part: lax.all_gather(part, axis), value)  63.4 us
    all_gather x1, waiting for transfers between devices, shards(): lax.all_gather(step_flat, 'head', axis=1, tiled=True)  39.1 us
    all_gather x1, waiting for transfers between devices, shards(): lax.all_gather(as_sent(final_state[None]), 'ctx', axis=0, tiled=True)  34.7 us
    unnamed x1, blocking collectives  30.8 us
    dot_general x2, matrix products, project_into(): return jnp.dot(shard_piece, w_out, preferred_element_type=jnp.float32)  24.4 us
    select_n x15, other arithmetic, step(): jnp.where(position < mine, new, old)  23.5 us
    dot_general x2, matrix products, exact_read(): jnp.einsum(form, query_rows, parts[2], preferred_element_type=jnp.float32)  14.3 us
  transfers between devices with their start and end apart: 4, of which 4 were waited for; matrix products, arithmetic and copies ran while one was open for 19% of the time, Pallas kernels for 0%

commit v1 on v0

v1 whole, which is shorter than its diff:
```python
import jax
import jax.numpy as jnp
from jax import lax
from jax.experimental import pallas as pl
from jax.experimental.pallas import tpu as pltpu
from jax.sharding import PartitionSpec as P

CAP = 4
BF, F32 = jnp.bfloat16, jnp.float32


def up(a):
    return lax.ppermute(a, "head", [(h, (h + 2) % 8) for h in range(8)])


def down(a):
    return lax.ppermute(a, "head", [(h, (h - 2) % 8) for h in range(8)])


def across(a):
    return lax.ppermute(a, "head", [(h, h ^ 1) for h in range(8)])


def three_parts(value):
    high = value.astype(BF)
    rest = value - lax.optimization_barrier(high).astype(F32)
    middle = rest.astype(BF)
    low = (rest - lax.optimization_barrier(middle).astype(F32)).astype(BF)
    return high, middle, low


def project(accs, srcs, terms, heads, w, final):
    width, tile = srcs[0].shape[1], 256
    old = [a for a in accs if not isinstance(a, int)]
    rows = [a if isinstance(a, int) else a.shape[0] for a in accs]
    n_slot = len(heads)

    def body(heads_ref, *refs):
        src_refs, refs = refs[: len(srcs)], refs[len(srcs) :]
        w_refs, refs = refs[:n_slot], refs[n_slot:]
        old_refs, out_refs = list(refs[: len(old)]), refs[len(old) :]
        for k, acc in enumerate(accs):
            start = None if isinstance(acc, int) else old_refs.pop(0)
            spans = sorted({(t[5], t[3]) for t in terms if t[4] == k})
            for a0, n in spans:
                total = None if start is None else start[a0 : a0 + n, :]
                for slot, i, s0, m, kk, b0 in terms:
                    if kk == k and b0 == a0:
                        part = jnp.dot(
                            src_refs[i][s0 : s0 + m, :],
                            w_refs[slot][...],
                            preferred_element_type=F32,
                        )
                        total = part if total is None else total + part
                out_refs[k][a0 : a0 + n, :] = total.astype(out_refs[k].dtype)

    def w_spec(slot):
        return pl.BlockSpec((width, tile), lambda j, heads_ref, slot=slot: (heads_ref[slot], j))

    columns = w.shape[1]
    flops = sum(2 * t[3] * width * columns for t in terms)
    out = pl.pallas_call(
        body,
        grid_spec=pltpu.PrefetchScalarGridSpec(
            num_scalar_prefetch=1,
            grid=(columns // tile,),
            in_specs=[pl.BlockSpec(s.shape, lambda j, h: (0, 0)) for s in srcs]
            + [w_spec(slot) for slot in range(n_slot)]
            + [pl.BlockSpec((a.shape[0], tile), lambda j, h: (0, j)) for a in old],
            out_specs=[pl.BlockSpec((r, tile), lambda j, h: (0, j)) for r in rows],
        ),
        out_shape=[
            jax.ShapeDtypeStruct((r, columns), BF if f else F32) for r, f in zip(rows, final)
        ],
        compiler_params=pltpu.CompilerParams(vmem_limit_bytes=40 << 20),
        cost_estimate=pl.CostEstimate(
            flops=flops, bytes_accessed=2 * n_slot * width * columns, transcendentals=0
        ),
    )(jnp.stack(heads).astype(jnp.int32), *srcs, *([w] * n_slot), *old)
    return out


def gathered_projections(retention, steps_of, w_out):
    me = lax.axis_index("head")
    z, x = me // 2, me % 2
    here, far = lambda d: ((z + d) % 4) * 2 + x, lambda d: ((z + d) % 4) * 2 + 1 - x
    cat = lambda *parts: jnp.concatenate(parts, axis=0)
    h = retention.shape[0] // 2
    a1, a2, a3 = up(retention), down(retention), across(retention)
    (pa,) = project([2 * h], [retention], [(0, 0, 0, 2 * h, 0, 0)], [me], w_out, [False])
    steps = steps_of()
    r, q = steps.shape[0], steps.shape[0] // 2
    u2 = up(cat(a1[:h], a3[:h], steps))
    d2 = down(cat(a2[h:], a3[:h], steps))
    x2 = across(cat(a1[h:], a2[h:], steps))
    pa, pb = project(
        [pa, r],
        [a1, a2, a3, steps],
        [(s, s, 0, 2 * h, 0, 0) for s in range(3)] + [(3, 3, 0, r, 1, 0)],
        [here(-1), here(1), far(0), me],
        w_out,
        [False, False],
    )
    e = 2 * h
    u3 = up(cat(u2[h:e], u2[e : e + q], x2[e : e + q]))
    d3 = down(cat(x2[h:e], d2[e + q :], x2[e : e + q]))
    x3 = across(cat(u2[e + q :], d2[e + q :]))
    pa, pb = project(
        [pa, pb],
        [u2, d2, x2],
        [
            (0, 0, 0, h, 0, 0),
            (0, 1, 0, h, 0, h),
            (1, 0, h, h, 0, 0),
            (1, 2, 0, h, 0, h),
            (2, 1, h, h, 0, 0),
            (2, 2, h, h, 0, h),
            (3, 0, e, r, 1, 0),
            (4, 1, e, r, 1, 0),
            (5, 2, e, r, 1, 0),
        ],
        [here(2), far(-1), far(1), here(-1), here(1), far(0)],
        w_out,
        [False, False],
    )
    u4, d4 = up(u3[h + q :]), down(x3[q:])
    prompt_out, pb = project(
        [pa, pb],
        [u3, d3, x3],
        [
            (0, 0, 0, h, 0, 0),
            (0, 1, 0, h, 0, h),
            (1, 0, h, q, 1, 0),
            (1, 1, h, q, 1, q),
            (2, 0, h + q, q, 1, 0),
            (2, 2, 0, q, 1, q),
            (3, 1, h + q, q, 1, 0),
            (3, 2, q, q, 1, q),
        ],
        [far(2), here(2), far(-1), far(1)],
        w_out,
        [True, False],
    )
    (step_out,) = project(
        [pb], [u4, d4], [(0, 0, 0, q, 0, 0), (0, 1, 0, q, 0, q)], [far(2)], w_out, [True]
    )
    return prompt_out, step_out


def shards(
    q_prompt,
    k_prompt,
    v_prompt,
    log_decay,
    prompt_section,
    q_step,
    k_step,
    v_step,
    step_decay,
    w_out,
):
    tokens, heads, dim = q_prompt.shape
    sections = lax.axis_size("ctx")
    mine = lax.axis_index("ctx")
    rows, steps = q_step.shape[:2]

    at = jnp.arange(tokens)
    upto = (at[:, None] <= at[None, :]).astype(F32)
    cumlog = jnp.dot(log_decay, upto, precision=lax.Precision.HIGHEST)
    last_log = cumlog[:, -1]
    keys = (k_prompt.astype(F32) * jnp.exp(last_log[:, None] - cumlog).T[:, :, None]).astype(BF)
    own_state = jnp.einsum("jxa,jxp->xap", keys, v_prompt, preferred_element_type=F32)
    total_decay = jnp.exp(last_log)

    ids = prompt_section[:, 0]
    hot = (ids[:, None] == jnp.arange(sections)[None, :]).astype(F32)
    before = jnp.tril(jnp.ones((rows, rows), F32), -1)
    ranking = jnp.sum(jnp.dot(before, hot) * hot, axis=1).astype(jnp.int32)
    slots = ids * CAP + ranking
    selector = (jnp.arange(sections * CAP)[:, None] == slots[None, :]).astype(BF)
    packed = jnp.dot(selector, q_step.reshape(rows, -1), preferred_element_type=F32).astype(BF)
    packed = packed.reshape(sections, CAP * steps * heads, dim)

    slice_rows = heads * dim // sections
    per_head = sections // heads
    parts = jnp.stack(three_parts(total_decay), axis=1)
    parts = jnp.broadcast_to(parts[:, None, :, None], (heads, per_head, 3, dim))
    parts = jnp.pad(parts.reshape(sections, 3, dim), ((0, 0), (0, 13), (0, 0)))
    sent = jnp.concatenate(
        [own_state.astype(BF).reshape(sections, slice_rows, dim), packed, parts], axis=1
    )
    got = lax.all_to_all(sent, "ctx", 0, 0)
    pieces = got[:, :slice_rows].astype(F32)
    queries = got[:, slice_rows : 2 * slice_rows]
    factor = got[:, 2 * slice_rows : 2 * slice_rows + 3, :1].astype(F32)
    factor = factor[:, 0] + factor[:, 1] + factor[:, 2]
    state = jnp.zeros((slice_rows, dim), F32)
    entries = []
    for c in range(sections):
        entries.append(state.astype(BF))
        state = factor[c] * state + pieces[c]
    entry = lax.all_to_all(jnp.stack(entries), "ctx", 0, 0).reshape(heads, dim, dim)

    causal = at[:, None] >= at[None, :]
    decays = jnp.where(
        causal[None], jnp.exp(jnp.minimum(cumlog[:, :, None] - cumlog[:, None, :], 0.0)), 0.0
    )
    scores = jnp.einsum("jsv,csv->sjc", q_prompt, k_prompt, preferred_element_type=F32)
    weights = (scores * decays).astype(BF)
    within = jnp.einsum("hnm,mhe->nhe", weights, v_prompt, preferred_element_type=F32)
    carried = jnp.einsum("nhd,hde->nhe", q_prompt, entry, preferred_element_type=F32)
    retention = (within + carried * jnp.exp(cumlog).T[:, :, None]).astype(BF)
    retention = retention.reshape(tokens, heads * dim)

    def steps_of():
        final = (total_decay[:, None, None] * entry.astype(F32) + own_state).astype(BF)
        asked = queries.reshape(sections, CAP * steps, heads, dim)
        reads = jnp.einsum("jchd,hde->jche", asked, final, preferred_element_type=F32)
        reads = lax.all_to_all(reads.astype(BF).reshape(sections, -1, dim), "ctx", 0, 0)
        reads = reads.reshape(sections * CAP, steps * heads * dim)
        prefix = jnp.dot(selector.T, reads, preferred_element_type=F32)
        prefix = prefix.reshape(rows, steps, heads, dim)
        rates = jnp.transpose(step_decay, (2, 1, 0))
        logs = [rates[:, 0]]
        for t in range(1, steps):
            logs.append(logs[-1] + rates[:, t])
        step_logs = jnp.stack(logs, axis=1)
        head_logs = jnp.transpose(step_logs, (0, 2, 1))
        turn = jnp.arange(steps)
        seen = turn[:, None] >= turn[None, :]
        gaps = head_logs[:, :, :, None] - head_logs[:, :, None, :]
        gains = jnp.where(seen[None, None], jnp.exp(jnp.minimum(gaps, 0.0)), 0.0)
        own = jnp.einsum("rthd,ruhd->rhtu", q_step, k_step, preferred_element_type=F32)
        own = jnp.einsum("rhtu,ruhe->rthe", own * gains, v_step.astype(F32))
        kept = (jnp.exp(step_logs)[:, :, :, None] * prefix + own).astype(BF)
        return kept.reshape(rows * steps, heads * dim)

    prompt_out, step_out = gathered_projections(retention, steps_of, w_out)
    return prompt_out, step_out.reshape(rows, steps, w_out.shape[1])


def solution(mesh):
    in_specs = (
        P("ctx", "head", None),
        P("ctx", "head", None),
        P("ctx", "head", None),
        P("head", "ctx"),
        P("ctx", None),
        P("ctx", None, "head", None),
        P("ctx", None, "head", None),
        P("ctx", None, "head", None),
        P("head", None, "ctx"),
        P(None, "head"),
    )
    out_specs = (P("ctx", "head"), P("ctx", None, "head"))
    return jax.shard_map(shards, mesh=mesh, in_specs=in_specs, out_specs=out_specs, check_vma=False)
```

time: 373 us -> 202 us (0.54)
  waiting for transfers between devices: 208 us -> 63.3 us
  matrix products: 64.5 us -> 16.8 us
  starting transfers between devices: 0.34 us -> 31.9 us
  Pallas kernels: 0 us -> 31 us
  blocking collectives: 30.8 us -> 0 us
  between operations: 14.7 us -> 1.79 us
  local copies, waits for them, and re-layouts: 8.8 us -> 16.3 us
  other arithmetic: 43.6 us -> 38.7 us
    all_gather x4 -> x0, waiting for transfers between devices: 208 us -> none  [the longest x1 71.2 us: shards(): lax.all_gather(retention, 'head', axis=1, tiled=True)]
    dot_general x16 -> x8, matrix products: 64.5 us -> 14.9 us  [the longest x1 4.68 us: shards(): jnp.einsum('hnm,mhe->nhe', weights, v_prompt, preferred_element_type=F32)]
    all_to_all x0 -> x3, waiting for transfers between devices: none -> 38.7 us  [the longest x1 17.4 us: shards(): got = lax.all_to_all(sent, 'ctx', 0, 0)]
    pallas_call x0 -> x5, Pallas kernels: none -> 31 us  [project(): pl.pallas_call(body, grid_spec=pltpu.PrefetchScalarGridSpec(num_scalar_pr...]
    unnamed x1 -> x0, blocking collectives: 30.8 us -> none
    unnamed x2 -> x14, other arithmetic: 0.08 us -> 30.8 us
    ppermute x0 -> x11, waiting for transfers between devices: none -> 24.6 us  [the longest x3 24 us: across(): return lax.ppermute(a, 'head', [(h, h ^ 1) for h in range(8)])]
    select_n x15 -> x0, other arithmetic: 23.5 us -> none  [step(): jnp.where(position < mine, new, old)]
  transfers between devices with their start and end apart: 4 -> 14, of which waited for: 4 -> 5; matrix products, arithmetic and copies ran while one was open for 19% -> 11% of each run, Pallas kernels for 0% -> 14%
where the time goes in v1:
time: 202 us; the launch traced here: 200 us
  waiting for transfers between devices  63.3 us (31%)
  other arithmetic  38.7 us (19%)
  starting transfers between devices  31.9 us (16%)
  Pallas kernels  31 us (15%)
  matrix products  16.8 us (8%)
  local copies, waits for them, and re-layouts  16.3 us (8%)
    pallas_call x5, Pallas kernels, project(): pl.pallas_call(body, grid_spec=pltpu.PrefetchScalarGridSpec(num_scalar_pr...  31 us
    unnamed x14, other arithmetic  30.8 us
    ppermute x3, waiting for transfers between devices, across(): return lax.ppermute(a, 'head', [(h, h ^ 1) for h in range(8)])  24 us
    all_to_all x1, waiting for transfers between devices, shards(): got = lax.all_to_all(sent, 'ctx', 0, 0)  17.4 us
    all_to_all x1, waiting for transfers between devices, steps_of(): lax.all_to_all(reads.astype(BF).reshape(sections, -1, dim), 'ctx', 0, 0)  16.6 us
    ppermute x4, starting transfers between devices, down(): return lax.ppermute(a, 'head', [(h, (h - 2) % 8) for h in range(8)])  7.86 us
    ppermute x3, starting transfers between devices, across(): return lax.ppermute(a, 'head', [(h, h ^ 1) for h in range(8)])  6.34 us
    all_to_all x1, starting transfers between devices, shards(): got = lax.all_to_all(sent, 'ctx', 0, 0)  5.59 us
  transfers between devices with their start and end apart: 14, of which 5 were waited for; matrix products, arithmetic and copies ran while one was open for 11% of the time, Pallas kernels for 14%

profile of v1, /device:TPU:0, one launch (start us, length us, event | category | flops | bytes accessed | tf_op | source)
XLA Modules:
  0.0 199.7 jit_solution(9075166756488374301)
XLA Ops:
  0.7 1.1 fusion.13
  2.5 0.9 fusion.8
  3.4 0.7 convert_add_fusion
  4.1 1.1 reshape.181
  5.2 0.4 convolution_convert_fusion
  5.9 0.7 multiply_convert_fusion.1
  6.6 1.5 fusion.57
  8.3 1.1 fusion.6
  9.4 5.6 %all-to-all-start = ((bf16[16,144,256]{2,1,0:T(8,128)(2,1)}), bf16[16,144,256]{2,1,0:T(8,128)(2,1)S(1)}, u32[]{:S(2)}, u32[]{:S(2)}) async-start(bf16[16,144,256]{2,1,0:T(8,128)(2,1)} %fusion.6), calls=%async_computation | async-start | bytes 2359296 | tf_op jit(solution)/shard_map/all_to_all | solution.py:192
  15.0 0.6 constant_dynamic-update-slice_fusion.15
  15.7 17.4 %all-to-all-done = bf16[16,144,256]{2,1,0:T(8,128)(2,1)S(1)} async-done(((bf16[16,144,256]{2,1,0:T(8,128)(2,1)}), bf16[16,144,256]{2,1,0:T(8,128)(2,1)S(1)}, u32[]{:S(2)}, u32[]{:S(2)}) %all-to-all-start) | async-done | bytes 1179680 | tf_op jit(solution)/shard_map/all_to_all | solution.py:192
  33.1 0.6 fusion.55
  34.6 0.7 constant_dynamic-update-slice_fusion.14
  35.3 1.3 constant_dynamic-update-slice_fusion.13
  36.6 2.1 %constant_dynamic-update-slice_fusion.12 = bf16[16,64,256]{2,1,0:T(8,128)(2,1)} fusion(bf16[16,64,256]{2,1,0:T(8,128)(2,1)} %get-tuple-element.26, f32[16,64,256]{2,1,0:T(8,128)} %copy-done.6, f32[1,64,256]{2,1,0:T(8,128)S(1)} %get-tuple-element.27, f32[]{:T(128)} %bitcast.13), kind=kLoop, calls=%fused_computation.81 | loop fusion | flops 49152 | bytes 164352
  38.6 2.7 %constant_dynamic-update-slice_fusion.11 = (bf16[16,64,256]{2,1,0:T(8,128)(2,1)}, f32[1,64,256]{2,1,0:T(8,128)S(1)}) fusion(bf16[16,64,256]{2,1,0:T(8,128)(2,1)} %constant_dynamic-update-slice_fusion.12, f32[16,64,256]{2,1,0:T(8,128)} %copy-done.6, f32[1,64,256]{2,1,0:T(8,128)S(1)} %get-tuple-element.27, f32[]{:T(128)} %bitcast.13, f32[]{:T(128)} %bitcast.14), kind=kLoop, calls=%fused_computation.80 | loop fusion | flops 81920 | bytes 295936
  41.4 2.1 %constant_dynamic-update-slice_fusion.10 = bf16[16,64,256]{2,1,0:T(8,128)(2,1)} fusion(bf16[16,64,256]{2,1,0:T(8,128)(2,1)} %get-tuple-element.24, f32[16,64,256]{2,1,0:T(8,128)} %copy-done.6, f32[1,64,256]{2,1,0:T(8,128)S(1)} %get-tuple-element.25, f32[]{:T(128)} %bitcast.15), kind=kLoop, calls=%fused_computation.79 | loop fusion | flops 49152 | bytes 164352
  43.5 2.7 %constant_dynamic-update-slice_fusion.9 = (bf16[16,64,256]{2,1,0:T(8,128)(2,1)}, f32[1,64,256]{2,1,0:T(8,128)S(1)}) fusion(bf16[16,64,256]{2,1,0:T(8,128)(2,1)} %constant_dynamic-update-slice_fusion.10, f32[16,64,256]{2,1,0:T(8,128)} %copy-done.6, f32[1,64,256]{2,1,0:T(8,128)S(1)} %get-tuple-element.25, f32[]{:T(128)} %bitcast.15, f32[]{:T(128)} %bitcast.16), kind=kLoop, calls=%fused_computation.78 | loop fusion | flops 81920 | bytes 295936
  46.2 2.0 constant_dynamic-update-slice_fusion.8
  48.2 2.7 %constant_dynamic-update-slice_fusion.7 = (bf16[16,64,256]{2,1,0:T(8,128)(2,1)}, f32[1,64,256]{2,1,0:T(8,128)S(1)}) fusion(bf16[16,64,256]{2,1,0:T(8,128)(2,1)} %constant_dynamic-update-slice_fusion.8, f32[16,64,256]{2,1,0:T(8,128)} %copy-done.6, f32[1,64,256]{2,1,0:T(8,128)S(1)} %get-tuple-element.23, f32[]{:T(128)} %bitcast.17, f32[]{:T(128)} %bitcast.18), kind=kLoop, calls=%fused_computation.76 | loop fusion | flops 81920 | bytes 295936
  50.9 2.1 %constant_dynamic-update-slice_fusion.6 = bf16[16,64,256]{2,1,0:T(8,128)(2,1)} fusion(bf16[16,64,256]{2,1,0:T(8,128)(2,1)} %get-tuple-element.20, f32[16,64,256]{2,1,0:T(8,128)} %copy-done.6, f32[1,64,256]{2,1,0:T(8,128)S(1)} %get-tuple-element.21, f32[]{:T(128)} %bitcast.19), kind=kLoop, calls=%fused_computation.75 | loop fusion | flops 49152 | bytes 164352
  53.0 2.8 %constant_dynamic-update-slice_fusion.5 = (bf16[16,64,256]{2,1,0:T(8,128)(2,1)}, f32[1,64,256]{2,1,0:T(8,128)S(1)}) fusion(bf16[16,64,256]{2,1,0:T(8,128)(2,1)} %constant_dynamic-update-slice_fusion.6, f32[16,64,256]{2,1,0:T(8,128)} %copy-done.6, f32[1,64,256]{2,1,0:T(8,128)S(1)} %get-tuple-element.21, f32[]{:T(128)} %bitcast.19, f32[]{:T(128)} %bitcast.20), kind=kLoop, calls=%fused_computation.74 | loop fusion | flops 81920 | bytes 295936
  55.8 2.1 %constant_dynamic-update-slice_fusion.4 = bf16[16,64,256]{2,1,0:T(8,128)(2,1)} fusion(bf16[16,64,256]{2,1,0:T(8,128)(2,1)} %get-tuple-element.18, f32[16,64,256]{2,1,0:T(8,128)} %copy-done.6, f32[1,64,256]{2,1,0:T(8,128)S(1)} %get-tuple-element.19, f32[]{:T(128)} %bitcast.21), kind=kLoop, calls=%fused_computation.73 | loop fusion | flops 49152 | bytes 164352
  57.9 2.7 %constant_dynamic-update-slice_fusion.3 = (bf16[16,64,256]{2,1,0:T(8,128)(2,1)}, f32[1,64,256]{2,1,0:T(8,128)S(1)}) fusion(bf16[16,64,256]{2,1,0:T(8,128)(2,1)} %constant_dynamic-update-slice_fusion.4, f32[16,64,256]{2,1,0:T(8,128)} %copy-done.6, f32[1,64,256]{2,1,0:T(8,128)S(1)} %get-tuple-element.19, f32[]{:T(128)} %bitcast.21, f32[]{:T(128)} %bitcast.22), kind=kLoop, calls=%fused_computation.72 | loop fusion | flops 81920 | bytes 295936
  60.7 2.0 %constant_dynamic-update-slice_fusion.2 = bf16[16,64,256]{2,1,0:T(8,128)(2,1)} fusion(bf16[16,64,256]{2,1,0:T(8,128)(2,1)} %get-tuple-element.16, f32[16,64,256]{2,1,0:T(8,128)} %copy-done.6, f32[1,64,256]{2,1,0:T(8,128)S(1)} %get-tuple-element.17, f32[]{:T(128)} %bitcast.23), kind=kLoop, calls=%fused_computation.71 | loop fusion | flops 49152 | bytes 164352
  62.7 2.7 %constant_dynamic-update-slice_fusion.1 = (bf16[16,64,256]{2,1,0:T(8,128)(2,1)}, f32[1,64,256]{2,1,0:T(8,128)S(1)}) fusion(bf16[16,64,256]{2,1,0:T(8,128)(2,1)} %constant_dynamic-update-slice_fusion.2, f32[16,64,256]{2,1,0:T(8,128)} %copy-done.6, f32[1,64,256]{2,1,0:T(8,128)S(1)} %get-tuple-element.17, f32[]{:T(128)} %bitcast.23, f32[]{:T(128)} %bitcast.24), kind=kLoop, calls=%fused_computation.70 | loop fusion | flops 81920 | bytes 295936
  65.4 2.1 %constant_dynamic-update-slice_fusion = bf16[16,64,256]{2,1,0:T(8,128)(2,1)} fusion(bf16[16,64,256]{2,1,0:T(8,128)(2,1)} %get-tuple-element.14, f32[16,64,256]{2,1,0:T(8,128)} %copy-done.6, f32[1,64,256]{2,1,0:T(8,128)S(1)} %get-tuple-element.15, f32[]{:T(128)} %bitcast.25), kind=kLoop, calls=%fused_computation.69 | loop fusion | flops 49152 | bytes 164352 | tf_op jit(solution)/shard_map/stack | solution.py:202
  67.5 3.6 %all-to-all-start.1 = ((bf16[16,64,256]{2,1,0:T(8,128)(2,1)}), bf16[16,64,256]{2,1,0:T(8,128)(2,1)S(1)}, u32[]{:S(2)}, u32[]{:S(2)}) async-start(bf16[16,64,256]{2,1,0:T(8,128)(2,1)} %constant_dynamic-update-slice_fusion), calls=%async_computation.1 | async-start | bytes 1048576 | tf_op jit(solution)/shard_map/all_to_all | solution.py:202
  71.1 4.7 %fusion.3 = f32[4,512,256]{1,2,0:T(8,128)} fusion(f32[4,512]{1,0:T(4,128)S(1)} %bitcast.83, pred[512,512]{1,0:T(8,128)(4,1)S(1)} %iota_compare_fusion.2, bf16[512,4,256]{2,1,0:T(4,128)(2,1)S(1)} %copy-done.9, bf16[512,4,256]{2,1,0:T(4,128)(2,1)S(1)} %copy-done, bf16[512,4,256]{2,1,0:T(4,128)(2,1)} %param.10), kind=kOutput, calls=%fused_computation.13 | convolution fusion | flops 1078984704 | bytes 5513216 | tf_op jit(solution)/shard_map/hnm,mhe->nhe/dot_general | solution.py:210
  76.1 1.1 copy.93
  77.2 4.7 %all-to-all-done.1 = bf16[16,64,256]{2,1,0:T(8,128)(2,1)S(1)} async-done(((bf16[16,64,256]{2,1,0:T(8,128)(2,1)}), bf16[16,64,256]{2,1,0:T(8,128)(2,1)S(1)}, u32[]{:S(2)}, u32[]{:S(2)}) %all-to-all-start.1) | async-done | bytes 524320 | tf_op jit(solution)/shard_map/all_to_all | solution.py:202
  81.9 2.3 %fusion.2 = bf16[512,4,256]{0,2,1:T(8,128)(2,1)S(1)} fusion(f32[4,512,256]{1,2,0:T(8,128)} %fusion.3, bf16[4,256,256]{2,1,0:T(8,128)(2,1)S(1)} %bitcast.71, f32[512,4]{0,1:T(4,128)S(1)} %get-tuple-element.40, bf16[512,4,256]{2,1,0:T(4,128)(2,1)S(1)} %copy-done.10), kind=kOutput, calls=%fused_computation.6 | convolution fusion | flops 270008320 | bytes 4726784 | tf_op jit(solution)/shard_map/nhd,hde->nhe/dot_general | solution.py:211
  84.3 0.5 copy.107.refs_0_
  84.8 2.0 collective-permute-start
  86.8 2.7 %collective-permute-start.1 = (bf16[512,1024]{1,0:T(8,128)(2,1)S(1)}, bf16[512,1024]{1,0:T(8,128)(2,1)S(1)}, u32[]{:S(2)}, u32[]{:S(2)}) collective-permute-start(bf16[512,1024]{1,0:T(8,128)(2,1)S(1)} %copy.107.refs_0_), channel_id=1, source_target_pairs={{0,1},{1,0},{2,3},{3,2},{4,5},{5,4},{6,7},{7,6},{8,9},{9,8},{10,11... | collective-permute-start | bytes 3145736 | tf_op jit(solution)/shard_map/ppermute | solution.py:21
  89.5 2.2 %collective-permute-start.3 = (bf16[512,1024]{1,0:T(8,128)(2,1)S(1)}, bf16[512,1024]{1,0:T(8,128)(2,1)}, u32[]{:S(2)}, u32[]{:S(2)}) collective-permute-start(bf16[512,1024]{1,0:T(8,128)(2,1)S(1)} %copy.107.refs_0_), channel_id=1, source_target_pairs={{0,6},{1,7},{2,0},{3,1},{4,2},{5,3},{6,4},{7,5},{8,14},{9,15},{10,... | collective-permute-start | bytes 3145736 | tf_op jit(solution)/shard_map/ppermute | solution.py:17
  91.7 1.9 fusion.19
  93.9 1.0 copy.95
  94.9 4.2 %all-to-all-start.2 = ((bf16[16,64,256]{2,1,0:T(8,128)(2,1)}), bf16[16,64,256]{2,1,0:T(8,128)(2,1)}, u32[]{:S(2)}, u32[]{:S(2)}) async-start(bf16[16,64,256]{2,1,0:T(8,128)(2,1)} %copy.95), calls=%async_computation.2 | async-start | bytes 1048576 | tf_op jit(solution)/shard_map/all_to_all | solution.py:219
  99.4 2.3 %fusion.7 = f32[32,4,4,256]{3,2,1,0:T(4,128)} fusion(bf16[32,4,4,256]{3,2,1,0:T(4,128)(2,1)} %param.17, bf16[32,4,4,256]{3,2,1,0:T(4,128)(2,1)} %param.16, bf16[32,4,4,256]{3,2,1,0:T(4,128)(2,1)S(1)} %copy-done.11, f32[32,4,4]{2,1,0:T(4,128)S(1)} %copy.99, pred[4,4]{1,0:T(4,128)(4,1)S(1)} %iota_compare_fusion.10), kind=kOutput, calls=%fused_computation.19 | convolution fusion | flops 2105344 | bytes 1312784 | tf_op jit(solution)/shard_map/rhtu,ruhe->rthe/dot_general | solution.py:234
  101.6 16.6 %all-to-all-done.2 = bf16[16,64,256]{2,1,0:T(8,128)(2,1)} async-done(((bf16[16,64,256]{2,1,0:T(8,128)(2,1)}), bf16[16,64,256]{2,1,0:T(8,128)(2,1)}, u32[]{:S(2)}, u32[]{:S(2)}) %all-to-all-start.2) | async-done | bytes 524320 | tf_op jit(solution)/shard_map/all_to_all | solution.py:219
  118.3 2.1 %reshape.187 = bf16[64,4096]{1,0:T(8,128)(2,1)} reshape(bf16[16,64,256]{2,1,0:T(8,128)(2,1)} %all-to-all-done.2) | data formatting | bytes 1048576 | tf_op jit(solution)/shard_map/reshape | solution.py:220
  120.4 2.2 %dot_general.49 = bf16[4,4,256,64]{2,1,0,3:T(4,128)(2,1)} reshape(bf16[4096,64]{0,1:T(8,128)(2,1)} %bitcast.78) | data formatting | bytes 1048576 | tf_op jit(solution)/shard_map/dot_general | solution.py:221
  122.6 1.7 fusion.5
  124.7 1.4 slice.274
  126.1 2.1 %pad_maximum_fusion = (bf16[640,1024]{1,0:T(8,128)(2,1)}, bf16[640,1024]{1,0:T(8,128)(2,1)}, bf16[640,1024]{1,0:T(8,128)(2,1)}) fusion(bf16[128,1024]{1,0:T(8,128)(2,1)S(1)} %bitcast.69, bf16[256,1024]{1,0:T(8,128)(2,1)S(1)} %slice.266, bf16[256,1024]{1,0:T(8,128)(2,1)S(1)} %slice.274, bf16[256,1024]{1,0:T(8,128)(2,1)S(1)} %get-tuple-element.34, ...), kind=kLoop, calls=%fused_computation.8 | loop fusion | flops 9830400 | bytes 6291456 | tf_op jit(solution)/shard_map/concatenate | solution.py:87
  128.3 2.0 %collective-permute-start.4 = (bf16[640,1024]{1,0:T(8,128)(2,1)}, bf16[640,1024]{1,0:T(8,128)(2,1)}, u32[]{:S(2)}, u32[]{:S(2)}) collective-permute-start(bf16[640,1024]{1,0:T(8,128)(2,1)} %get-tuple-element.36), channel_id=1, source_target_pairs={{0,1},{1,0},{2,3},{3,2},{4,5},{5,4},{6,7},{7,6},{8,9},{9,8},{10,11... | collective-permute-start | bytes 3932168 | tf_op jit(solution)/shard_map/ppermute | solution.py:21
  130.3 2.5 %collective-permute-start.6 = (bf16[640,1024]{1,0:T(8,128)(2,1)}, bf16[640,1024]{1,0:T(8,128)(2,1)}, u32[]{:S(2)}, u32[]{:S(2)}) collective-permute-start(bf16[640,1024]{1,0:T(8,128)(2,1)} %get-tuple-element.35), channel_id=1, source_target_pairs={{0,6},{1,7},{2,0},{3,1},{4,2},{5,3},{6,4},{7,5},{8,14},{9,15},{10,... | collective-permute-start | bytes 3932168 | tf_op jit(solution)/shard_map/ppermute | solution.py:17
  133.0 3.5 %shard_map.113.refs_8_ = f32[512,1024]{1,0:T(8,128)S(1)} custom-call(s32[1]{0:T(128)} %bitcast.44.heads_ref, bf16[512,1024]{1,0:T(8,128)(2,1)S(1)} %copy.107.refs_0_, bf16[8192,1024]{1,0:T(8,128)(2,1)} %refs_2_.1), custom_call_target="tpu_custom_call" | custom-call | flops 1073741824 | bytes 2097152 | tf_op jit(solution)/shard_map/pallas_call | solution.py:62
  136.6 24.0 %collective-permute-done.4.refs_2_ = bf16[640,1024]{1,0:T(8,128)(2,1)} collective-permute-done((bf16[640,1024]{1,0:T(8,128)(2,1)}, bf16[640,1024]{1,0:T(8,128)(2,1)}, u32[]{:S(2)}, u32[]{:S(2)}) %collective-permute-start.4) | collective-permute-done | bytes 1310752 | tf_op jit(solution)/shard_map/ppermute | solution.py:21
  160.5 1.1 slice.276
  161.6 0.9 slice.275
  162.5 0.9 slice.277
  163.5 0.6 collective-permute-done.2.refs_0_
  164.3 1.4 collective-permute-start.5
  165.7 1.9 collective-permute-start.7
  167.6 7.6 %shard_map.114 = (f32[512,1024]{1,0:T(8,128)S(1)}, f32[128,1024]{1,0:T(8,128)S(1)}) custom-call(s32[4]{0:T(128)S(1)} %pad_add_fusion.1.heads_ref, bf16[512,1024]{1,0:T(8,128)(2,1)S(1)} %collective-permute-done.refs_0_, bf16[512,1024]{1,0:T(8,128)(2,1)} %collective-permute-done.3.refs_1_, bf16[512,1024]{1,0:T(8,128)(2,1)S(1)} %copy-done.3, ...), custom_call_target="tpu_custom_call" | custom-call | flops 3489660928 | bytes 8388608 | tf_op jit(solution)/shard_map/pallas_call | solution.py:62
  175.3 1.6 collective-permute-start.8
  176.9 9.3 %shard_map.115 = (f32[512,1024]{1,0:T(8,128)S(1)}, f32[128,1024]{1,0:T(8,128)S(1)}) custom-call(s32[6]{0:T(128)S(1)} %stack.92.heads_ref, bf16[640,1024]{1,0:T(8,128)(2,1)S(1)} %collective-permute-done.2.refs_0_, bf16[640,1024]{1,0:T(8,128)(2,1)} %collective-permute-done.6.refs_1_, bf16[640,1024]{1,0:T(8,128)(2,1)} %collective-permute-done.4.refs_2_, ...), custom_call_target="tpu_custom_call" | custom-call | flops 4026531840 | bytes 12582912 | tf_op jit(solution)/shard_map/pallas_call | solution.py:62
  186.2 1.3 collective-permute-start.10
  187.5 0.9 collective-permute-start.9
  188.4 7.3 %shard_map.116 = (bf16[512,1024]{1,0:T(8,128)(2,1)}, f32[128,1024]{1,0:T(8,128)S(1)}) custom-call(s32[4]{0:T(128)S(1)} %pad_add_fusion.heads_ref, bf16[384,1024]{1,0:T(8,128)(2,1)S(1)} %collective-permute-done.5.refs_0_, bf16[384,1024]{1,0:T(8,128)(2,1)S(1)} %collective-permute-done.7.refs_1_, bf16[128,1024]{1,0:T(8,128)(2,1)S(1)} %collective-permute-done.8.refs_2_, ...), custom_call_target="tpu_custom_call" | custom-call | flops 1879048192 | bytes 8388608 | tf_op jit(solution)/shard_map/pallas_call | solution.py:62
  195.7 3.2 %shard_map.117 = bf16[128,1024]{1,0:T(8,128)(2,1)S(1)} custom-call(s32[1]{0:T(128)} %bitcast.heads_ref, bf16[64,1024]{1,0:T(8,128)(2,1)S(1)} %collective-permute-done.9.refs_0_, bf16[64,1024]{1,0:T(8,128)(2,1)S(1)} %collective-permute-done.10.refs_1_, bf16[8192,1024]{1,0:T(8,128)(2,1)} %refs_2_.1, f32[128,1024]{1,0:T(8,128)S(1)} %get-tuple-element.13.refs_3_), custom_call_target="tpu_custom_call" | custom-call | flops 268435456 | bytes 2097152 | tf_op jit(solution)/shard_map/pallas_call | solution.py:62
  198.9 0.8 reshape.189
  (74 shorter events, 2.9 us)
Async XLA Ops:
  0.6 6.0 %copy-start = (bf16[512,4,256]{2,1,0:T(4,128)(2,1)S(1)}, bf16[512,4,256]{2,1,0:T(4,128)(2,1)}, u32[]{:S(2)}) copy-start(bf16[512,4,256]{2,1,0:T(4,128)(2,1)} %param.12) | copy-start | bytes 3145732
  0.6 5.2 %copy-start.8 = (bf16[512,4,256]{2,1,0:T(4,128)(2,1)S(1)}, bf16[512,4,256]{2,1,0:T(4,128)(2,1)}, u32[]{:S(2)}) copy-start(bf16[512,4,256]{2,1,0:T(4,128)(2,1)} %param.11) | copy-start | bytes 3145732
  9.4 23.7 %all-to-all-start = ((bf16[16,144,256]{2,1,0:T(8,128)(2,1)}), bf16[16,144,256]{2,1,0:T(8,128)(2,1)S(1)}, u32[]{:S(2)}, u32[]{:S(2)}) async-start(bf16[16,144,256]{2,1,0:T(8,128)(2,1)} %fusion.6), calls=%async_computation | async-start | bytes 2359296 | tf_op jit(solution)/shard_map/all_to_all | solution.py:192
  34.6 2.0 %copy-start.6 = (f32[16,64,256]{2,1,0:T(8,128)}, f32[16,64,256]{2,1,0:T(8,128)S(1)}, u32[]{:S(2)}) copy-start(f32[16,64,256]{2,1,0:T(8,128)S(1)} %get-tuple-element.31) | copy-start | bytes 3145732
  35.2 35.9 %copy-start.9 = (bf16[512,4,256]{2,1,0:T(4,128)(2,1)S(1)}, bf16[512,4,256]{2,1,0:T(4,128)(2,1)}, u32[]{:S(2)}) copy-start(bf16[512,4,256]{2,1,0:T(4,128)(2,1)} %param.11) | copy-start | bytes 3145732
  67.5 14.4 %all-to-all-start.1 = ((bf16[16,64,256]{2,1,0:T(8,128)(2,1)}), bf16[16,64,256]{2,1,0:T(8,128)(2,1)S(1)}, u32[]{:S(2)}, u32[]{:S(2)}) async-start(bf16[16,64,256]{2,1,0:T(8,128)(2,1)} %constant_dynamic-update-slice_fusion), calls=%async_computation.1 | async-start | bytes 1048576 | tf_op jit(solution)/shard_map/all_to_all | solution.py:202
  75.8 6.1 %copy-start.10 = (bf16[512,4,256]{2,1,0:T(4,128)(2,1)S(1)}, bf16[512,4,256]{2,1,0:T(4,128)(2,1)}, u32[]{:S(2)}) copy-start(bf16[512,4,256]{2,1,0:T(4,128)(2,1)} %param.10) | copy-start | bytes 3145732
  81.9 2.3 %copy-start.7 = (bf16[16,64,256]{2,1,0:T(8,128)(2,1)}, bf16[16,64,256]{2,1,0:T(8,128)(2,1)S(1)}, u32[]{:S(2)}) copy-start(bf16[16,64,256]{2,1,0:T(8,128)(2,1)S(1)} %all-to-all-done.1) | copy-start | bytes 1572868
  84.8 39.8 %collective-permute-start = (bf16[512,1024]{1,0:T(8,128)(2,1)S(1)}, bf16[512,1024]{1,0:T(8,128)(2,1)S(1)}, u32[]{:S(2)}, u32[]{:S(2)}) collective-permute-start(bf16[512,1024]{1,0:T(8,128)(2,1)S(1)} %copy.107.refs_0_), channel_id=1, source_target_pairs={{0,2},{1,3},{2,4},{3,5},{4,6},{5,7},{6,0},{7,1},{8,10},{9,11},{10,... | collective-permute-start | bytes 3145736 | tf_op jit(solution)/shard_map/ppermute | solution.py:13
  86.8 37.7 %collective-permute-start.1 = (bf16[512,1024]{1,0:T(8,128)(2,1)S(1)}, bf16[512,1024]{1,0:T(8,128)(2,1)S(1)}, u32[]{:S(2)}, u32[]{:S(2)}) collective-permute-start(bf16[512,1024]{1,0:T(8,128)(2,1)S(1)} %copy.107.refs_0_), channel_id=1, source_target_pairs={{0,1},{1,0},{2,3},{3,2},{4,5},{5,4},{6,7},{7,6},{8,9},{9,8},{10,11... | collective-permute-start | bytes 3145736 | tf_op jit(solution)/shard_map/ppermute | solution.py:21
  89.5 35.2 %collective-permute-start.3 = (bf16[512,1024]{1,0:T(8,128)(2,1)S(1)}, bf16[512,1024]{1,0:T(8,128)(2,1)}, u32[]{:S(2)}, u32[]{:S(2)}) collective-permute-start(bf16[512,1024]{1,0:T(8,128)(2,1)S(1)} %copy.107.refs_0_), channel_id=1, source_target_pairs={{0,6},{1,7},{2,0},{3,1},{4,2},{5,3},{6,4},{7,5},{8,14},{9,15},{10,... | collective-permute-start | bytes 3145736 | tf_op jit(solution)/shard_map/ppermute | solution.py:17
  93.7 5.5 %copy-start.12 = (f32[4,4,32]{2,1,0:T(4,128)S(1)}, f32[4,4,32]{2,1,0:T(4,128)}, u32[]{:S(2)}) copy-start(f32[4,4,32]{2,1,0:T(4,128)} %param.18) | copy-start | bytes 6148
  93.7 5.7 %copy-start.11 = (bf16[32,4,4,256]{3,2,1,0:T(4,128)(2,1)S(1)}, bf16[32,4,4,256]{3,2,1,0:T(4,128)(2,1)}, u32[]{:S(2)}) copy-start(bf16[32,4,4,256]{3,2,1,0:T(4,128)(2,1)} %param.15) | copy-start | bytes 786436
  94.9 23.4 %all-to-all-start.2 = ((bf16[16,64,256]{2,1,0:T(8,128)(2,1)}), bf16[16,64,256]{2,1,0:T(8,128)(2,1)}, u32[]{:S(2)}, u32[]{:S(2)}) async-start(bf16[16,64,256]{2,1,0:T(8,128)(2,1)} %copy.95), calls=%async_computation.2 | async-start | bytes 1048576 | tf_op jit(solution)/shard_map/all_to_all | solution.py:219
  124.5 1.6 copy-start.4
  124.6 1.5 copy-start.2
  128.3 32.3 %collective-permute-start.4 = (bf16[640,1024]{1,0:T(8,128)(2,1)}, bf16[640,1024]{1,0:T(8,128)(2,1)}, u32[]{:S(2)}, u32[]{:S(2)}) collective-permute-start(bf16[640,1024]{1,0:T(8,128)(2,1)} %get-tuple-element.36), channel_id=1, source_target_pairs={{0,1},{1,0},{2,3},{3,2},{4,5},{5,4},{6,7},{7,6},{8,9},{9,8},{10,11... | collective-permute-start | bytes 3932168 | tf_op jit(solution)/shard_map/ppermute | solution.py:21
  130.3 32.3 %collective-permute-start.6 = (bf16[640,1024]{1,0:T(8,128)(2,1)}, bf16[640,1024]{1,0:T(8,128)(2,1)}, u32[]{:S(2)}, u32[]{:S(2)}) collective-permute-start(bf16[640,1024]{1,0:T(8,128)(2,1)} %get-tuple-element.35), channel_id=1, source_target_pairs={{0,6},{1,7},{2,0},{3,1},{4,2},{5,3},{6,4},{7,5},{8,14},{9,15},{10,... | collective-permute-start | bytes 3932168 | tf_op jit(solution)/shard_map/ppermute | solution.py:17
  132.8 31.3 %collective-permute-start.2 = (bf16[640,1024]{1,0:T(8,128)(2,1)}, bf16[640,1024]{1,0:T(8,128)(2,1)S(1)}, u32[]{:S(2)}, u32[]{:S(2)}) collective-permute-start(bf16[640,1024]{1,0:T(8,128)(2,1)} %get-tuple-element.37), channel_id=1, source_target_pairs={{0,2},{1,3},{2,4},{3,5},{4,6},{5,7},{6,0},{7,1},{8,10},{9,11},{10,... | collective-permute-start | bytes 3932168 | tf_op jit(solution)/shard_map/ppermute | solution.py:13
  163.5 4.1 %copy-start.3 = (bf16[512,1024]{1,0:T(8,128)(2,1)S(1)}, bf16[512,1024]{1,0:T(8,128)(2,1)}, u32[]{:S(2)}) copy-start(bf16[512,1024]{1,0:T(8,128)(2,1)} %copy-done.2) | copy-start | bytes 3145732
  163.5 4.1 %copy-start.5 = (bf16[16,8,4,256]{3,1,2,0:T(8,128)(2,1)S(1)}, bf16[16,8,4,256]{3,1,2,0:T(8,128)(2,1)}, u32[]{:S(2)}) copy-start(bf16[16,8,4,256]{3,1,2,0:T(8,128)(2,1)} %copy-done.4) | copy-start | bytes 786436
  164.3 23.1 %collective-permute-start.5 = (bf16[384,1024]{1,0:T(8,128)(2,1)S(1)}, bf16[384,1024]{1,0:T(8,128)(2,1)S(1)}, u32[]{:S(2)}, u32[]{:S(2)}) collective-permute-start(bf16[384,1024]{1,0:T(8,128)(2,1)S(1)} %get-tuple-element.39), channel_id=1, source_target_pairs={{0,2},{1,3},{2,4},{3,5},{4,6},{5,7},{6,0},{7,1},{8,10},{9,11},{10,... | collective-permute-start | bytes 2359304 | tf_op jit(solution)/shard_map/ppermute | solution.py:13
  165.7 22.7 %collective-permute-start.7 = (bf16[384,1024]{1,0:T(8,128)(2,1)S(1)}, bf16[384,1024]{1,0:T(8,128)(2,1)S(1)}, u32[]{:S(2)}, u32[]{:S(2)}) collective-permute-start(bf16[384,1024]{1,0:T(8,128)(2,1)S(1)} %get-tuple-element.38), channel_id=1, source_target_pairs={{0,6},{1,7},{2,0},{3,1},{4,2},{5,3},{6,4},{7,5},{8,14},{9,15},{10,... | collective-permute-start | bytes 2359304 | tf_op jit(solution)/shard_map/ppermute | solution.py:17
  175.3 10.9 %collective-permute-start.8 = (bf16[128,1024]{1,0:T(8,128)(2,1)S(1)}, bf16[128,1024]{1,0:T(8,128)(2,1)S(1)}, u32[]{:S(2)}, u32[]{:S(2)}) collective-permute-start(bf16[128,1024]{1,0:T(8,128)(2,1)S(1)} %pad_maximum_fusion.7), channel_id=1, source_target_pairs={{0,1},{1,0},{2,3},{3,2},{4,5},{5,4},{6,7},{7,6},{8,9},{9,8},{10,11... | collective-permute-start | bytes 786440 | tf_op jit(solution)/shard_map/ppermute | solution.py:21
  186.2 9.5 %collective-permute-start.10 = (bf16[64,1024]{1,0:T(8,128)(2,1)S(1)}, bf16[64,1024]{1,0:T(8,128)(2,1)S(1)}, u32[]{:S(2)}, u32[]{:S(2)}) collective-permute-start(bf16[64,1024]{1,0:T(8,128)(2,1)S(1)} %slice.280), channel_id=1, source_target_pairs={{0,6},{1,7},{2,0},{3,1},{4,2},{5,3},{6,4},{7,5},{8,14},{9,15},{10,... | collective-permute-start | bytes 393224 | tf_op jit(solution)/shard_map/ppermute | solution.py:17
  187.5 8.2 %collective-permute-start.9 = (bf16[64,1024]{1,0:T(8,128)(2,1)S(1)}, bf16[64,1024]{1,0:T(8,128)(2,1)S(1)}, u32[]{:S(2)}, u32[]{:S(2)}) collective-permute-start(bf16[64,1024]{1,0:T(8,128)(2,1)S(1)} %slice.279), channel_id=1, source_target_pairs={{0,2},{1,3},{2,4},{3,5},{4,6},{5,7},{6,0},{7,1},{8,10},{9,11},{10,... | collective-permute-start | bytes 393224 | tf_op jit(solution)/shard_map/ppermute | solution.py:13
  195.7 4.0 %copy-start.1 = (bf16[512,4,256]{2,1,0:T(4,128)(2,1)S(1)}, bf16[512,4,256]{2,1,0:T(4,128)(2,1)}, u32[]{:S(2)}) copy-start(bf16[512,4,256]{2,1,0:T(4,128)(2,1)} %param.12) | copy-start | bytes 3145732

commit v2 on v1

v2 whole, which is shorter than its diff:
```python
import jax
import jax.numpy as jnp
from jax import lax
from jax.experimental import pallas as pl
from jax.experimental.pallas import tpu as pltpu
from jax.sharding import PartitionSpec as P

CAP = 4
BF, F32 = jnp.bfloat16, jnp.float32
WHOLE = pl.BlockSpec(memory_space=pltpu.VMEM)


def up(a):
    return lax.ppermute(a, "head", [(h, (h + 2) % 8) for h in range(8)])


def down(a):
    return lax.ppermute(a, "head", [(h, (h - 2) % 8) for h in range(8)])


def across(a):
    return lax.ppermute(a, "head", [(h, h ^ 1) for h in range(8)])


def after(values, *others):
    return lax.optimization_barrier((values, others))[0]


def call(body, out, ins, flops, limit=6 << 20):
    size = sum(a.size * a.dtype.itemsize for a in (*ins, *out))
    return pl.pallas_call(
        body,
        in_specs=[WHOLE] * len(ins),
        out_specs=[WHOLE] * len(out),
        out_shape=list(out),
        compiler_params=pltpu.CompilerParams(vmem_limit_bytes=limit),
        cost_estimate=pl.CostEstimate(flops=flops, bytes_accessed=size, transcendentals=0),
    )(*ins)


def project(accs, srcs, terms, heads, w, final):
    width, tile = srcs[0].shape[1], 256
    columns = w.shape[1]
    old = [a for a in accs if not isinstance(a, int)]
    rows = [a if isinstance(a, int) else a.shape[0] for a in accs]

    n_slot = len(heads)

    def body(heads_ref, *refs):
        src_refs, refs = refs[: len(srcs)], refs[len(srcs) :]
        w_ref, refs = refs[0], refs[1:]
        old_refs, out_refs = list(refs[: len(old)]), refs[len(old) : len(old) + len(accs)]
        sums, (w_held, arrived) = refs[len(old) + len(accs) : -2], refs[-2:]
        copies = []
        for slot in range(n_slot):
            first = pl.multiple_of(heads_ref[slot] * width, width)
            copies.append(
                pltpu.make_async_copy(
                    w_ref.at[pl.ds(first, width), :], w_held.at[slot], arrived.at[slot]
                )
            )
            copies[-1].start()
        fresh = {}
        for k, acc in enumerate(accs):
            if not isinstance(acc, int):
                fresh[k] = old_refs.pop(0)
        seen = set()
        last = {(t[4], t[5]): t[0] for t in terms}
        for slot in range(n_slot):
            copies[slot].wait()
            mine = [t for t in terms if t[0] == slot]

            @pl.loop(0, columns // tile)
            def _(j, slot=slot, mine=mine, seen=frozenset(seen)):
                cols = pl.ds(pl.multiple_of(j * tile, tile), tile)
                for _, i, s0, m, k, a0 in mine:
                    total = jnp.dot(
                        src_refs[i][s0 : s0 + m, :],
                        w_held[slot, :, cols],
                        preferred_element_type=F32,
                    )
                    span = slice(a0, a0 + m)
                    if (k, a0) in seen:
                        total += sums[k][span, cols]
                    elif k in fresh:
                        total += fresh[k][span, cols]
                    if last[k, a0] == slot:
                        out_refs[k][span, cols] = total.astype(out_refs[k].dtype)
                    else:
                        sums[k][span, cols] = total

            seen |= {(t[4], t[5]) for t in mine}

    flops = sum(2 * t[3] * width * columns for t in terms)
    return pl.pallas_call(
        body,
        in_specs=[pl.BlockSpec(memory_space=pltpu.SMEM)]
        + [WHOLE] * len(srcs)
        + [pl.BlockSpec(memory_space=pltpu.HBM)]
        + [WHOLE] * len(old),
        out_specs=[WHOLE] * len(rows),
        out_shape=[
            jax.ShapeDtypeStruct((r, columns), BF if f else F32) for r, f in zip(rows, final)
        ],
        scratch_shapes=[pltpu.VMEM((r, columns), F32) for r in rows]
        + [
            pltpu.VMEM((n_slot, width, columns), BF),
            pltpu.SemaphoreType.DMA((n_slot,)),
        ],
        compiler_params=pltpu.CompilerParams(vmem_limit_bytes=48 << 20),
        cost_estimate=pl.CostEstimate(
            flops=flops, bytes_accessed=n_slot * 2 * width * columns, transcendentals=0
        ),
    )(jnp.stack(heads).astype(jnp.int32), *srcs, w, *old)


def scan_sections(got, slice_rows):
    sections, _, dim = got.shape

    def body(got_ref, out_ref):
        state = jnp.zeros((slice_rows, dim), F32)
        for c in range(sections):
            out_ref[c] = state.astype(BF)
            parts = got_ref[c, slice_rows : slice_rows + 16, :].astype(F32)
            factor = parts[0:1] + parts[1:2] + parts[2:3]
            state = factor * state + got_ref[c, :slice_rows, :].astype(F32)

    shape = jax.ShapeDtypeStruct((sections, slice_rows, dim), BF)
    return call(body, [shape], [got], sections * slice_rows * dim * 4)[0]


def read_states(queries, within, gains, entry, own_state, decay, asked):
    heads, dim, _ = entry.shape

    def body(q_ref, in_ref, g_ref, e_ref, s_ref, d_ref, a_ref, r_ref, o_ref):
        for h in range(heads):
            cols = slice(h * dim, (h + 1) * dim)
            state = e_ref[h]
            last = (d_ref[0, h] * state.astype(F32) + s_ref[h]).astype(BF)
            rows = a_ref[:, h].reshape(-1, dim)
            reads = jnp.dot(rows, last, preferred_element_type=F32)
            o_ref[:, h] = reads.astype(BF).reshape(a_ref.shape[0], -1, dim)
            carried = jnp.dot(q_ref[:, cols], state, preferred_element_type=F32)
            total = in_ref[:, cols] + g_ref[:, h : h + 1] * carried
            r_ref[:, cols] = total.astype(BF)

    specs = [WHOLE] * 7
    specs[5] = pl.BlockSpec(memory_space=pltpu.SMEM)
    return pl.pallas_call(
        body,
        in_specs=specs,
        out_specs=[WHOLE] * 2,
        out_shape=[
            jax.ShapeDtypeStruct(queries.shape, BF),
            jax.ShapeDtypeStruct(asked.shape, BF),
        ],
        compiler_params=pltpu.CompilerParams(vmem_limit_bytes=8 << 20),
        cost_estimate=pl.CostEstimate(
            flops=2 * 768 * heads * dim * dim, bytes_accessed=8 << 20, transcendentals=0
        ),
    )(queries, within, gains, entry, own_state, decay, asked)


def pack_queries(selector, queries, sections, heads):
    dim = queries.shape[1] // heads

    def body(s_ref, q_ref, o_ref):
        for h in range(heads):
            picked = jnp.dot(
                s_ref[...], q_ref[:, h * dim : (h + 1) * dim], preferred_element_type=F32
            )
            o_ref[:, h] = picked.astype(BF).reshape(sections, -1, dim)

    slots = selector.shape[0] // sections
    shape = jax.ShapeDtypeStruct((sections, heads, slots, dim), BF)
    return call(body, [shape], [selector, queries], 2 * selector.size * queries.shape[1])[0]


def finish_steps(selector, reads, gains, own):
    _, heads, _, dim = reads.shape

    def body(s_ref, r_ref, g_ref, own_ref, o_ref):
        for h in range(heads):
            cols = slice(h * dim, (h + 1) * dim)
            prefix = jnp.dot(
                s_ref[...], r_ref[:, h].reshape(-1, dim), preferred_element_type=F32
            )
            o_ref[:, cols] = (g_ref[:, h : h + 1] * prefix + own_ref[:, cols]).astype(BF)

    shape = jax.ShapeDtypeStruct(own.shape, BF)
    return call(body, [shape], [selector, reads, gains, own], 2 * selector.size * own.shape[1])[0]


def gathered_projections(retention, steps_of, w):
    me = lax.axis_index("head")
    z, x = me // 2, me % 2
    here, far = lambda d: ((z + d) % 4) * 2 + x, lambda d: ((z + d) % 4) * 2 + 1 - x
    n = retention.shape[0]
    third = n * 11 // 32

    a1, a2, a3 = up(retention), down(retention), across(retention)
    (pa,) = project([n], [retention], [(0, 0, 0, n, 0, 0)], [me], w, [False])
    a1, a2, a3, pa = lax.optimization_barrier((a1, a2, a3, pa))

    b1, b2, b3 = up(a3), down(a2), across(a2)
    steps = steps_of(a1)
    r = steps.shape[0]
    c1, c2, c3 = up(steps), down(steps), across(steps)
    (pa,) = project(
        [pa],
        [a1, a2, a3],
        [(s, s, 0, n, 0, 0) for s in range(3)],
        [here(-1), here(1), far(0)],
        w,
        [False],
    )
    b1, b2, b3, c1, c2, c3, pa = lax.optimization_barrier((b1, b2, b3, c1, c2, c3, pa))

    e1, e2, e3 = up(b1[:third]), down(b3[third : 2 * third]), across(b2[2 * third :])
    d1, d2, d3 = up(c3), down(c2), across(c2)
    pa, pb = project(
        [pa, r],
        [b1, b2, b3, steps, c1, c2, c3],
        [(s, s, 0, n, 0, 0) for s in range(3)] + [(3 + s, 3 + s, 0, r, 1, 0) for s in range(4)],
        [far(-1), here(2), far(1), me, here(-1), here(1), far(0)],
        w,
        [False, False],
    )
    e1, e2, e3, d1, d2, d3, pa, pb = lax.optimization_barrier((e1, e2, e3, d1, d2, d3, pa, pb))

    f1, f2 = up(d1[: r // 2]), down(d3[r // 2 :])
    prompt_out, pb = project(
        [pa, pb],
        [e1, e2, e3, d1, d2, d3],
        [
            (0, 0, 0, third, 0, 0),
            (0, 1, 0, third, 0, third),
            (0, 2, 0, n - 2 * third, 0, 2 * third),
        ]
        + [(1 + s, 3 + s, 0, r, 1, 0) for s in range(3)],
        [far(2), far(-1), here(2), far(1)],
        w,
        [True, False],
    )
    f1, f2, pb = lax.optimization_barrier((f1, f2, pb))
    (step_out,) = project(
        [pb],
        [f1, f2],
        [(0, 0, 0, r // 2, 0, 0), (0, 1, 0, r // 2, 0, r // 2)],
        [far(2)],
        w,
        [True],
    )
    return prompt_out, step_out


def shards(
    q_prompt,
    k_prompt,
    v_prompt,
    log_decay,
    prompt_section,
    q_step,
    k_step,
    v_step,
    step_decay,
    w_out,
):
    tokens, heads, dim = q_prompt.shape
    sections = lax.axis_size("ctx")
    rows, steps = q_step.shape[:2]

    at = jnp.arange(tokens)
    upto = (at[:, None] <= at[None, :]).astype(F32)
    cumlog = jnp.dot(log_decay, upto, precision=lax.Precision.HIGHEST)
    last_log = cumlog[:, -1]
    keys = (k_prompt.astype(F32) * jnp.exp(last_log[:, None] - cumlog).T[:, :, None]).astype(BF)
    own_state = jnp.einsum("jxa,jxp->xap", keys, v_prompt, preferred_element_type=F32)
    total_decay = jnp.exp(last_log)
    slice_rows = heads * dim // sections
    high = lax.reduce_precision(total_decay, 8, 7)
    middle = lax.reduce_precision(total_decay - high, 8, 7)
    parts = jnp.stack([high, middle, total_decay - high - middle], axis=1).astype(BF)
    parts = jnp.broadcast_to(parts[:, None, :, None], (heads, sections // heads, 3, dim))
    parts = jnp.pad(parts.reshape(sections, 3, dim), ((0, 0), (0, 13), (0, 0)))
    sent = jnp.concatenate([own_state.astype(BF).reshape(sections, slice_rows, dim), parts], axis=1)
    got = lax.all_to_all(sent, "ctx", 0, 0)

    q_step, prompt_section = after((q_step, prompt_section), sent)
    ids = prompt_section[:, 0]
    hot = (ids[:, None] == jnp.arange(sections)[None, :]).astype(F32)
    before = jnp.tril(jnp.ones((rows, rows), F32), -1)
    ranking = jnp.sum(jnp.dot(before, hot) * hot, axis=1).astype(jnp.int32)
    slots = (ids * CAP + ranking)[:, None] * steps + jnp.arange(steps)[None, :]
    slots = slots.reshape(rows * steps)
    every = jnp.arange(sections * CAP * steps)
    selector = (slots[:, None] == every[None, :]).astype(BF)
    flipped = (every[:, None] == slots[None, :]).astype(BF)
    packed = pack_queries(flipped, q_step.reshape(rows * steps, -1), sections, heads)
    asked = lax.all_to_all(packed, "ctx", 0, 0)

    q_late, k_late, v_late, cum_late = after((q_prompt, k_prompt, v_prompt, cumlog), packed)
    causal = at[:, None] >= at[None, :]
    decays = jnp.where(
        causal[None], jnp.exp(jnp.minimum(cum_late[:, :, None] - cum_late[:, None, :], 0.0)), 0.0
    )
    scores = jnp.einsum("jsv,csv->sjc", q_late, k_late, preferred_element_type=F32)
    weights = (scores * decays).astype(BF)
    within = jnp.einsum("hnm,mhe->nhe", weights, v_late, preferred_element_type=F32)
    within = within.reshape(tokens, heads * dim)
    queries = q_late.reshape(tokens, heads * dim)
    gains = jnp.exp(cum_late).T

    entries = scan_sections(got, slice_rows)
    entry = lax.all_to_all(entries, "ctx", 0, 0).reshape(heads, dim, dim)

    q_own, k_own, v_own, rates = after((q_step, k_step, v_step, step_decay), entries)
    rates = jnp.transpose(rates, (2, 1, 0))
    logs = [rates[:, 0]]
    for t in range(1, steps):
        logs.append(logs[-1] + rates[:, t])
    step_logs = jnp.stack(logs, axis=1)
    head_logs = jnp.transpose(step_logs, (0, 2, 1))
    turn = jnp.arange(steps)
    seen = turn[:, None] >= turn[None, :]
    gaps = head_logs[:, :, :, None] - head_logs[:, :, None, :]
    step_gains = jnp.where(seen[None, None], jnp.exp(jnp.minimum(gaps, 0.0)), 0.0)
    own = jnp.einsum("rthd,ruhd->rhtu", q_own, k_own, preferred_element_type=F32)
    own = jnp.einsum("rhtu,ruhe->rthe", own * step_gains, v_own.astype(F32))
    own = own.reshape(rows * steps, heads * dim)
    kept = jnp.exp(step_logs).reshape(rows * steps, heads)

    within, queries, gains, own, kept, entry, asked = lax.optimization_barrier(
        (within, queries, gains, own, kept, entry, asked)
    )
    retention, reads = read_states(
        queries, within, gains, entry, own_state, total_decay[None, :], asked
    )
    reads = lax.all_to_all(reads, "ctx", 0, 0)

    def steps_of(ready):
        return finish_steps(selector, after(reads, ready), kept, own)

    prompt_out, step_out = gathered_projections(retention, steps_of, w_out)
    return prompt_out, step_out.reshape(rows, steps, w_out.shape[1])


def solution(mesh):
    in_specs = (
        P("ctx", "head", None),
        P("ctx", "head", None),
        P("ctx", "head", None),
        P("head", "ctx"),
        P("ctx", None),
        P("ctx", None, "head", None),
        P("ctx", None, "head", None),
        P("ctx", None, "head", None),
        P("head", None, "ctx"),
        P(None, "head"),
    )
    out_specs = (P("ctx", "head"), P("ctx", None, "head"))
    return jax.shard_map(shards, mesh=mesh, in_specs=in_specs, out_specs=out_specs, check_vma=False)
```

time: 202 us -> 184 us (0.911)
  other arithmetic: 38.7 us -> 3.87 us
  starting transfers between devices: 31.9 us -> 46.1 us
  Pallas kernels: 31 us -> 43.7 us
  waiting for transfers between devices: 63.3 us -> 53.8 us
  local copies, waits for them, and re-layouts: 16.3 us -> 24.6 us
  matrix products: 16.8 us -> 9.44 us
    unnamed x14 -> x0, other arithmetic: 30.8 us -> none
    unnamed x29 -> x44, local copies, waits for them, and re-layouts: 1 us -> 17 us
    all_to_all x2 -> x3, waiting for transfers between devices: 21.4 us -> 6.21 us  [the longest x1 6.2 us: shards(): entry = lax.all_to_all(entries, 'ctx', 0, 0).reshape(heads, dim, dim)]
    pallas_call x5 -> x9, Pallas kernels: 31 us -> 43.7 us  [the longest x5 38.7 us: project(): pl.pallas_call(body, in_specs=[pl.BlockSpec(memory_space=pltpu.SMEM)] + [...]
    ppermute x3 -> x5, waiting for transfers between devices: 24 us -> 33.9 us  [across(): return lax.ppermute(a, 'head', [(h, h ^ 1) for h in range(8)])]
    all_to_all x1, waiting for transfers between devices: 17.4 us -> 10.5 us  [shards(): got = lax.all_to_all(sent, 'ctx', 0, 0)]
    all_to_all x2 -> x3, starting transfers between devices: 7.8 us -> 13.4 us  [the longest x1 5.64 us: shards(): entry = lax.all_to_all(entries, 'ctx', 0, 0).reshape(heads, dim, dim)]
    ppermute x4 -> x6, starting transfers between devices: 7.86 us -> 12.9 us  [down(): return lax.ppermute(a, 'head', [(h, (h - 2) % 8) for h in range(8)])]
  transfers between devices with their start and end apart: 14 -> 21, of which waited for: 5 -> 6; matrix products, arithmetic and copies ran while one was open for 11% -> 10% of each run, Pallas kernels for 14% -> 21%
where the time goes in v2:
time: 184 us; the launch traced here: 183 us
  waiting for transfers between devices  53.8 us (29%)
  starting transfers between devices  46.1 us (25%)
  Pallas kernels  43.7 us (24%)
  local copies, waits for them, and re-layouts  24.6 us (13%)
  matrix products  9.44 us (5%)
  other arithmetic  3.87 us (2%)
    pallas_call x5, Pallas kernels, project(): pl.pallas_call(body, in_specs=[pl.BlockSpec(memory_space=pltpu.SMEM)] + [...  38.7 us
    ppermute x5, waiting for transfers between devices, across(): return lax.ppermute(a, 'head', [(h, h ^ 1) for h in range(8)])  33.9 us
    unnamed x44, local copies, waits for them, and re-layouts  17 us
    ppermute x6, starting transfers between devices, down(): return lax.ppermute(a, 'head', [(h, (h - 2) % 8) for h in range(8)])  12.9 us
    all_to_all x1, waiting for transfers between devices, shards(): got = lax.all_to_all(sent, 'ctx', 0, 0)  10.5 us
    ppermute x5, starting transfers between devices, across(): return lax.ppermute(a, 'head', [(h, h ^ 1) for h in range(8)])  9.49 us
    all_to_all x1, waiting for transfers between devices, shards(): entry = lax.all_to_all(entries, 'ctx', 0, 0).reshape(heads, dim, dim)  6.2 us
    all_to_all x1, starting transfers between devices, shards(): entry = lax.all_to_all(entries, 'ctx', 0, 0).reshape(heads, dim, dim)  5.64 us
  transfers between devices with their start and end apart: 21, of which 6 were waited for; matrix products, arithmetic and copies ran while one was open for 10% of the time, Pallas kernels for 21%

profile of v2, /device:TPU:0, one launch (start us, length us, event | category | flops | bytes accessed | tf_op | source)
XLA Modules:
  0.0 182.6 jit_solution(11913071453774346640)
XLA Ops:
  0.6 1.0 fusion.11
  1.6 0.2 copy.26
  2.1 0.1 copy.27
  2.2 1.8 %multiply_convert_fusion.1 = bf16[512,4,256]{2,1,0:T(4,128)(2,1)S(1)} fusion(bf16[512,4,256]{2,1,0:T(4,128)(2,1)} %param.11, f32[512,4]{1,0:T(8,128)S(1)} %copy.27), kind=kLoop, calls=%fused_computation.1 | loop fusion | flops 1572864 | bytes 2105344 | tf_op jit(solution)/shard_map/convert_element_type | solution.py:277
  4.1 0.6 fusion.43
  4.8 0.9 fusion.12
  5.7 5.6 %all-to-all-start = ((bf16[16,80,256]{2,1,0:T(8,128)(2,1)}), bf16[16,80,256]{2,1,0:T(8,128)(2,1)S(1)}, u32[]{:S(2)}, u32[]{:S(2)}) async-start(bf16[16,80,256]{2,1,0:T(8,128)(2,1)} %fusion.12), calls=%async_computation | async-start | bytes 1310720 | tf_op jit(solution)/shard_map/all_to_all | solution.py:287
  11.3 0.2 fusion.2
  11.6 0.1 add.147
  11.8 1.1 shard_map.113
  13.0 10.5 %all-to-all-done.got_ref = bf16[16,80,256]{2,1,0:T(8,128)(2,1)S(1)} async-done(((bf16[16,80,256]{2,1,0:T(8,128)(2,1)}), bf16[16,80,256]{2,1,0:T(8,128)(2,1)S(1)}, u32[]{:S(2)}, u32[]{:S(2)}) %all-to-all-start) | async-done | bytes 655392 | tf_op jit(solution)/shard_map/all_to_all | solution.py:287
  23.6 4.2 %all-to-all-start.2 = ((bf16[16,4,16,256]{3,2,1,0:T(8,128)(2,1)}), bf16[16,4,16,256]{3,2,1,0:T(8,128)(2,1)}, u32[]{:S(2)}, u32[]{:S(2)}) async-start(bf16[16,4,16,256]{3,2,1,0:T(8,128)(2,1)} %shard_map.113), calls=%async_computation.2 | async-start | bytes 1048576 | tf_op jit(solution)/shard_map/all_to_all | solution.py:300
  27.8 5.3 %fusion = f32[4,256,512]{2,1,0:T(8,128)} fusion(f32[4,512]{1,0:T(4,128)S(1)} %copy.31, pred[512,512]{1,0:T(8,128)(4,1)S(1)} %iota_compare_fusion.1, bf16[512,4,256]{2,1,0:T(4,128)(2,1)} %param.11, bf16[512,4,256]{2,1,0:T(4,128)(2,1)} %param.10, bf16[512,4,256]{2,1,0:T(4,128)(2,1)} %param.12), kind=kOutput, calls=%fused_computation.2 | convolution fusion | flops 1078984704 | bytes 5513216 | tf_op jit(solution)/shard_map/hnm,mhe->nhe/dot_general | solution.py:309
  33.2 2.4 %copy.48 = bf16[64,8,4,256]{3,1,2,0:T(8,128)(2,1)} copy(bf16[64,8,4,256]{3,2,1,0:T(4,128)(2,1)} %bitcast.55) | data formatting | bytes 2097152
  35.6 1.9 %copy.45.in_ref = f32[512,1024]{1,0:T(8,128)S(1)} copy(f32[512,1024]{0,1:T(8,128)} %bitcast.53) | data formatting | bytes 4194304 | tf_op jit(solution)/shard_map/reshape | solution.py:310
  37.5 0.6 iota_compare_fusion.10
  38.1 1.7 exponential_bitcast_fusion.g_ref
  39.8 1.1 copy-done.5
  40.9 0.1 shard_map.114
  41.0 0.8 copy-done.7
  41.8 5.6 %all-to-all-start.1 = ((bf16[16,64,256]{2,1,0:T(8,128)(2,1)}), bf16[16,64,256]{2,1,0:T(8,128)(2,1)}, u32[]{:S(2)}, u32[]{:S(2)}) async-start(bf16[16,64,256]{2,1,0:T(8,128)(2,1)} %copy-done.7), calls=%async_computation.1 | async-start | bytes 1048576 | tf_op jit(solution)/shard_map/all_to_all | solution.py:315
  47.5 0.1 copy.39
  47.6 0.1 copy.35
  47.8 2.3 %convolution_bitcast_fusion = f32[32,4,4,256]{3,1,2,0:T(4,128)} fusion(bf16[32,4,4,256]{3,2,1,0:T(4,128)(2,1)S(1)} %copy-done, bf16[32,4,4,256]{3,2,1,0:T(4,128)(2,1)} %param.15, bf16[32,4,4,256]{3,2,1,0:T(4,128)(2,1)} %param.17, f32[32,4,4]{2,1,0:T(4,128)S(1)} %copy.35, pred[4,4]{1,0:T(4,128)(4,1)} %iota_compare_fusion.10), kind=kOutput, calls=%fused_computation.5 | convolution fusion | flops 2105344 | bytes 1312784 | tf_op jit(solution)/shard_map/rhtu,ruhe->rthe/dot_general | solution.py:329
  50.1 1.2 copy.38
  51.3 0.9 copy.49
  52.2 6.2 %all-to-all-done.1 = bf16[16,64,256]{2,1,0:T(8,128)(2,1)} async-done(((bf16[16,64,256]{2,1,0:T(8,128)(2,1)}), bf16[16,64,256]{2,1,0:T(8,128)(2,1)}, u32[]{:S(2)}, u32[]{:S(2)}) %all-to-all-start.1) | async-done | bytes 524320 | tf_op jit(solution)/shard_map/all_to_all | solution.py:315
  58.4 1.2 copy-done.3
  59.6 0.9 copy-done.9
  60.6 2.8 %shard_map.115 = (bf16[512,1024]{1,0:T(8,128)(2,1)}, bf16[16,4,16,256]{3,2,1,0:T(8,128)(2,1)S(1)}) custom-call(bf16[512,1024]{1,0:T(8,128)(2,1)S(1)} %bitcast.45, f32[512,1024]{1,0:T(8,128)S(1)} %copy.45.in_ref, f32[512,4]{1,0:T(8,128)S(1)} %copy-done.9, bf16[4,256,256]{2,1,0:T(8,128)(2,1)} %bitcast.18.e_ref, f32[4,256,256]{2,1,0:T(8,128)S(1)} %get-tuple-element.106.s_ref, ...), custom_call_target="tpu_custom_call" | custom-call | flops 402653184 | bytes 8388608 | tf_op jit(solution)/shard_map/pallas_call | solution.py:149
  63.4 0.8 copy-done.14
  64.2 2.7 %collective-permute-start.2 = (bf16[512,1024]{1,0:T(8,128)(2,1)}, bf16[512,1024]{1,0:T(8,128)(2,1)}, u32[]{:S(2)}, u32[]{:S(2)}) collective-permute-start(bf16[512,1024]{1,0:T(8,128)(2,1)} %get-tuple-element.63.refs_0_), channel_id=1, source_target_pairs={{0,1},{1,0},{2,3},{3,2},{4,5},{5,4},{6,7},{7,6},{8,9},{9,8},{10,11... | collective-permute-start | bytes 3145736 | tf_op jit(solution)/shard_map/ppermute | solution.py:22
  66.9 4.0 %collective-permute-start.1 = (bf16[512,1024]{1,0:T(8,128)(2,1)}, bf16[512,1024]{1,0:T(8,128)(2,1)S(1)}, u32[]{:S(2)}, u32[]{:S(2)}) collective-permute-start(bf16[512,1024]{1,0:T(8,128)(2,1)} %get-tuple-element.63.refs_0_), channel_id=1, source_target_pairs={{0,6},{1,7},{2,0},{3,1},{4,2},{5,3},{6,4},{7,5},{8,14},{9,15},{10,... | collective-permute-start | bytes 3145736 | tf_op jit(solution)/shard_map/ppermute | solution.py:18
  70.9 3.6 %all-to-all-start.3 = ((bf16[16,4,16,256]{3,2,1,0:T(8,128)(2,1)}), bf16[16,4,16,256]{3,2,1,0:T(8,128)(2,1)S(1)}, u32[]{:S(2)}, u32[]{:S(2)}) async-start(bf16[16,4,16,256]{3,2,1,0:T(8,128)(2,1)} %copy-done.14), calls=%async_computation.3 | async-start | bytes 1048576 | tf_op jit(solution)/shard_map/all_to_all | solution.py:339
  74.5 4.7 %shard_map.116.refs_4_ = f32[512,1024]{1,0:T(8,128)S(1)} custom-call(s32[1]{0:T(128)} %bitcast.20.heads_ref, bf16[512,1024]{1,0:T(8,128)(2,1)} %get-tuple-element.63.refs_0_, bf16[8192,1024]{1,0:T(8,128)(2,1)} %refs_2_.1), custom_call_target="tpu_custom_call" | custom-call | flops 1073741824 | bytes 2097152 | tf_op jit(solution)/shard_map/pallas_call | solution.py:95
  79.2 1.3 copy-done.2
  80.6 11.5 %collective-permute-done.2.refs_2_ = bf16[512,1024]{1,0:T(8,128)(2,1)} collective-permute-done((bf16[512,1024]{1,0:T(8,128)(2,1)}, bf16[512,1024]{1,0:T(8,128)(2,1)}, u32[]{:S(2)}, u32[]{:S(2)}) %collective-permute-start.2) | collective-permute-done | bytes 1048608 | tf_op jit(solution)/shard_map/ppermute | solution.py:22
  92.1 0.8 collective-permute-done.1.refs_1_
  92.9 1.0 copy-done.10
  93.9 2.3 %collective-permute-done.refs_0_ = bf16[512,1024]{1,0:T(8,128)(2,1)S(1)} collective-permute-done((bf16[512,1024]{1,0:T(8,128)(2,1)}, bf16[512,1024]{1,0:T(8,128)(2,1)S(1)}, u32[]{:S(2)}, u32[]{:S(2)}) %collective-permute-start) | collective-permute-done | bytes 1048608 | tf_op jit(solution)/shard_map/ppermute | solution.py:14
  96.2 1.0 copy-done.12
  97.2 1.5 collective-permute-start.5
  98.7 2.5 %collective-permute-start.4 = (bf16[512,1024]{1,0:T(8,128)(2,1)}, bf16[512,1024]{1,0:T(8,128)(2,1)}, u32[]{:S(2)}, u32[]{:S(2)}) collective-permute-start(bf16[512,1024]{1,0:T(8,128)(2,1)} %copy-done.10), channel_id=1, source_target_pairs={{0,6},{1,7},{2,0},{3,1},{4,2},{5,3},{6,4},{7,5},{8,14},{9,15},{10,... | collective-permute-start | bytes 3145736 | tf_op jit(solution)/shard_map/ppermute | solution.py:18
  101.3 0.9 shard_map.117.refs_3_
  102.3 2.7 %collective-permute-start.8 = (bf16[128,1024]{1,0:T(8,128)(2,1)}, bf16[128,1024]{1,0:T(8,128)(2,1)S(1)}, u32[]{:S(2)}, u32[]{:S(2)}) collective-permute-start(bf16[128,1024]{1,0:T(8,128)(2,1)} %shard_map.117.refs_3_), channel_id=1, source_target_pairs={{0,1},{1,0},{2,3},{3,2},{4,5},{5,4},{6,7},{7,6},{8,9},{9,8},{10,11... | collective-permute-start | bytes 786440 | tf_op jit(solution)/shard_map/ppermute | solution.py:22
  105.1 22.3 %collective-permute-done.8.refs_6_ = bf16[128,1024]{1,0:T(8,128)(2,1)S(1)} collective-permute-done((bf16[128,1024]{1,0:T(8,128)(2,1)}, bf16[128,1024]{1,0:T(8,128)(2,1)S(1)}, u32[]{:S(2)}, u32[]{:S(2)}) %collective-permute-start.8) | collective-permute-done | bytes 262176 | tf_op jit(solution)/shard_map/ppermute | solution.py:22
  127.5 1.2 copy-done.11
  128.7 1.2 copy-done.13
  129.9 9.0 %shard_map.118.refs_8_ = f32[512,1024]{1,0:T(8,128)S(1)} custom-call(s32[3]{0:T(128)S(1)} %pad_add_fusion.1.heads_ref, bf16[512,1024]{1,0:T(8,128)(2,1)S(1)} %copy-done.13, bf16[512,1024]{1,0:T(8,128)(2,1)S(1)} %copy-done.11, bf16[512,1024]{1,0:T(8,128)(2,1)} %collective-permute-done.2.refs_2_, bf16[8192,1024]{1,0:T(8,128)(2,1)} %refs_2_.1, ...), custom_call_target="tpu_custom_call" | custom-call | flops 3221225472 | bytes 6291456 | tf_op jit(solution)/shard_map/pallas_call | solution.py:95
  138.9 1.3 copy-done.1
  140.3 2.8 %collective-permute-start.12 = (bf16[128,1024]{1,0:T(8,128)(2,1)S(1)}, bf16[128,1024]{1,0:T(8,128)(2,1)S(1)}, u32[]{:S(2)}, u32[]{:S(2)}) collective-permute-start(bf16[128,1024]{1,0:T(8,128)(2,1)S(1)} %collective-permute-done.8.refs_6_), channel_id=1, source_target_pairs={{0,2},{1,3},{2,4},{3,5},{4,6},{5,7},{6,0},{7,1},{8,10},{9,11},{10,... | collective-permute-start | bytes 786440 | tf_op jit(solution)/shard_map/ppermute | solution.py:14
  143.3 0.9 collective-permute-start.14
  144.1 1.6 collective-permute-start.13
  145.8 1.0 slice.37
  146.8 1.6 collective-permute-start.11
  148.5 1.5 collective-permute-start.9
  150.0 1.7 collective-permute-start.10
  151.7 14.3 %shard_map.119 = (f32[512,1024]{1,0:T(8,128)}, f32[128,1024]{1,0:T(8,128)S(1)}) custom-call(s32[7]{0:T(128)S(1)} %stack.65.heads_ref, bf16[512,1024]{1,0:T(8,128)(2,1)S(1)} %collective-permute-done.3.refs_0_, bf16[512,1024]{1,0:T(8,128)(2,1)} %collective-permute-done.4.refs_1_, bf16[512,1024]{1,0:T(8,128)(2,1)S(1)} %collective-permute-done.5.refs_2_, ...), custom_call_target="tpu_custom_call" | custom-call | flops 4294967296 | bytes 14680064 | tf_op jit(solution)/shard_map/pallas_call | solution.py:95
  166.1 0.4 collective-permute-start.15
  166.5 2.9 %collective-permute-start.16 = (bf16[64,1024]{1,0:T(8,128)(2,1)S(1)}, bf16[64,1024]{1,0:T(8,128)(2,1)S(1)}, u32[]{:S(2)}, u32[]{:S(2)}) collective-permute-start(bf16[64,1024]{1,0:T(8,128)(2,1)S(1)} %slice.39), channel_id=1, source_target_pairs={{0,6},{1,7},{2,0},{3,1},{4,2},{5,3},{6,4},{7,5},{8,14},{9,15},{10,... | collective-permute-start | bytes 393224 | tf_op jit(solution)/shard_map/ppermute | solution.py:18
  169.4 1.6 copy-done.6
  171.0 7.9 %shard_map.120 = (bf16[512,1024]{1,0:T(8,128)(2,1)}, f32[128,1024]{1,0:T(8,128)S(1)}) custom-call(s32[4]{0:T(128)S(1)} %pad_add_fusion.heads_ref, bf16[176,1024]{1,0:T(8,128)(2,1)S(1)} %collective-permute-done.9.refs_0_, bf16[176,1024]{1,0:T(8,128)(2,1)S(1)} %collective-permute-done.10.refs_1_, bf16[160,1024]{1,0:T(8,128)(2,1)S(1)} %collective-permute-done.11.refs_2_, ...), custom_call_target="tpu_custom_call" | custom-call | flops 1879048192 | bytes 8388608 | tf_op jit(solution)/shard_map/pallas_call | solution.py:95
  179.0 2.8 %shard_map.121 = bf16[128,1024]{1,0:T(8,128)(2,1)S(1)} custom-call(s32[1]{0:T(128)} %bitcast.heads_ref, bf16[64,1024]{1,0:T(8,128)(2,1)S(1)} %collective-permute-done.15.refs_0_, bf16[64,1024]{1,0:T(8,128)(2,1)S(1)} %collective-permute-done.16.refs_1_, bf16[8192,1024]{1,0:T(8,128)(2,1)} %refs_2_.1, f32[128,1024]{1,0:T(8,128)S(1)} %get-tuple-element.93.refs_3_), custom_call_target="tpu_custom_call" | custom-call | flops 268435456 | bytes 2097152 | tf_op jit(solution)/shard_map/pallas_call | solution.py:95
  181.8 0.8 reshape.134
  (70 shorter events, 1.2 us)
Async XLA Ops:
  0.6 47.1 %copy-start = (bf16[32,4,4,256]{3,2,1,0:T(4,128)(2,1)S(1)}, bf16[32,4,4,256]{3,2,1,0:T(4,128)(2,1)}, u32[]{:S(2)}) copy-start(bf16[32,4,4,256]{3,2,1,0:T(4,128)(2,1)} %param.16) | copy-start | bytes 786436
  1.8 31.3 %copy-start.15 = (f32[512,4]{1,0:T(8,128)}, f32[512,4]{1,0:T(8,128)S(1)}, u32[]{:S(2)}) copy-start(f32[512,4]{1,0:T(8,128)S(1)} %copy.26) | copy-start | bytes 24580
  2.2 1.9 %copy-start.16 = (bf16[512,4,256]{2,1,0:T(4,128)(2,1)S(1)}, bf16[512,4,256]{2,1,0:T(4,128)(2,1)}, u32[]{:S(2)}) copy-start(bf16[512,4,256]{2,1,0:T(4,128)(2,1)} %param.12) | copy-start | bytes 3145732
  4.6 6.6 %copy-start.19 = (s32[32,1]{0,1:T(1,128)S(1)}, s32[32,1]{0,1:T(1,128)}, u32[]{:S(2)}) copy-start(s32[32,1]{0,1:T(1,128)} %param.14) | copy-start | bytes 388
  4.7 7.0 %copy-start.17 = (bf16[32,4,4,256]{3,2,1,0:T(4,128)(2,1)S(1)}, bf16[32,4,4,256]{3,2,1,0:T(4,128)(2,1)}, u32[]{:S(2)}) copy-start(bf16[32,4,4,256]{3,2,1,0:T(4,128)(2,1)} %param.15) | copy-start | bytes 786436
  5.7 17.9 %all-to-all-start = ((bf16[16,80,256]{2,1,0:T(8,128)(2,1)}), bf16[16,80,256]{2,1,0:T(8,128)(2,1)S(1)}, u32[]{:S(2)}, u32[]{:S(2)}) async-start(bf16[16,80,256]{2,1,0:T(8,128)(2,1)} %fusion.12), calls=%async_computation | async-start | bytes 1310720 | tf_op jit(solution)/shard_map/all_to_all | solution.py:287
  23.6 9.6 %copy-start.4 = (bf16[16,80,256]{2,1,0:T(8,128)(2,1)}, bf16[16,80,256]{2,1,0:T(8,128)(2,1)S(1)}, u32[]{:S(2)}) copy-start(bf16[16,80,256]{2,1,0:T(8,128)(2,1)S(1)} %all-to-all-done.got_ref) | copy-start | bytes 1966084
  23.6 18.3 %all-to-all-start.2 = ((bf16[16,4,16,256]{3,2,1,0:T(8,128)(2,1)}), bf16[16,4,16,256]{3,2,1,0:T(8,128)(2,1)}, u32[]{:S(2)}, u32[]{:S(2)}) async-start(bf16[16,4,16,256]{3,2,1,0:T(8,128)(2,1)} %shard_map.113), calls=%async_computation.2 | async-start | bytes 1048576 | tf_op jit(solution)/shard_map/all_to_all | solution.py:300
  37.5 10.0 %copy-start.18 = (f32[4,4,32]{2,1,0:T(4,128)S(1)}, f32[4,4,32]{2,1,0:T(4,128)}, u32[]{:S(2)}) copy-start(f32[4,4,32]{2,1,0:T(4,128)} %param.18) | copy-start | bytes 6148
  39.8 1.1 copy-start.5
  41.0 0.8 copy-start.7
  41.8 16.6 %all-to-all-start.1 = ((bf16[16,64,256]{2,1,0:T(8,128)(2,1)}), bf16[16,64,256]{2,1,0:T(8,128)(2,1)}, u32[]{:S(2)}, u32[]{:S(2)}) async-start(bf16[16,64,256]{2,1,0:T(8,128)(2,1)} %copy-done.7), calls=%async_computation.1 | async-start | bytes 1048576 | tf_op jit(solution)/shard_map/all_to_all | solution.py:315
  58.4 1.2 copy-start.3
  59.6 0.9 copy-start.9
  63.4 0.8 copy-start.14
  64.2 27.9 %collective-permute-start.2 = (bf16[512,1024]{1,0:T(8,128)(2,1)}, bf16[512,1024]{1,0:T(8,128)(2,1)}, u32[]{:S(2)}, u32[]{:S(2)}) collective-permute-start(bf16[512,1024]{1,0:T(8,128)(2,1)} %get-tuple-element.63.refs_0_), channel_id=1, source_target_pairs={{0,1},{1,0},{2,3},{3,2},{4,5},{5,4},{6,7},{7,6},{8,9},{9,8},{10,11... | collective-permute-start | bytes 3145736 | tf_op jit(solution)/shard_map/ppermute | solution.py:22
  66.9 26.0 %collective-permute-start.1 = (bf16[512,1024]{1,0:T(8,128)(2,1)}, bf16[512,1024]{1,0:T(8,128)(2,1)S(1)}, u32[]{:S(2)}, u32[]{:S(2)}) collective-permute-start(bf16[512,1024]{1,0:T(8,128)(2,1)} %get-tuple-element.63.refs_0_), channel_id=1, source_target_pairs={{0,6},{1,7},{2,0},{3,1},{4,2},{5,3},{6,4},{7,5},{8,14},{9,15},{10,... | collective-permute-start | bytes 3145736 | tf_op jit(solution)/shard_map/ppermute | solution.py:18
  70.9 25.3 %collective-permute-start = (bf16[512,1024]{1,0:T(8,128)(2,1)}, bf16[512,1024]{1,0:T(8,128)(2,1)S(1)}, u32[]{:S(2)}, u32[]{:S(2)}) collective-permute-start(bf16[512,1024]{1,0:T(8,128)(2,1)} %get-tuple-element.63.refs_0_), channel_id=1, source_target_pairs={{0,2},{1,3},{2,4},{3,5},{4,6},{5,7},{6,0},{7,1},{8,10},{9,11},{10,... | collective-permute-start | bytes 3145736 | tf_op jit(solution)/shard_map/ppermute | solution.py:14
  70.9 30.4 %all-to-all-start.3 = ((bf16[16,4,16,256]{3,2,1,0:T(8,128)(2,1)}), bf16[16,4,16,256]{3,2,1,0:T(8,128)(2,1)S(1)}, u32[]{:S(2)}, u32[]{:S(2)}) async-start(bf16[16,4,16,256]{3,2,1,0:T(8,128)(2,1)} %copy-done.14), calls=%async_computation.3 | async-start | bytes 1048576 | tf_op jit(solution)/shard_map/all_to_all | solution.py:339
  74.5 26.8 %copy-start.8 = (f32[16,8,4,256]{3,1,2,0:T(8,128)S(1)}, f32[16,8,4,256]{3,1,2,0:T(8,128)}, u32[]{:S(2)}) copy-start(f32[16,8,4,256]{3,1,2,0:T(8,128)} %copy.49) | copy-start | bytes 1572868
  79.2 1.3 copy-start.2
  92.9 1.0 copy-start.10
  96.2 1.0 copy-start.12
  97.2 43.0 %collective-permute-start.3 = (bf16[512,1024]{1,0:T(8,128)(2,1)}, bf16[512,1024]{1,0:T(8,128)(2,1)S(1)}, u32[]{:S(2)}, u32[]{:S(2)}) collective-permute-start(bf16[512,1024]{1,0:T(8,128)(2,1)} %collective-permute-done.2.refs_2_), channel_id=1, source_target_pairs={{0,2},{1,3},{2,4},{3,5},{4,6},{5,7},{6,0},{7,1},{8,10},{9,11},{10,... | collective-permute-start | bytes 3145736 | tf_op jit(solution)/shard_map/ppermute | solution.py:14
  97.2 43.0 %collective-permute-start.5 = (bf16[512,1024]{1,0:T(8,128)(2,1)}, bf16[512,1024]{1,0:T(8,128)(2,1)S(1)}, u32[]{:S(2)}, u32[]{:S(2)}) collective-permute-start(bf16[512,1024]{1,0:T(8,128)(2,1)} %copy-done.10), channel_id=1, source_target_pairs={{0,1},{1,0},{2,3},{3,2},{4,5},{5,4},{6,7},{7,6},{8,9},{9,8},{10,11... | collective-permute-start | bytes 3145736 | tf_op jit(solution)/shard_map/ppermute | solution.py:22
  98.7 41.6 %collective-permute-start.4 = (bf16[512,1024]{1,0:T(8,128)(2,1)}, bf16[512,1024]{1,0:T(8,128)(2,1)}, u32[]{:S(2)}, u32[]{:S(2)}) collective-permute-start(bf16[512,1024]{1,0:T(8,128)(2,1)} %copy-done.10), channel_id=1, source_target_pairs={{0,6},{1,7},{2,0},{3,1},{4,2},{5,3},{6,4},{7,5},{8,14},{9,15},{10,... | collective-permute-start | bytes 3145736 | tf_op jit(solution)/shard_map/ppermute | solution.py:18
  102.3 25.2 %collective-permute-start.8 = (bf16[128,1024]{1,0:T(8,128)(2,1)}, bf16[128,1024]{1,0:T(8,128)(2,1)S(1)}, u32[]{:S(2)}, u32[]{:S(2)}) collective-permute-start(bf16[128,1024]{1,0:T(8,128)(2,1)} %shard_map.117.refs_3_), channel_id=1, source_target_pairs={{0,1},{1,0},{2,3},{3,2},{4,5},{5,4},{6,7},{7,6},{8,9},{9,8},{10,11... | collective-permute-start | bytes 786440 | tf_op jit(solution)/shard_map/ppermute | solution.py:22
  105.1 35.1 %collective-permute-start.7 = (bf16[128,1024]{1,0:T(8,128)(2,1)}, bf16[128,1024]{1,0:T(8,128)(2,1)S(1)}, u32[]{:S(2)}, u32[]{:S(2)}) collective-permute-start(bf16[128,1024]{1,0:T(8,128)(2,1)} %shard_map.117.refs_3_), channel_id=1, source_target_pairs={{0,6},{1,7},{2,0},{3,1},{4,2},{5,3},{6,4},{7,5},{8,14},{9,15},{10,... | collective-permute-start | bytes 786440 | tf_op jit(solution)/shard_map/ppermute | solution.py:18
  127.5 12.8 %collective-permute-start.6 = (bf16[128,1024]{1,0:T(8,128)(2,1)}, bf16[128,1024]{1,0:T(8,128)(2,1)S(1)}, u32[]{:S(2)}, u32[]{:S(2)}) collective-permute-start(bf16[128,1024]{1,0:T(8,128)(2,1)} %shard_map.117.refs_3_), channel_id=1, source_target_pairs={{0,2},{1,3},{2,4},{3,5},{4,6},{5,7},{6,0},{7,1},{8,10},{9,11},{10,... | collective-permute-start | bytes 786440 | tf_op jit(solution)/shard_map/ppermute | solution.py:14
  127.5 1.2 copy-start.11
  128.7 1.2 copy-start.13
  138.9 1.3 copy-start.1
  140.3 9.7 %collective-permute-start.12 = (bf16[128,1024]{1,0:T(8,128)(2,1)S(1)}, bf16[128,1024]{1,0:T(8,128)(2,1)S(1)}, u32[]{:S(2)}, u32[]{:S(2)}) collective-permute-start(bf16[128,1024]{1,0:T(8,128)(2,1)S(1)} %collective-permute-done.8.refs_6_), channel_id=1, source_target_pairs={{0,2},{1,3},{2,4},{3,5},{4,6},{5,7},{6,0},{7,1},{8,10},{9,11},{10,... | collective-permute-start | bytes 786440 | tf_op jit(solution)/shard_map/ppermute | solution.py:14
  143.3 22.8 %collective-permute-start.14 = (bf16[128,1024]{1,0:T(8,128)(2,1)S(1)}, bf16[128,1024]{1,0:T(8,128)(2,1)S(1)}, u32[]{:S(2)}, u32[]{:S(2)}) collective-permute-start(bf16[128,1024]{1,0:T(8,128)(2,1)S(1)} %collective-permute-done.7.refs_5_), channel_id=1, source_target_pairs={{0,1},{1,0},{2,3},{3,2},{4,5},{5,4},{6,7},{7,6},{8,9},{9,8},{10,11... | collective-permute-start | bytes 786440 | tf_op jit(solution)/shard_map/ppermute | solution.py:22
  144.1 21.9 %collective-permute-start.13 = (bf16[128,1024]{1,0:T(8,128)(2,1)S(1)}, bf16[128,1024]{1,0:T(8,128)(2,1)S(1)}, u32[]{:S(2)}, u32[]{:S(2)}) collective-permute-start(bf16[128,1024]{1,0:T(8,128)(2,1)S(1)} %collective-permute-done.7.refs_5_), channel_id=1, source_target_pairs={{0,6},{1,7},{2,0},{3,1},{4,2},{5,3},{6,4},{7,5},{8,14},{9,15},{10,... | collective-permute-start | bytes 786440 | tf_op jit(solution)/shard_map/ppermute | solution.py:18
  146.8 19.3 %collective-permute-start.11 = (bf16[160,1024]{1,0:T(8,128)(2,1)S(1)}, bf16[160,1024]{1,0:T(8,128)(2,1)S(1)}, u32[]{:S(2)}, u32[]{:S(2)}) collective-permute-start(bf16[160,1024]{1,0:T(8,128)(2,1)S(1)} %slice.37), channel_id=1, source_target_pairs={{0,1},{1,0},{2,3},{3,2},{4,5},{5,4},{6,7},{7,6},{8,9},{9,8},{10,11... | collective-permute-start | bytes 983048 | tf_op jit(solution)/shard_map/ppermute | solution.py:22
  148.5 17.6 %collective-permute-start.9 = (bf16[176,1024]{1,0:T(8,128)(2,1)S(1)}, bf16[176,1024]{1,0:T(8,128)(2,1)S(1)}, u32[]{:S(2)}, u32[]{:S(2)}) collective-permute-start(bf16[176,1024]{1,0:T(8,128)(2,1)S(1)} %slice.35), channel_id=1, source_target_pairs={{0,2},{1,3},{2,4},{3,5},{4,6},{5,7},{6,0},{7,1},{8,10},{9,11},{10,... | collective-permute-start | bytes 1081352 | tf_op jit(solution)/shard_map/ppermute | solution.py:14
  150.0 16.1 %collective-permute-start.10 = (bf16[176,1024]{1,0:T(8,128)(2,1)S(1)}, bf16[176,1024]{1,0:T(8,128)(2,1)S(1)}, u32[]{:S(2)}, u32[]{:S(2)}) collective-permute-start(bf16[176,1024]{1,0:T(8,128)(2,1)S(1)} %slice.36), channel_id=1, source_target_pairs={{0,6},{1,7},{2,0},{3,1},{4,2},{5,3},{6,4},{7,5},{8,14},{9,15},{10,... | collective-permute-start | bytes 1081352 | tf_op jit(solution)/shard_map/ppermute | solution.py:18
  166.1 12.8 %collective-permute-start.15 = (bf16[64,1024]{1,0:T(8,128)(2,1)S(1)}, bf16[64,1024]{1,0:T(8,128)(2,1)S(1)}, u32[]{:S(2)}, u32[]{:S(2)}) collective-permute-start(bf16[64,1024]{1,0:T(8,128)(2,1)S(1)} %slice.38), channel_id=1, source_target_pairs={{0,2},{1,3},{2,4},{3,5},{4,6},{5,7},{6,0},{7,1},{8,10},{9,11},{10,... | collective-permute-start | bytes 393224 | tf_op jit(solution)/shard_map/ppermute | solution.py:14
  166.5 12.4 %collective-permute-start.16 = (bf16[64,1024]{1,0:T(8,128)(2,1)S(1)}, bf16[64,1024]{1,0:T(8,128)(2,1)S(1)}, u32[]{:S(2)}, u32[]{:S(2)}) collective-permute-start(bf16[64,1024]{1,0:T(8,128)(2,1)S(1)} %slice.39), channel_id=1, source_target_pairs={{0,6},{1,7},{2,0},{3,1},{4,2},{5,3},{6,4},{7,5},{8,14},{9,15},{10,... | collective-permute-start | bytes 393224 | tf_op jit(solution)/shard_map/ppermute | solution.py:18
  169.4 1.6 copy-start.6

commit v3 on v2

v3 whole, which is shorter than its diff:
```python
import jax
import jax.numpy as jnp
from jax import lax
from jax.experimental import pallas as pl
from jax.experimental.pallas import tpu as pltpu
from jax.sharding import PartitionSpec as P

TILE = 256
BF, F32 = jnp.bfloat16, jnp.float32
WHOLE = pl.BlockSpec(memory_space=pltpu.VMEM)


def up(a):
    return lax.ppermute(a, "head", [(h, (h + 2) % 8) for h in range(8)])


def down(a):
    return lax.ppermute(a, "head", [(h, (h - 2) % 8) for h in range(8)])


def across(a):
    return lax.ppermute(a, "head", [(h, h ^ 1) for h in range(8)])


def after(values, *others):
    return lax.optimization_barrier((values, others))[0]


def call(body, out, ins, flops, limit=6 << 20):
    size = sum(a.size * a.dtype.itemsize for a in (*ins, *out))
    return pl.pallas_call(
        body,
        in_specs=[WHOLE] * len(ins),
        out_specs=[WHOLE] * len(out),
        out_shape=list(out),
        compiler_params=pltpu.CompilerParams(vmem_limit_bytes=limit),
        cost_estimate=pl.CostEstimate(flops=flops, bytes_accessed=size, transcendentals=0),
    )(*ins)


def project(total, srcs, terms, heads, w, split=None):
    width, tile = srcs[0].shape[1], TILE
    columns, n_slot = w.shape[1], len(heads)
    old = [] if isinstance(total, int) else [total]
    rows = total if isinstance(total, int) else total.shape[0]

    def body(heads_ref, *refs):
        src_refs, w_ref, refs = refs[: len(srcs)], refs[len(srcs)], refs[len(srcs) + 1 :]
        old_refs, out_refs, (w_held, arrived) = refs[: len(old)], refs[len(old) : -2], refs[-2:]
        copies = []
        for slot in range(n_slot):
            first = pl.multiple_of(heads_ref[slot] * width, width)
            copies.append(
                pltpu.make_async_copy(
                    w_ref.at[pl.ds(first, width), :], w_held.at[slot], arrived.at[slot]
                )
            )
            copies[-1].start()
        for slot in range(n_slot):
            copies[slot].wait()
            mine = [t for t in terms if t[0] == slot]

            @pl.loop(0, columns // tile)
            def _(j, slot=slot, mine=mine):
                cols = pl.ds(pl.multiple_of(j * tile, tile), tile)
                for _, i, s0, n, a0 in mine:
                    part = jnp.dot(
                        src_refs[i][s0 : s0 + n, :],
                        w_held[slot, :, cols],
                        preferred_element_type=F32,
                    )
                    if slot:
                        part += out_refs[0][a0 : a0 + n, cols]
                    elif old:
                        part += old_refs[0][a0 : a0 + n, cols]
                    if split is None:
                        out_refs[0][a0 : a0 + n, cols] = part
                    else:
                        top = min(max(split - a0, 0), n)
                        if top:
                            out_refs[0][a0 : a0 + top, cols] = part[:top].astype(BF)
                        if top < n:
                            below = a0 + top - split
                            out_refs[1][below : below + n - top, cols] = part[top:].astype(BF)

    if split is None:
        out = [jax.ShapeDtypeStruct((rows, columns), F32)]
    else:
        out = [jax.ShapeDtypeStruct((r, columns), BF) for r in (split, rows - split)]
    flops = sum(2 * t[3] * width * columns for t in terms)
    return pl.pallas_call(
        body,
        in_specs=[pl.BlockSpec(memory_space=pltpu.SMEM)]
        + [WHOLE] * len(srcs)
        + [pl.BlockSpec(memory_space=pltpu.HBM)]
        + [WHOLE] * len(old),
        out_specs=[WHOLE] * len(out),
        out_shape=out,
        scratch_shapes=[
            pltpu.VMEM((n_slot, width, columns), BF),
            pltpu.SemaphoreType.DMA((n_slot,)),
        ],
        compiler_params=pltpu.CompilerParams(vmem_limit_bytes=46 << 20),
        cost_estimate=pl.CostEstimate(
            flops=flops, bytes_accessed=n_slot * 2 * width * columns, transcendentals=0
        ),
    )(jnp.stack(heads).astype(jnp.int32), *srcs, w, *old)


NT = (((1,), (1,)), ((), ()))


def scan_and_read(got, slice_rows, slots):
    sections, _, dim = got.shape
    head_rows, piece = got.shape[1] - slice_rows - slots, slots * slice_rows // dim
    packs = dim // 128

    def body(got_ref, out_ref, ends):
        state = jnp.zeros((slice_rows, dim), F32)
        for c in range(sections):
            out_ref[c, :slice_rows, :] = state.astype(BF)
            header = got_ref[c, slice_rows : slice_rows + 16, :].astype(F32)
            factor = header[0:1] + header[1:2] + header[2:3]
            state = factor * state + got_ref[c, :slice_rows, :].astype(F32)
            ends[c * slice_rows : (c + 1) * slice_rows, :] = state.astype(BF)
        lane = lax.broadcasted_iota(jnp.int32, (slots, 128), 1)
        row = lax.broadcasted_iota(jnp.int32, (slots, 128), 0)
        upper = (lane >= slice_rows).astype(F32)
        low = lax.broadcasted_iota(jnp.int32, (piece, 128), 1) < slice_rows

        @pl.loop(0, sections)
        def _(c):
            asked = got_ref[c, slice_rows + head_rows :, :]
            reads = lax.dot_general(asked, ends[...], NT, preferred_element_type=F32)
            header = got_ref[c, slice_rows : slice_rows + 16, :].astype(F32)
            named = jnp.where(row == lane, header[3:4, :128], 0.0).sum(axis=1, keepdims=True)
            wanted = named - upper
            total = jnp.zeros((slots, 128), F32)
            for j in range(0, sections, 2):
                part = reads[:, j * slice_rows : (j + 2) * slice_rows]
                total += jnp.where(wanted == float(j), part, 0.0)
            total += pltpu.roll(total, slice_rows, 1)
            for p in range(packs):
                first = total[2 * p * piece : (2 * p + 1) * piece]
                second = total[(2 * p + 1) * piece : (2 * p + 2) * piece]
                out_ref[c, slice_rows:, p * 128 : (p + 1) * 128] = jnp.where(
                    low, first, second
                ).astype(BF)

    return pl.pallas_call(
        body,
        in_specs=[WHOLE],
        out_specs=WHOLE,
        out_shape=jax.ShapeDtypeStruct((sections, slice_rows + piece, dim), BF),
        scratch_shapes=[pltpu.VMEM((sections * slice_rows, dim), BF)],
        compiler_params=pltpu.CompilerParams(vmem_limit_bytes=12 << 20),
        cost_estimate=pl.CostEstimate(
            flops=2 * sections * slots * sections * slice_rows * dim,
            bytes_accessed=6 << 20,
            transcendentals=0,
        ),
    )(got)


def retain(queries, within, gains, got, slice_rows, own, kept):
    sections, _, dim = got.shape
    tokens, width = queries.shape
    slots, heads = kept.shape
    per_head = sections // heads
    piece = got.shape[1] - slice_rows

    def body(q_ref, in_ref, g_ref, got_ref, own_ref, k_ref, o_ref):
        low = lax.broadcasted_iota(jnp.int32, (piece, 128), 1) < slice_rows
        for h in range(heads):
            cols = slice(h * dim, (h + 1) * dim)
            state = got_ref[h * per_head : (h + 1) * per_head, :slice_rows, :].reshape(dim, dim)
            carried = lax.dot_general(q_ref[:, cols], state, NT, preferred_element_type=F32)
            total = in_ref[:, cols] + g_ref[:, h : h + 1] * carried
            o_ref[:tokens, cols] = total.astype(BF)
            for b in range(slots // piece):
                rows = slice(b * piece, (b + 1) * piece)
                for p in range(dim // 128):
                    halves = []
                    for side in range(2):
                        held = got_ref[
                            h * per_head + 2 * p + side,
                            slice_rows:,
                            b // 2 * 128 : (b // 2 + 1) * 128,
                        ].astype(F32)
                        halves.append(held if b % 2 == side else pltpu.roll(held, slice_rows, 1))
                    read = jnp.where(low, halves[0], halves[1])
                    at = slice(h * dim + p * 128, h * dim + (p + 1) * 128)
                    mixed = k_ref[rows, h : h + 1] * read + own_ref[rows, at]
                    o_ref[tokens + b * piece : tokens + (b + 1) * piece, at] = mixed.astype(BF)

    out = jax.ShapeDtypeStruct((tokens + slots, width), BF)
    flops = 2 * tokens * width * dim
    return call(body, [out], [queries, within, gains, got, own, kept], flops, 12 << 20)[0]


def gathered_projection(block, split, w):
    me = lax.axis_index("head")
    z, x = me // 2, me % 2
    here, far = lambda d: ((z + d) % 4) * 2 + x, lambda d: ((z + d) % 4) * 2 + 1 - x
    n = block.shape[0]
    third = -(-n // 48) * 16
    whole = lambda s: (s, s, 0, n, 0)

    a1, a2, a3 = up(block), down(block), across(block)
    (total,) = project(n, [block], [whole(0)], [me], w)
    a1, a2, a3, total = lax.optimization_barrier((a1, a2, a3, total))

    b1, b2, b3 = up(a3), down(a2), across(a2)
    (total,) = project(
        total, [a1, a2, a3], [whole(s) for s in range(3)], [here(-1), here(1), far(0)], w
    )
    b1, b2, b3, total = lax.optimization_barrier((b1, b2, b3, total))

    c1, c2, c3 = up(b1[:third]), down(b3[third : 2 * third]), across(b2[2 * third :])
    (total,) = project(
        total, [b1, b2, b3], [whole(s) for s in range(3)], [far(-1), here(2), far(1)], w
    )
    c1, c2, c3, total = lax.optimization_barrier((c1, c2, c3, total))
    return project(
        total,
        [c1, c2, c3],
        [(0, i, 0, c.shape[0], i * third) for i, c in enumerate((c1, c2, c3))],
        [far(2)],
        w,
        split,
    )


def shards(
    q_prompt,
    k_prompt,
    v_prompt,
    log_decay,
    prompt_section,
    q_step,
    k_step,
    v_step,
    step_decay,
    w_out,
):
    tokens, heads, dim = q_prompt.shape
    sections = lax.axis_size("ctx")
    rows, steps = q_step.shape[:2]

    at = jnp.arange(tokens)
    upto = (at[:, None] <= at[None, :]).astype(F32)
    cumlog = jnp.dot(log_decay, upto, precision=lax.Precision.HIGHEST)
    last_log = cumlog[:, -1]
    keys = (k_prompt.astype(F32) * jnp.exp(last_log[:, None] - cumlog).T[:, :, None]).astype(BF)
    own_state = jnp.einsum("jxp,jxa->xpa", v_prompt, keys, preferred_element_type=F32)
    total_decay = jnp.exp(last_log)
    slice_rows, slots = heads * dim // sections, rows * steps
    high = lax.reduce_precision(total_decay, 8, 7)
    middle = lax.reduce_precision(total_decay - high, 8, 7)
    parts = jnp.stack([high, middle, total_decay - high - middle], axis=1).astype(BF)
    parts = jnp.broadcast_to(parts[:, None, :, None], (heads, sections // heads, 3, dim))
    named = jnp.broadcast_to(prompt_section, (rows, steps)).reshape(1, 1, slots).astype(BF)
    named = jnp.pad(named, ((0, 0), (0, 0), (0, dim - slots)))
    named = jnp.broadcast_to(named, (sections, 1, dim))
    header = jnp.concatenate([parts.reshape(sections, 3, dim), named], axis=1)
    header = jnp.pad(header, ((0, 0), (0, 12), (0, 0)))
    asked = q_step.reshape(slots, heads, dim).transpose(1, 0, 2)
    asked = jnp.broadcast_to(asked[:, None], (heads, sections // heads, slots, dim))
    sent = jnp.concatenate(
        [
            own_state.astype(BF).reshape(sections, slice_rows, dim),
            header,
            asked.reshape(sections, slots, dim),
        ],
        axis=1,
    )
    got = lax.all_to_all(sent, "ctx", 0, 0)

    q_late, k_late, v_late, cum_late = after((q_prompt, k_prompt, v_prompt, cumlog), sent)
    causal = at[:, None] >= at[None, :]
    decays = jnp.where(
        causal[None], jnp.exp(jnp.minimum(cum_late[:, :, None] - cum_late[:, None, :], 0.0)), 0.0
    )
    scores = jnp.einsum("jsv,csv->sjc", q_late, k_late, preferred_element_type=F32)
    weights = (scores * decays).astype(BF)
    within = jnp.einsum("hnm,mhe->nhe", weights, v_late, preferred_element_type=F32)
    within = within.reshape(tokens, heads * dim)
    queries = q_late.reshape(tokens, heads * dim)
    gains = jnp.exp(cum_late).T
    got, within, queries, gains = lax.optimization_barrier((got, within, queries, gains))

    sent = scan_and_read(got, slice_rows, slots)
    got = lax.all_to_all(sent, "ctx", 0, 0)

    q_own, k_own, v_own, rates = after((q_step, k_step, v_step, step_decay), sent)
    rates = jnp.transpose(rates, (2, 1, 0))
    logs = [rates[:, 0]]
    for t in range(1, steps):
        logs.append(logs[-1] + rates[:, t])
    step_logs = jnp.stack(logs, axis=1)
    head_logs = jnp.transpose(step_logs, (0, 2, 1))
    turn = jnp.arange(steps)
    seen = turn[:, None] >= turn[None, :]
    gaps = head_logs[:, :, :, None] - head_logs[:, :, None, :]
    step_gains = jnp.where(seen[None, None], jnp.exp(jnp.minimum(gaps, 0.0)), 0.0)
    own = jnp.einsum("rthd,ruhd->rhtu", q_own, k_own, preferred_element_type=F32)
    own = jnp.einsum("rhtu,ruhe->rthe", own * step_gains, v_own.astype(F32))
    own = own.reshape(slots, heads * dim)
    kept = jnp.exp(step_logs).reshape(slots, heads)
    got, own, kept = lax.optimization_barrier((got, own, kept))

    block = retain(queries, within, gains, got, slice_rows, own, kept)
    prompt_out, step_out = gathered_projection(block, tokens, w_out)
    return prompt_out, step_out.reshape(rows, steps, w_out.shape[1])


def solution(mesh):
    in_specs = (
        P("ctx", "head", None),
        P("ctx", "head", None),
        P("ctx", "head", None),
        P("head", "ctx"),
        P("ctx", None),
        P("ctx", None, "head", None),
        P("ctx", None, "head", None),
        P("ctx", None, "head", None),
        P("head", None, "ctx"),
        P(None, "head"),
    )
    out_specs = (P("ctx", "head"), P("ctx", None, "head"))
    return jax.shard_map(shards, mesh=mesh, in_specs=in_specs, out_specs=out_specs, check_vma=False)
```

time: 184 us -> 165 us (0.90)
  starting transfers between devices: 46.1 us -> 26.9 us
  waiting for transfers between devices: 53.8 us -> 61.4 us
  local copies, waits for them, and re-layouts: 24.6 us -> 20.6 us
    ppermute x5 -> x3, waiting for transfers between devices: 33.9 us -> 19.1 us  [across(): return lax.ppermute(a, 'head', [(h, h ^ 1) for h in range(8)])]
    ppermute x6 -> x3, waiting for transfers between devices: 2.35 us -> 16.2 us  [up(): return lax.ppermute(a, 'head', [(h, (h + 2) % 8) for h in range(8)])]
    all_to_all x3 -> x0, starting transfers between devices: 13.4 us -> none  [the longest x1 5.64 us: shards(): entry = lax.all_to_all(entries, 'ctx', 0, 0).reshape(heads, dim, dim)]
    all_to_all x1 -> x2, waiting for transfers between devices: 10.5 us -> 23.7 us  [shards(): got = lax.all_to_all(sent, 'ctx', 0, 0)]
    unnamed x44 -> x29, local copies, waits for them, and re-layouts: 17 us -> 9.54 us
    pallas_call x5 -> x4, Pallas kernels: 38.7 us -> 31.4 us  [project(): pl.pallas_call(body, in_specs=[pl.BlockSpec(memory_space=pltpu.SMEM)] + [...]
    all_to_all x3 -> x0, waiting for transfers between devices: 6.21 us -> none  [the longest x1 6.2 us: shards(): entry = lax.all_to_all(entries, 'ctx', 0, 0).reshape(heads, dim, dim)]
    pallas_call x1, Pallas kernels: 2.8 us -> 7.76 us  [scan_and_read(): pl.pallas_call(body, in_specs=[WHOLE], out_specs=WHOLE, out_shape=jax.Sha...]
  transfers between devices with their start and end apart: 21 -> 11, of which waited for: 6 -> 7; matrix products, arithmetic and copies ran while one was open for 10% -> 8% of each run, Pallas kernels for 21% -> 16%
where the time goes in v3:
time: 165 us; the launch traced here: 164 us
  waiting for transfers between devices  61.4 us (37%)
  Pallas kernels  42 us (25%)
  starting transfers between devices  26.9 us (16%)
  local copies, waits for them, and re-layouts  20.6 us (12%)
  matrix products  8.86 us (5%)
  other arithmetic  3.27 us (2%)
    pallas_call x4, Pallas kernels, project(): pl.pallas_call(body, in_specs=[pl.BlockSpec(memory_space=pltpu.SMEM)] + [...  31.4 us
    all_to_all x2, waiting for transfers between devices, shards(): got = lax.all_to_all(sent, 'ctx', 0, 0)  23.7 us
    ppermute x3, waiting for transfers between devices, across(): return lax.ppermute(a, 'head', [(h, h ^ 1) for h in range(8)])  19.1 us
    ppermute x3, waiting for transfers between devices, up(): return lax.ppermute(a, 'head', [(h, (h + 2) % 8) for h in range(8)])  16.2 us
    ppermute x3, starting transfers between devices, down(): return lax.ppermute(a, 'head', [(h, (h - 2) % 8) for h in range(8)])  11 us
    all_to_all x2, starting transfers between devices, shards(): got = lax.all_to_all(sent, 'ctx', 0, 0)  10 us
    unnamed x29, local copies, waits for them, and re-layouts  9.54 us
    pallas_call x1, Pallas kernels, scan_and_read(): pl.pallas_call(body, in_specs=[WHOLE], out_specs=WHOLE, out_shape=jax.Sha...  7.76 us
  transfers between devices with their start and end apart: 11, of which 7 were waited for; matrix products, arithmetic and copies ran while one was open for 8% of the time, Pallas kernels for 16%

profile of v3, /device:TPU:0, one launch (start us, length us, event | category | flops | bytes accessed | tf_op | source)
XLA Modules:
  0.0 163.9 jit_solution(17168289539064817898)
XLA Ops:
  0.6 0.0 copy-start
  0.6 0.0 copy-start.10
  0.7 0.0 copy-start.12
  0.7 0.8 convert_bitcast_fusion
  1.5 0.1 broadcast_in_dim.33
  1.6 0.1 convert_element_type.50
  1.7 1.0 fusion.8
  2.7 0.2 copy.27
  2.8 0.0 copy-start.8
  2.9 0.1 subtract_exponential_fusion
  3.0 0.1 copy.48
  3.1 0.1 copy.28
  3.2 1.0 copy.32
  4.2 0.1 broadcast_in_dim.32
  4.4 0.7 multiply_convert_fusion.1
  5.1 0.6 convolution_convert_fusion
  5.7 0.1 broadcast_in_dim.36
  5.8 1.3 pad_maximum_fusion
  7.1 5.8 %all-to-all-start = ((bf16[16,208,256]{2,1,0:T(8,128)(2,1)}), bf16[16,208,256]{2,1,0:T(8,128)(2,1)}, u32[]{:S(2)}, u32[]{:S(2)}) async-start(bf16[16,208,256]{2,1,0:T(8,128)(2,1)} %pad_maximum_fusion), calls=%async_computation | async-start | bytes 3407872 | tf_op jit(solution)/shard_map/all_to_all | solution.py:277
  12.9 0.1 copy.33
  13.0 0.2 copy.49
  13.3 0.1 iota_compare_fusion
  13.3 5.0 %fusion = f32[4,256,512]{2,1,0:T(8,128)} fusion(f32[4,512]{1,0:T(4,128)S(1)} %copy.33, pred[512,512]{1,0:T(8,128)(4,1)S(1)} %iota_compare_fusion, bf16[512,4,256]{2,1,0:T(4,128)(2,1)} %param.11, bf16[512,4,256]{2,1,0:T(4,128)(2,1)S(1)} %copy-done.9, bf16[512,4,256]{2,1,0:T(4,128)(2,1)} %param.12), kind=kOutput, calls=%fused_computation.3 | convolution fusion | flops 1078984704 | bytes 5513216 | tf_op jit(solution)/shard_map/hnm,mhe->nhe/dot_general | solution.py:286
  18.4 1.9 %copy.47.in_ref = f32[512,1024]{1,0:T(8,128)S(1)} copy(f32[512,1024]{0,1:T(8,128)} %bitcast.45) | data formatting | bytes 4194304 | tf_op jit(solution)/shard_map/reshape | solution.py:287
  20.3 1.7 %exponential_bitcast_fusion.g_ref = f32[512,4]{1,0:T(8,128)} fusion(f32[4,512]{0,1:T(8,128)} %bitcast.44), kind=kLoop, calls=%fused_computation.25 | loop fusion | bytes 16384 | tf_op jit(solution)/shard_map/transpose | solution.py:289
  22.0 14.6 %all-to-all-done.got_ref = bf16[16,208,256]{2,1,0:T(8,128)(2,1)} async-done(((bf16[16,208,256]{2,1,0:T(8,128)(2,1)}), bf16[16,208,256]{2,1,0:T(8,128)(2,1)}, u32[]{:S(2)}, u32[]{:S(2)}) %all-to-all-start) | async-done | bytes 1703968 | tf_op jit(solution)/shard_map/all_to_all | solution.py:277
  36.6 7.8 %shard_map.113 = bf16[16,96,256]{2,1,0:T(8,128)(2,1)S(1)} custom-call(bf16[16,208,256]{2,1,0:T(8,128)(2,1)} %all-to-all-done.got_ref), custom_call_target="tpu_custom_call" | custom-call | flops 1073741824 | bytes 6291456 | tf_op jit(solution)/shard_map/pallas_call | solution.py:150
  44.4 0.0 copy-start.7
  44.4 0.9 copy-done.7
  45.3 4.3 %all-to-all-start.1 = ((bf16[16,96,256]{2,1,0:T(8,128)(2,1)}), bf16[16,96,256]{2,1,0:T(8,128)(2,1)}, u32[]{:S(2)}, u32[]{:S(2)}) async-start(bf16[16,96,256]{2,1,0:T(8,128)(2,1)} %copy-done.7), calls=%async_computation.1 | async-start | bytes 1572864 | tf_op jit(solution)/shard_map/all_to_all | solution.py:293
  49.6 0.1 copy.41
  49.8 0.1 copy.37
  49.9 2.3 %convolution_bitcast_fusion = f32[32,4,4,256]{3,1,2,0:T(4,128)} fusion(bf16[32,4,4,256]{3,2,1,0:T(4,128)(2,1)S(1)} %copy-done, bf16[32,4,4,256]{3,2,1,0:T(4,128)(2,1)} %param.15, bf16[32,4,4,256]{3,2,1,0:T(4,128)(2,1)} %param.17, f32[32,4,4]{2,1,0:T(4,128)S(1)} %copy.37, pred[4,4]{1,0:T(4,128)(4,1)S(1)} %iota_compare_fusion.4), kind=kOutput, calls=%fused_computation.5 | convolution fusion | flops 2105344 | bytes 1312784 | tf_op jit(solution)/shard_map/rhtu,ruhe->rthe/dot_general | solution.py:307
  52.2 1.2 copy.40
  53.4 0.9 copy.50
  54.3 9.0 %all-to-all-done.1.got_ref = bf16[16,96,256]{2,1,0:T(8,128)(2,1)} async-done(((bf16[16,96,256]{2,1,0:T(8,128)(2,1)}), bf16[16,96,256]{2,1,0:T(8,128)(2,1)}, u32[]{:S(2)}, u32[]{:S(2)}) %all-to-all-start.1) | async-done | bytes 786464 | tf_op jit(solution)/shard_map/all_to_all | solution.py:293
  63.4 1.0 copy-done.3
  64.4 0.9 copy-done.6
  65.3 2.8 %shard_map.114.refs_0_ = bf16[640,1024]{1,0:T(8,128)(2,1)} custom-call(bf16[512,1024]{1,0:T(8,128)(2,1)S(1)} %bitcast.38, f32[512,1024]{1,0:T(8,128)S(1)} %copy.47.in_ref, f32[512,4]{1,0:T(8,128)S(1)} %copy-done.6, bf16[16,96,256]{2,1,0:T(8,128)(2,1)} %all-to-all-done.1.got_ref, f32[128,1024]{1,0:T(8,128)S(1)} %bitcast.39, f32[128,4]{1,0:T(8,128)S(1)} %bitcast.40), custom_call_target="tpu_custom_call" | custom-call | flops 268435456 | bytes 5777408 | tf_op jit(solution)/shard_map/pallas_call | solution.py:31
  68.2 2.7 %collective-permute-start.2 = (bf16[640,1024]{1,0:T(8,128)(2,1)}, bf16[640,1024]{1,0:T(8,128)(2,1)}, u32[]{:S(2)}, u32[]{:S(2)}) collective-permute-start(bf16[640,1024]{1,0:T(8,128)(2,1)} %shard_map.114.refs_0_), channel_id=1, source_target_pairs={{0,1},{1,0},{2,3},{3,2},{4,5},{5,4},{6,7},{7,6},{8,9},{9,8},{10,11... | collective-permute-start | bytes 3932168 | tf_op jit(solution)/shard_map/ppermute | solution.py:22
  70.9 4.0 %collective-permute-start.1 = (bf16[640,1024]{1,0:T(8,128)(2,1)}, bf16[640,1024]{1,0:T(8,128)(2,1)}, u32[]{:S(2)}, u32[]{:S(2)}) collective-permute-start(bf16[640,1024]{1,0:T(8,128)(2,1)} %shard_map.114.refs_0_), channel_id=1, source_target_pairs={{0,6},{1,7},{2,0},{3,1},{4,2},{5,3},{6,4},{7,5},{8,14},{9,15},{10,... | collective-permute-start | bytes 3932168 | tf_op jit(solution)/shard_map/ppermute | solution.py:18
  74.9 5.1 %shard_map.115.refs_4_ = f32[640,1024]{1,0:T(8,128)S(1)} custom-call(s32[1]{0:T(128)} %bitcast.17.heads_ref, bf16[640,1024]{1,0:T(8,128)(2,1)} %shard_map.114.refs_0_, bf16[8192,1024]{1,0:T(8,128)(2,1)} %refs_3_.5), custom_call_target="tpu_custom_call" | custom-call | flops 1342177280 | bytes 2097152 | tf_op jit(solution)/shard_map/pallas_call | solution.py:91
  80.0 1.5 copy-done.1
  81.5 18.8 %collective-permute-done.2.refs_2_ = bf16[640,1024]{1,0:T(8,128)(2,1)} collective-permute-done((bf16[640,1024]{1,0:T(8,128)(2,1)}, bf16[640,1024]{1,0:T(8,128)(2,1)}, u32[]{:S(2)}, u32[]{:S(2)}) %collective-permute-start.2) | collective-permute-done | bytes 1310752 | tf_op jit(solution)/shard_map/ppermute | solution.py:22
  100.3 2.5 %collective-permute-done.1.refs_1_ = bf16[640,1024]{1,0:T(8,128)(2,1)} collective-permute-done((bf16[640,1024]{1,0:T(8,128)(2,1)}, bf16[640,1024]{1,0:T(8,128)(2,1)}, u32[]{:S(2)}, u32[]{:S(2)}) %collective-permute-start.1) | collective-permute-done | bytes 1310752 | tf_op jit(solution)/shard_map/ppermute | solution.py:18
  102.8 3.3 %collective-permute-done.refs_0_ = bf16[640,1024]{1,0:T(8,128)(2,1)S(1)} collective-permute-done((bf16[640,1024]{1,0:T(8,128)(2,1)}, bf16[640,1024]{1,0:T(8,128)(2,1)S(1)}, u32[]{:S(2)}, u32[]{:S(2)}) %collective-permute-start) | collective-permute-done | bytes 1310752 | tf_op jit(solution)/shard_map/ppermute | solution.py:14
  106.1 1.1 copy-done.4
  107.2 0.8 collective-permute-start.5
  108.0 3.2 %collective-permute-start.4 = (bf16[640,1024]{1,0:T(8,128)(2,1)}, bf16[640,1024]{1,0:T(8,128)(2,1)}, u32[]{:S(2)}, u32[]{:S(2)}) collective-permute-start(bf16[640,1024]{1,0:T(8,128)(2,1)} %collective-permute-done.1.refs_1_), channel_id=1, source_target_pairs={{0,6},{1,7},{2,0},{3,1},{4,2},{5,3},{6,4},{7,5},{8,14},{9,15},{10,... | collective-permute-start | bytes 3932168 | tf_op jit(solution)/shard_map/ppermute | solution.py:18
  111.2 0.1 pad_add_fusion.heads_ref
  111.3 1.3 copy-done.5
  112.6 10.4 %shard_map.116.refs_4_ = f32[640,1024]{1,0:T(8,128)S(1)} custom-call(s32[3]{0:T(128)S(1)} %pad_add_fusion.heads_ref, bf16[640,1024]{1,0:T(8,128)(2,1)S(1)} %copy-done.5, bf16[640,1024]{1,0:T(8,128)(2,1)} %collective-permute-done.1.refs_1_, bf16[640,1024]{1,0:T(8,128)(2,1)} %collective-permute-done.2.refs_2_, bf16[8192,1024]{1,0:T(8,128)(2,1)} %refs_3_.5, ...), custom_call_target="tpu_custom_call" | custom-call | flops 4026531840 | bytes 6291456 | tf_op jit(solution)/shard_map/pallas_call | solution.py:91
  123.1 1.5 copy-done.2
  124.6 12.9 %collective-permute-done.3.refs_0_ = bf16[640,1024]{1,0:T(8,128)(2,1)S(1)} collective-permute-done((bf16[640,1024]{1,0:T(8,128)(2,1)}, bf16[640,1024]{1,0:T(8,128)(2,1)S(1)}, u32[]{:S(2)}, u32[]{:S(2)}) %collective-permute-start.3) | collective-permute-done | bytes 1310752 | tf_op jit(solution)/shard_map/ppermute | solution.py:14
  137.4 0.3 collective-permute-done.5.refs_2_
  137.7 1.8 %slice.31 = bf16[192,1024]{1,0:T(8,128)(2,1)} slice(bf16[640,1024]{1,0:T(8,128)(2,1)} %collective-permute-done.4.refs_1_), slice={[448:640], [0:1024]} | slice | bytes 786432 | tf_op jit(solution)/shard_map/slice | solution.py:219
  139.5 0.8 slice.30
  140.3 0.8 slice.29
  141.1 2.3 %collective-permute-start.8 = (bf16[192,1024]{1,0:T(8,128)(2,1)}, bf16[192,1024]{1,0:T(8,128)(2,1)}, u32[]{:S(2)}, u32[]{:S(2)}) collective-permute-start(bf16[192,1024]{1,0:T(8,128)(2,1)} %slice.31), channel_id=1, source_target_pairs={{0,1},{1,0},{2,3},{3,2},{4,5},{5,4},{6,7},{7,6},{8,9},{9,8},{10,11... | collective-permute-start | bytes 1179656 | tf_op jit(solution)/shard_map/ppermute | solution.py:22
  143.5 3.7 %collective-permute-start.7 = (bf16[224,1024]{1,0:T(8,128)(2,1)}, bf16[224,1024]{1,0:T(8,128)(2,1)}, u32[]{:S(2)}, u32[]{:S(2)}) collective-permute-start(bf16[224,1024]{1,0:T(8,128)(2,1)} %slice.30), channel_id=1, source_target_pairs={{0,6},{1,7},{2,0},{3,1},{4,2},{5,3},{6,4},{7,5},{8,14},{9,15},{10,... | collective-permute-start | bytes 1376264 | tf_op jit(solution)/shard_map/ppermute | solution.py:18
  147.1 0.1 pad_add_fusion.1.heads_ref
  147.2 10.0 %shard_map.117.refs_4_ = f32[640,1024]{1,0:T(8,128)S(1)} custom-call(s32[3]{0:T(128)S(1)} %pad_add_fusion.1.heads_ref, bf16[640,1024]{1,0:T(8,128)(2,1)S(1)} %collective-permute-done.3.refs_0_, bf16[640,1024]{1,0:T(8,128)(2,1)} %collective-permute-done.4.refs_1_, bf16[640,1024]{1,0:T(8,128)(2,1)S(1)} %collective-permute-done.5.refs_2_, ...), custom_call_target="tpu_custom_call" | custom-call | flops 4026531840 | bytes 6291456 | tf_op jit(solution)/shard_map/pallas_call | solution.py:91
  157.3 5.8 %shard_map.118 = (bf16[512,1024]{1,0:T(8,128)(2,1)}, bf16[128,1024]{1,0:T(8,128)(2,1)S(1)}) custom-call(s32[1]{0:T(128)} %bitcast.heads_ref, bf16[224,1024]{1,0:T(8,128)(2,1)S(1)} %collective-permute-done.6.refs_0_, bf16[224,1024]{1,0:T(8,128)(2,1)} %collective-permute-done.7.refs_1_, bf16[192,1024]{1,0:T(8,128)(2,1)} %collective-permute-done.8.refs_2_, ...), custom_call_target="tpu_custom_call" | custom-call | flops 1342177280 | bytes 2097152 | tf_op jit(solution)/shard_map/pallas_call | solution.py:91
  163.1 0.8 reshape.105
  (30 shorter events, 0.2 us)
Async XLA Ops:
  0.6 49.2 %copy-start = (bf16[32,4,4,256]{3,2,1,0:T(4,128)(2,1)S(1)}, bf16[32,4,4,256]{3,2,1,0:T(4,128)(2,1)}, u32[]{:S(2)}) copy-start(bf16[32,4,4,256]{3,2,1,0:T(4,128)(2,1)} %param.16) | copy-start | bytes 786436
  0.6 3.7 %copy-start.10 = (bf16[512,4,256]{2,1,0:T(4,128)(2,1)S(1)}, bf16[512,4,256]{2,1,0:T(4,128)(2,1)}, u32[]{:S(2)}) copy-start(bf16[512,4,256]{2,1,0:T(4,128)(2,1)} %param.11) | copy-start | bytes 3145732
  0.7 4.5 %copy-start.12 = (bf16[512,4,256]{2,1,0:T(4,128)(2,1)S(1)}, bf16[512,4,256]{2,1,0:T(4,128)(2,1)}, u32[]{:S(2)}) copy-start(bf16[512,4,256]{2,1,0:T(4,128)(2,1)} %param.12) | copy-start | bytes 3145732
  2.8 10.1 %copy-start.8 = (f32[512,4]{1,0:T(8,128)}, f32[512,4]{1,0:T(8,128)S(1)}, u32[]{:S(2)}) copy-start(f32[512,4]{1,0:T(8,128)S(1)} %copy.27) | copy-start | bytes 24580
  7.1 5.9 %copy-start.9 = (bf16[512,4,256]{2,1,0:T(4,128)(2,1)S(1)}, bf16[512,4,256]{2,1,0:T(4,128)(2,1)}, u32[]{:S(2)}) copy-start(bf16[512,4,256]{2,1,0:T(4,128)(2,1)} %param.10) | copy-start | bytes 3145732
  7.1 29.5 %all-to-all-start = ((bf16[16,208,256]{2,1,0:T(8,128)(2,1)}), bf16[16,208,256]{2,1,0:T(8,128)(2,1)}, u32[]{:S(2)}, u32[]{:S(2)}) async-start(bf16[16,208,256]{2,1,0:T(8,128)(2,1)} %pad_maximum_fusion), calls=%async_computation | async-start | bytes 3407872 | tf_op jit(solution)/shard_map/all_to_all | solution.py:277
  36.6 13.0 %copy-start.11 = (f32[4,4,32]{2,1,0:T(4,128)S(1)}, f32[4,4,32]{2,1,0:T(4,128)}, u32[]{:S(2)}) copy-start(f32[4,4,32]{2,1,0:T(4,128)} %param.18) | copy-start | bytes 6148
  44.4 0.9 copy-start.7
  45.3 18.1 %all-to-all-start.1 = ((bf16[16,96,256]{2,1,0:T(8,128)(2,1)}), bf16[16,96,256]{2,1,0:T(8,128)(2,1)}, u32[]{:S(2)}, u32[]{:S(2)}) async-start(bf16[16,96,256]{2,1,0:T(8,128)(2,1)} %copy-done.7), calls=%async_computation.1 | async-start | bytes 1572864 | tf_op jit(solution)/shard_map/all_to_all | solution.py:293
  63.3 1.0 copy-start.3
  64.4 0.9 copy-start.6
  68.2 32.1 %collective-permute-start.2 = (bf16[640,1024]{1,0:T(8,128)(2,1)}, bf16[640,1024]{1,0:T(8,128)(2,1)}, u32[]{:S(2)}, u32[]{:S(2)}) collective-permute-start(bf16[640,1024]{1,0:T(8,128)(2,1)} %shard_map.114.refs_0_), channel_id=1, source_target_pairs={{0,1},{1,0},{2,3},{3,2},{4,5},{5,4},{6,7},{7,6},{8,9},{9,8},{10,11... | collective-permute-start | bytes 3932168 | tf_op jit(solution)/shard_map/ppermute | solution.py:22
  70.9 31.9 %collective-permute-start.1 = (bf16[640,1024]{1,0:T(8,128)(2,1)}, bf16[640,1024]{1,0:T(8,128)(2,1)}, u32[]{:S(2)}, u32[]{:S(2)}) collective-permute-start(bf16[640,1024]{1,0:T(8,128)(2,1)} %shard_map.114.refs_0_), channel_id=1, source_target_pairs={{0,6},{1,7},{2,0},{3,1},{4,2},{5,3},{6,4},{7,5},{8,14},{9,15},{10,... | collective-permute-start | bytes 3932168 | tf_op jit(solution)/shard_map/ppermute | solution.py:18
  74.9 31.2 %collective-permute-start = (bf16[640,1024]{1,0:T(8,128)(2,1)}, bf16[640,1024]{1,0:T(8,128)(2,1)S(1)}, u32[]{:S(2)}, u32[]{:S(2)}) collective-permute-start(bf16[640,1024]{1,0:T(8,128)(2,1)} %shard_map.114.refs_0_), channel_id=1, source_target_pairs={{0,2},{1,3},{2,4},{3,5},{4,6},{5,7},{6,0},{7,1},{8,10},{9,11},{10,... | collective-permute-start | bytes 3932168 | tf_op jit(solution)/shard_map/ppermute | solution.py:14
  80.0 1.5 copy-start.1
  106.1 1.1 copy-start.4
  107.2 30.3 %collective-permute-start.3 = (bf16[640,1024]{1,0:T(8,128)(2,1)}, bf16[640,1024]{1,0:T(8,128)(2,1)S(1)}, u32[]{:S(2)}, u32[]{:S(2)}) collective-permute-start(bf16[640,1024]{1,0:T(8,128)(2,1)} %collective-permute-done.2.refs_2_), channel_id=1, source_target_pairs={{0,2},{1,3},{2,4},{3,5},{4,6},{5,7},{6,0},{7,1},{8,10},{9,11},{10,... | collective-permute-start | bytes 3932168 | tf_op jit(solution)/shard_map/ppermute | solution.py:14
  107.2 30.5 %collective-permute-start.5 = (bf16[640,1024]{1,0:T(8,128)(2,1)}, bf16[640,1024]{1,0:T(8,128)(2,1)S(1)}, u32[]{:S(2)}, u32[]{:S(2)}) collective-permute-start(bf16[640,1024]{1,0:T(8,128)(2,1)} %collective-permute-done.1.refs_1_), channel_id=1, source_target_pairs={{0,1},{1,0},{2,3},{3,2},{4,5},{5,4},{6,7},{7,6},{8,9},{9,8},{10,11... | collective-permute-start | bytes 3932168 | tf_op jit(solution)/shard_map/ppermute | solution.py:22
  108.0 29.8 %collective-permute-start.4 = (bf16[640,1024]{1,0:T(8,128)(2,1)}, bf16[640,1024]{1,0:T(8,128)(2,1)}, u32[]{:S(2)}, u32[]{:S(2)}) collective-permute-start(bf16[640,1024]{1,0:T(8,128)(2,1)} %collective-permute-done.1.refs_1_), channel_id=1, source_target_pairs={{0,6},{1,7},{2,0},{3,1},{4,2},{5,3},{6,4},{7,5},{8,14},{9,15},{10,... | collective-permute-start | bytes 3932168 | tf_op jit(solution)/shard_map/ppermute | solution.py:18
  111.3 1.3 copy-start.5
  123.1 1.5 copy-start.2
  141.1 16.1 %collective-permute-start.8 = (bf16[192,1024]{1,0:T(8,128)(2,1)}, bf16[192,1024]{1,0:T(8,128)(2,1)}, u32[]{:S(2)}, u32[]{:S(2)}) collective-permute-start(bf16[192,1024]{1,0:T(8,128)(2,1)} %slice.31), channel_id=1, source_target_pairs={{0,1},{1,0},{2,3},{3,2},{4,5},{5,4},{6,7},{7,6},{8,9},{9,8},{10,11... | collective-permute-start | bytes 1179656 | tf_op jit(solution)/shard_map/ppermute | solution.py:22
  143.4 13.8 %collective-permute-start.6 = (bf16[224,1024]{1,0:T(8,128)(2,1)}, bf16[224,1024]{1,0:T(8,128)(2,1)S(1)}, u32[]{:S(2)}, u32[]{:S(2)}) collective-permute-start(bf16[224,1024]{1,0:T(8,128)(2,1)} %slice.29), channel_id=1, source_target_pairs={{0,2},{1,3},{2,4},{3,5},{4,6},{5,7},{6,0},{7,1},{8,10},{9,11},{10,... | collective-permute-start | bytes 1376264 | tf_op jit(solution)/shard_map/ppermute | solution.py:14
  143.5 13.8 %collective-permute-start.7 = (bf16[224,1024]{1,0:T(8,128)(2,1)}, bf16[224,1024]{1,0:T(8,128)(2,1)}, u32[]{:S(2)}, u32[]{:S(2)}) collective-permute-start(bf16[224,1024]{1,0:T(8,128)(2,1)} %slice.30), channel_id=1, source_target_pairs={{0,6},{1,7},{2,0},{3,1},{4,2},{5,3},{6,4},{7,5},{8,14},{9,15},{10,... | collective-permute-start | bytes 1376264 | tf_op jit(solution)/shard_map/ppermute | solution.py:18

commit v4 on v3

v4 whole, which is shorter than its diff:
```python
import jax
import jax.numpy as jnp
from jax import lax
from jax.experimental import pallas as pl
from jax.experimental.pallas import tpu as pltpu
from jax.sharding import PartitionSpec as P

BF, F32 = jnp.bfloat16, jnp.float32
WHOLE = pl.BlockSpec(memory_space=pltpu.VMEM)


def up(a):
    return lax.ppermute(a, "head", [(h, (h + 2) % 8) for h in range(8)])


def down(a):
    return lax.ppermute(a, "head", [(h, (h - 2) % 8) for h in range(8)])


def across(a):
    return lax.ppermute(a, "head", [(h, h ^ 1) for h in range(8)])


def after(values, *others):
    return lax.optimization_barrier((values, others))[0]


def project(total, srcs, terms, heads, w, split=None):
    width, columns = srcs[0].shape[1], w.shape[1]
    n_slot = 0 if heads is None else len(heads)
    old = [] if isinstance(total, int) else [total]
    rows = total if isinstance(total, int) else total.shape[0]

    def add(slot, weights, src_refs, old_refs, out_refs):
        for s, i, s0, n, a0 in terms:
            if s != slot:
                continue
            part = jnp.dot(src_refs[i][s0 : s0 + n, :], weights, preferred_element_type=F32)
            if slot:
                part += out_refs[0][a0 : a0 + n, :]
            elif old:
                part += old_refs[0][a0 : a0 + n, :]
            if split is None:
                out_refs[0][a0 : a0 + n, :] = part
                continue
            top = min(max(split - a0, 0), n)
            if top:
                out_refs[0][a0 : a0 + top, :] = part[:top].astype(BF)
            if top < n:
                below = a0 + top - split
                out_refs[1][below : below + n - top, :] = part[top:].astype(BF)

    def body(*refs):
        if heads is None:
            src_refs, w_ref, refs = refs[: len(srcs)], refs[len(srcs)], refs[len(srcs) + 1 :]
            add(0, w_ref[...], src_refs, refs[: len(old)], refs[len(old) :])
            return
        heads_ref, *refs = refs
        src_refs, w_ref, refs = refs[: len(srcs)], refs[len(srcs)], refs[len(srcs) + 1 :]
        w_held, arrived = refs[-2:]
        copies = []
        for slot in range(n_slot):
            first = pl.multiple_of(heads_ref[slot] * width, width)
            copies.append(
                pltpu.make_async_copy(
                    w_ref.at[pl.ds(first, width), :], w_held.at[slot], arrived.at[slot]
                )
            )
            copies[-1].start()
        for slot in range(n_slot):
            copies[slot].wait()
            add(slot, w_held[slot], src_refs, refs[: len(old)], refs[len(old) : -2])

    if split is None:
        out = [jax.ShapeDtypeStruct((rows, columns), F32)]
    else:
        out = [jax.ShapeDtypeStruct((r, columns), BF) for r in (split, rows - split)]
    flops = sum(2 * t[3] * width * columns for t in terms)
    cost = pl.CostEstimate(
        flops=flops, bytes_accessed=max(n_slot, 1) * 2 * width * columns, transcendentals=0
    )
    if heads is None:
        return pl.pallas_call(
            body,
            in_specs=[WHOLE] * (len(srcs) + 1 + len(old)),
            out_specs=[WHOLE] * len(out),
            out_shape=out,
            compiler_params=pltpu.CompilerParams(vmem_limit_bytes=16 << 20),
            cost_estimate=cost,
        )(*srcs, w, *old)
    return pl.pallas_call(
        body,
        in_specs=[pl.BlockSpec(memory_space=pltpu.SMEM)]
        + [WHOLE] * len(srcs)
        + [pl.BlockSpec(memory_space=pltpu.HBM)]
        + [WHOLE] * len(old),
        out_specs=[WHOLE] * len(out),
        out_shape=out,
        scratch_shapes=[
            pltpu.VMEM((n_slot, width, columns), BF),
            pltpu.SemaphoreType.DMA((n_slot,)),
        ],
        compiler_params=pltpu.CompilerParams(vmem_limit_bytes=42 << 20),
        cost_estimate=cost,
    )(jnp.stack(heads).astype(jnp.int32), *srcs, w, *old)


def cut(pieces):
    def body(*refs):
        k = len(pieces)
        copies = [
            pltpu.make_async_copy(
                refs[i].at[pl.ds(start, n), :], refs[k + i], refs[2 * k].at[i]
            )
            for i, (_, start, n) in enumerate(pieces)
        ]
        for copy in copies:
            copy.start()
        for copy in copies:
            copy.wait()

    return pl.pallas_call(
        body,
        in_specs=[pl.BlockSpec(memory_space=pl.ANY)] * len(pieces),
        out_specs=[pl.BlockSpec(memory_space=pl.ANY)] * len(pieces),
        out_shape=[jax.ShapeDtypeStruct((n, a.shape[1]), a.dtype) for a, _, n in pieces],
        scratch_shapes=[pltpu.SemaphoreType.DMA((len(pieces),))],
        cost_estimate=pl.CostEstimate(flops=0, bytes_accessed=3 << 20, transcendentals=0),
    )(*[a for a, _, _ in pieces])


NT = (((1,), (1,)), ((), ()))


def scan_and_read(got, slice_rows, slots):
    sections, _, dim = got.shape
    head_rows, half = got.shape[1] - slice_rows - slots, slice_rows // 2

    def body(got_ref, out_ref, ends):
        state = jnp.zeros((slice_rows, dim), F32)
        for c in range(sections):
            out_ref[c, :slice_rows, :] = state.astype(BF)
            header = got_ref[c, slice_rows : slice_rows + 16, :].astype(F32)
            factor = header[0:1] + header[1:2] + header[2:3]
            state = factor * state + got_ref[c, :slice_rows, :].astype(F32)
            ends[c * slice_rows : (c + 1) * slice_rows, :] = state.astype(BF)

        @pl.loop(0, sections // 2)
        def _(p):
            asked, named = [], []
            for c in (2 * p, 2 * p + 1):
                asked.append(got_ref[c, slice_rows + head_rows :, :])
                header = got_ref[c, slice_rows : slice_rows + 16, :].astype(F32)
                named.append(header[3:4, :slots])
            asked, named = jnp.concatenate(asked, axis=0), jnp.concatenate(named, axis=1)
            total = jnp.zeros((slice_rows, 2 * slots), F32)
            for j in range(0, sections, 4):
                reads = lax.dot_general(
                    ends[j * slice_rows : (j + 4) * slice_rows, :],
                    asked,
                    NT,
                    preferred_element_type=F32,
                )
                for i in range(4):
                    part = reads[i * slice_rows : (i + 1) * slice_rows]
                    total += jnp.where(named == float(j + i), part, 0.0)
            total = total.astype(BF)
            for k in range(2):
                mine = total[:, k * slots : (k + 1) * slots]
                out_ref[2 * p + k, slice_rows:, :slots] = mine[:half]
                out_ref[2 * p + k, slice_rows:, slots:] = mine[half:]

    return pl.pallas_call(
        body,
        in_specs=[WHOLE],
        out_specs=WHOLE,
        out_shape=jax.ShapeDtypeStruct((sections, slice_rows + half, dim), BF),
        scratch_shapes=[pltpu.VMEM((sections * slice_rows, dim), BF)],
        compiler_params=pltpu.CompilerParams(vmem_limit_bytes=12 << 20),
        cost_estimate=pl.CostEstimate(
            flops=2 * sections * slots * sections * slice_rows * dim,
            bytes_accessed=6 << 20,
            transcendentals=0,
        ),
    )(got)


def retain(queries, within, logs, got, slice_rows, own, kept):
    sections, _, dim = got.shape
    tokens, width = queries.shape
    slots, heads = kept.shape
    per_head = sections // heads

    def body(q_ref, in_ref, l_ref, got_ref, own_ref, k_ref, o_ref, own_held, arrived):
        fetch = pltpu.make_async_copy(own_ref, own_held, arrived)
        fetch.start()
        gains = jnp.exp(l_ref[...])
        gains = jnp.concatenate([gains] * (8 // heads), axis=0).T
        for h in range(heads):
            cols = slice(h * dim, (h + 1) * dim)
            state = got_ref[h * per_head : (h + 1) * per_head, :slice_rows, :].reshape(dim, dim)
            carried = lax.dot_general(q_ref[:, cols], state, NT, preferred_element_type=F32)
            total = in_ref[:, cols] + gains[:, h : h + 1] * carried
            o_ref[:tokens, cols] = total.astype(BF)
        fetch.wait()
        for h in range(heads):
            cols = slice(h * dim, (h + 1) * dim)
            parts = []
            for c in range(h * per_head, (h + 1) * per_head):
                held = got_ref[c, slice_rows:, :].astype(F32)
                parts += [held[:, :slots], held[:, slots:]]
            read = jnp.concatenate(parts, axis=0).T
            mixed = k_ref[:, h : h + 1] * read + own_held[:, cols]
            o_ref[tokens:, cols] = mixed.astype(BF)

    specs = [WHOLE] * 6
    specs[4] = pl.BlockSpec(memory_space=pl.ANY)
    return pl.pallas_call(
        body,
        in_specs=specs,
        out_specs=WHOLE,
        out_shape=jax.ShapeDtypeStruct((tokens + slots, width), BF),
        scratch_shapes=[pltpu.VMEM(own.shape, F32), pltpu.SemaphoreType.DMA],
        compiler_params=pltpu.CompilerParams(vmem_limit_bytes=12 << 20),
        cost_estimate=pl.CostEstimate(
            flops=2 * tokens * width * dim, bytes_accessed=6 << 20, transcendentals=0
        ),
    )(queries, within, logs, got, own, kept)


def gathered_projection(block, split, w):
    me = lax.axis_index("head")
    z, x = me // 2, me % 2
    here, far = lambda d: ((z + d) % 4) * 2 + x, lambda d: ((z + d) % 4) * 2 + 1 - x
    n = block.shape[0]
    third = -(-n // 48) * 16
    whole = lambda s: (s, s, 0, n, 0)

    a1, a2, a3 = up(block), down(block), across(block)
    (total,) = project(n, [block], [whole(0)], [me], w)
    a1, a2, a3, total = lax.optimization_barrier((a1, a2, a3, total))

    b1, b2, b3 = up(a3), down(a2), across(a2)
    width = block.shape[1]
    w_last = lax.dynamic_slice_in_dim(after(w, total), far(2) * width, width, 0)
    (total,) = project(
        total, [a1, a2, a3], [whole(s) for s in range(3)], [here(-1), here(1), far(0)], w
    )
    b1, b2, b3, total, w_last = lax.optimization_barrier((b1, b2, b3, total, w_last))

    c1, c2, c3 = cut([(b1, 0, third), (b3, third, third), (b2, 2 * third, n - 2 * third)])
    c1, c2, c3 = up(c1), down(c2), across(c3)
    (total,) = project(
        total, [b1, b2, b3], [whole(s) for s in range(3)], [far(-1), here(2), far(1)], w
    )
    c1, c2, c3, total = lax.optimization_barrier((c1, c2, c3, total))
    return project(
        total,
        [c1, c2, c3],
        [(0, i, 0, c.shape[0], i * third) for i, c in enumerate((c1, c2, c3))],
        None,
        w_last,
        split,
    )


def shards(
    q_prompt,
    k_prompt,
    v_prompt,
    log_decay,
    prompt_section,
    q_step,
    k_step,
    v_step,
    step_decay,
    w_out,
):
    tokens, heads, dim = q_prompt.shape
    sections = lax.axis_size("ctx")
    rows, steps = q_step.shape[:2]

    at = jnp.arange(tokens)
    upto = (at[:, None] <= at[None, :]).astype(F32)
    cumlog = jnp.dot(log_decay, upto, precision=lax.Precision.HIGHEST)
    last_log = cumlog[:, -1]
    keys = (k_prompt.astype(F32) * jnp.exp(last_log[:, None] - cumlog).T[:, :, None]).astype(BF)
    own_state = jnp.einsum("jxp,jxa->xpa", v_prompt, keys, preferred_element_type=F32)
    total_decay = jnp.exp(last_log)
    slice_rows, slots = heads * dim // sections, rows * steps
    high = lax.reduce_precision(total_decay, 8, 7)
    middle = lax.reduce_precision(total_decay - high, 8, 7)
    parts = jnp.stack([high, middle, total_decay - high - middle], axis=1).astype(BF)
    parts = jnp.broadcast_to(parts[:, None, :, None], (heads, sections // heads, 3, dim))
    named = jnp.broadcast_to(prompt_section, (rows, steps)).reshape(1, 1, slots).astype(BF)
    named = jnp.pad(named, ((0, 0), (0, 0), (0, dim - slots)))
    named = jnp.broadcast_to(named, (sections, 1, dim))
    header = jnp.concatenate([parts.reshape(sections, 3, dim), named], axis=1)
    header = jnp.pad(header, ((0, 0), (0, 12), (0, 0)))
    asked = q_step.reshape(slots, heads, dim).transpose(1, 0, 2)
    asked = jnp.broadcast_to(asked[:, None], (heads, sections // heads, slots, dim))
    sent = jnp.concatenate(
        [
            own_state.astype(BF).reshape(sections, slice_rows, dim),
            header,
            asked.reshape(sections, slots, dim),
        ],
        axis=1,
    )
    got = lax.all_to_all(sent, "ctx", 0, 0)

    q_late, k_late, v_late, cum_late = after((q_prompt, k_prompt, v_prompt, cumlog), sent)
    causal = at[:, None] >= at[None, :]
    decays = jnp.where(
        causal[None], jnp.exp(jnp.minimum(cum_late[:, :, None] - cum_late[:, None, :], 0.0)), 0.0
    )
    scores = jnp.einsum("jsv,csv->sjc", q_late, k_late, preferred_element_type=F32)
    weights = (scores * decays).astype(BF)
    within = jnp.einsum("hnm,mhe->nhe", weights, v_late, preferred_element_type=F32)
    within = within.reshape(tokens, heads * dim)
    queries = q_late.reshape(tokens, heads * dim)
    got, within, queries, cum_late = lax.optimization_barrier((got, within, queries, cum_late))

    sent = scan_and_read(got, slice_rows, slots)
    got = lax.all_to_all(sent, "ctx", 0, 0)

    q_own, k_own, v_own, rates = after((q_step, k_step, v_step, step_decay), sent)
    rates = jnp.transpose(rates, (2, 1, 0))
    logs = [rates[:, 0]]
    for t in range(1, steps):
        logs.append(logs[-1] + rates[:, t])
    step_logs = jnp.stack(logs, axis=1)
    head_logs = jnp.transpose(step_logs, (0, 2, 1))
    turn = jnp.arange(steps)
    seen = turn[:, None] >= turn[None, :]
    gaps = head_logs[:, :, :, None] - head_logs[:, :, None, :]
    step_gains = jnp.where(seen[None, None], jnp.exp(jnp.minimum(gaps, 0.0)), 0.0)
    own = jnp.einsum("rthd,ruhd->rhtu", q_own, k_own, preferred_element_type=F32)
    own = jnp.einsum("rhtu,ruhe->rthe", own * step_gains, v_own.astype(F32))
    own = own.reshape(slots, heads * dim)
    kept = jnp.exp(step_logs).reshape(slots, heads)
    got, own, kept = lax.optimization_barrier((got, own, kept))

    block = retain(queries, within, cum_late, got, slice_rows, own, kept)
    prompt_out, step_out = gathered_projection(block, tokens, w_out)
    return prompt_out, step_out.reshape(rows, steps, w_out.shape[1])


def solution(mesh):
    in_specs = (
        P("ctx", "head", None),
        P("ctx", "head", None),
        P("ctx", "head", None),
        P("head", "ctx"),
        P("ctx", None),
        P("ctx", None, "head", None),
        P("ctx", None, "head", None),
        P("ctx", None, "head", None),
        P("head", None, "ctx"),
        P(None, "head"),
    )
    out_specs = (P("ctx", "head"), P("ctx", None, "head"))
    return jax.shard_map(shards, mesh=mesh, in_specs=in_specs, out_specs=out_specs, check_vma=False)
```

time: 165 us -> 193 us (1.17)
  Pallas kernels: 42 us -> 72.3 us
  local copies, waits for them, and re-layouts: 20.6 us -> 13.4 us
  waiting for transfers between devices: 61.4 us -> 64.8 us
  other arithmetic: 3.27 us -> 5.76 us
    pallas_call x1 -> x3, Pallas kernels: 2.83 us -> 46.3 us  [the longest x1 40.8 us: cut(): pl.pallas_call(body, in_specs=[pl.BlockSpec(memory_space=pl.ANY)] * len(p...]
    pallas_call x4 -> x3, Pallas kernels: 31.4 us -> 21.6 us  [project(): pl.pallas_call(body, in_specs=[pl.BlockSpec(memory_space=pltpu.SMEM)] + [...]
    unnamed x29 -> x22, local copies, waits for them, and re-layouts: 9.54 us -> 4.56 us
    slice x3 -> x0, local copies, waits for them, and re-layouts: 3.38 us -> none  [the longest x1 1.77 us: gathered_projection(): b2[2 * third:]]
    pallas_call x1, Pallas kernels: 7.76 us -> 4.41 us  [scan_and_read(): pl.pallas_call(body, in_specs=[WHOLE], out_specs=WHOLE, out_shape=jax.Sha...]
    dynamic_slice x0 -> x1, local copies, waits for them, and re-layouts: none -> 3.12 us  [gathered_projection(): w_last = lax.dynamic_slice_in_dim(after(w, total), far(2) * width, width, 0)]
    ppermute x3, waiting for transfers between devices: 19.1 us -> 21.2 us  [across(): return lax.ppermute(a, 'head', [(h, h ^ 1) for h in range(8)])]
  transfers between devices with their start and end apart: 11 -> 11, of which waited for: 7 -> 7; matrix products, arithmetic and copies ran while one was open for 8% -> 8% of each run, Pallas kernels for 16% -> 11%
where the time goes in v4:
time: 193 us
  Pallas kernels  72.3 us (37%)
  waiting for transfers between devices  64.8 us (34%)
  starting transfers between devices  26.9 us (14%)
  local copies, waits for them, and re-layouts  13.4 us (7%)
  matrix products  8.59 us (4%)
  other arithmetic  5.76 us (3%)
    pallas_call x1, Pallas kernels, cut(): pl.pallas_call(body, in_specs=[pl.BlockSpec(memory_space=pl.ANY)] * len(p...  40.8 us
    all_to_all x2, waiting for transfers between devices, shards(): got = lax.all_to_all(sent, 'ctx', 0, 0)  24.6 us
    pallas_call x3, Pallas kernels, project(): pl.pallas_call(body, in_specs=[pl.BlockSpec(memory_space=pltpu.SMEM)] + [...  21.6 us
    ppermute x3, waiting for transfers between devices, across(): return lax.ppermute(a, 'head', [(h, h ^ 1) for h in range(8)])  21.2 us
    ppermute x3, waiting for transfers between devices, up(): return lax.ppermute(a, 'head', [(h, (h + 2) % 8) for h in range(8)])  16.6 us
    ppermute x3, starting transfers between devices, down(): return lax.ppermute(a, 'head', [(h, (h - 2) % 8) for h in range(8)])  10.9 us
    all_to_all x2, starting transfers between devices, shards(): got = lax.all_to_all(sent, 'ctx', 0, 0)  10 us
    ppermute x3, starting transfers between devices, across(): return lax.ppermute(a, 'head', [(h, h ^ 1) for h in range(8)])  5.92 us
  transfers between devices with their start and end apart: 11, of which 7 were waited for; matrix products, arithmetic and copies ran while one was open for 8% of the time, Pallas kernels for 11%

profile of v4, /device:TPU:0, one launch (start us, length us, event | category | flops | bytes accessed | tf_op | source)
XLA Modules:
  0.0 192.7 jit_solution(16785864938408298746)
XLA Ops:
  0.6 0.0 copy-start
  0.6 0.0 copy-start.9
  0.7 0.8 convert_bitcast_fusion
  1.4 0.1 broadcast_in_dim.33
  1.5 0.1 convert_element_type.50
  1.6 1.0 fusion.8
  2.6 0.2 slice_reduce_fusion
  2.8 0.1 subtract_exponential_fusion
  2.9 0.2 copy.25
  3.1 1.0 copy.30
  4.0 0.1 pad_maximum_fusion.2
  4.1 0.1 broadcast_in_dim.32
  4.3 1.8 multiply_convert_fusion.1
  6.1 0.6 convolution_convert_fusion
  6.6 0.1 broadcast_in_dim.36
  6.7 1.3 pad_maximum_fusion
  8.1 5.8 %all-to-all-start = ((bf16[16,208,256]{2,1,0:T(8,128)(2,1)}), bf16[16,208,256]{2,1,0:T(8,128)(2,1)}, u32[]{:S(2)}, u32[]{:S(2)}) async-start(bf16[16,208,256]{2,1,0:T(8,128)(2,1)} %pad_maximum_fusion), calls=%async_computation | async-start | bytes 3407872 | tf_op jit(solution)/shard_map/all_to_all | solution.py:310
  13.9 0.2 copy.45
  14.1 0.8 iota_compare_fusion
  14.9 0.0 copy-done.7
  14.9 4.8 %fusion = f32[4,256,512]{2,1,0:T(8,128)} fusion(f32[4,512]{1,0:T(4,128)S(1)} %bitcast.37, pred[512,512]{1,0:T(8,128)(4,1)} %iota_compare_fusion, bf16[512,4,256]{2,1,0:T(4,128)(2,1)S(1)} %copy-done.7, bf16[512,4,256]{2,1,0:T(4,128)(2,1)S(1)} %copy-done.6, bf16[512,4,256]{2,1,0:T(4,128)(2,1)} %param.12), kind=kOutput, calls=%fused_computation.3 | convolution fusion | flops 1078984704 | bytes 5513216 | tf_op jit(solution)/shard_map/hnm,mhe->nhe/dot_general | solution.py:319
  19.6 1.9 copy.43.in_ref
  21.6 16.0 %all-to-all-done.got_ref = bf16[16,208,256]{2,1,0:T(8,128)(2,1)} async-done(((bf16[16,208,256]{2,1,0:T(8,128)(2,1)}), bf16[16,208,256]{2,1,0:T(8,128)(2,1)}, u32[]{:S(2)}, u32[]{:S(2)}) %all-to-all-start) | async-done | bytes 1703968 | tf_op jit(solution)/shard_map/all_to_all | solution.py:310
  37.6 4.4 %shard_map.113 = bf16[16,96,256]{2,1,0:T(8,128)(2,1)S(1)} custom-call(bf16[16,208,256]{2,1,0:T(8,128)(2,1)} %all-to-all-done.got_ref), custom_call_target="tpu_custom_call" | custom-call | flops 1073741824 | bytes 6291456 | tf_op jit(solution)/shard_map/pallas_call | solution.py:173
  42.0 0.0 copy-start.5
  42.0 0.9 copy-done.5
  42.9 4.3 %all-to-all-start.1 = ((bf16[16,96,256]{2,1,0:T(8,128)(2,1)}), bf16[16,96,256]{2,1,0:T(8,128)(2,1)}, u32[]{:S(2)}, u32[]{:S(2)}) async-start(bf16[16,96,256]{2,1,0:T(8,128)(2,1)} %copy-done.5), calls=%async_computation.1 | async-start | bytes 1572864 | tf_op jit(solution)/shard_map/all_to_all | solution.py:325
  47.2 0.5 iota_compare_fusion.4
  47.7 0.1 copy.37
  47.9 0.1 copy.33
  48.0 2.3 %convolution_bitcast_fusion = f32[32,4,4,256]{3,1,2,0:T(4,128)} fusion(bf16[32,4,4,256]{3,2,1,0:T(4,128)(2,1)S(1)} %copy-done, bf16[32,4,4,256]{3,2,1,0:T(4,128)(2,1)} %param.15, bf16[32,4,4,256]{3,2,1,0:T(4,128)(2,1)} %param.17, f32[32,4,4]{2,1,0:T(4,128)S(1)} %copy.33, pred[4,4]{1,0:T(4,128)(4,1)} %iota_compare_fusion.4), kind=kOutput, calls=%fused_computation.5 | convolution fusion | flops 2105344 | bytes 1312784 | tf_op jit(solution)/shard_map/rhtu,ruhe->rthe/dot_general | solution.py:339
  50.3 1.2 copy.36
  51.5 0.9 copy.46
  52.4 8.6 %all-to-all-done.1.got_ref = bf16[16,96,256]{2,1,0:T(8,128)(2,1)} async-done(((bf16[16,96,256]{2,1,0:T(8,128)(2,1)}), bf16[16,96,256]{2,1,0:T(8,128)(2,1)}, u32[]{:S(2)}, u32[]{:S(2)}) %all-to-all-start.1) | async-done | bytes 786464 | tf_op jit(solution)/shard_map/all_to_all | solution.py:325
  61.0 1.0 copy-done.4
  62.0 3.0 %shard_map.114.refs_1_ = bf16[640,1024]{1,0:T(8,128)(2,1)} custom-call(bf16[512,1024]{1,0:T(8,128)(2,1)S(1)} %bitcast.33, f32[512,1024]{1,0:T(8,128)S(1)} %copy.43.in_ref, f32[4,512]{1,0:T(4,128)S(1)} %bitcast.38, bf16[16,96,256]{2,1,0:T(8,128)(2,1)} %all-to-all-done.1.got_ref, f32[128,1024]{1,0:T(8,128)S(1)} %bitcast.34, f32[128,4]{1,0:T(8,128)S(1)} %bitcast.35), custom_call_target="tpu_custom_call" | custom-call | flops 268435456 | bytes 6291456 | tf_op jit(solution)/shard_map/pallas_call | solution.py:218
  65.0 2.8 %collective-permute-start.2 = (bf16[640,1024]{1,0:T(8,128)(2,1)}, bf16[640,1024]{1,0:T(8,128)(2,1)}, u32[]{:S(2)}, u32[]{:S(2)}) collective-permute-start(bf16[640,1024]{1,0:T(8,128)(2,1)} %shard_map.114.refs_1_), channel_id=1, source_target_pairs={{0,1},{1,0},{2,3},{3,2},{4,5},{5,4},{6,7},{7,6},{8,9},{9,8},{10,11... | collective-permute-start | bytes 3932168 | tf_op jit(solution)/shard_map/ppermute | solution.py:21
  67.9 4.0 %collective-permute-start.1 = (bf16[640,1024]{1,0:T(8,128)(2,1)}, bf16[640,1024]{1,0:T(8,128)(2,1)}, u32[]{:S(2)}, u32[]{:S(2)}) collective-permute-start(bf16[640,1024]{1,0:T(8,128)(2,1)} %shard_map.114.refs_1_), channel_id=1, source_target_pairs={{0,6},{1,7},{2,0},{3,1},{4,2},{5,3},{6,4},{7,5},{8,14},{9,15},{10,... | collective-permute-start | bytes 3932168 | tf_op jit(solution)/shard_map/ppermute | solution.py:17
  71.9 0.0 collective-permute-start
  71.9 4.5 %shard_map.115.refs_5_ = f32[640,1024]{1,0:T(8,128)S(1)} custom-call(s32[1]{0:T(128)} %bitcast.14.refs_0_, bf16[640,1024]{1,0:T(8,128)(2,1)} %shard_map.114.refs_1_, bf16[8192,1024]{1,0:T(8,128)(2,1)} %refs_4_.3), custom_call_target="tpu_custom_call" | custom-call | flops 1342177280 | bytes 2097152 | tf_op jit(solution)/shard_map/pallas_call | solution.py:91
  76.4 20.9 %collective-permute-done.2.refs_3_ = bf16[640,1024]{1,0:T(8,128)(2,1)} collective-permute-done((bf16[640,1024]{1,0:T(8,128)(2,1)}, bf16[640,1024]{1,0:T(8,128)(2,1)}, u32[]{:S(2)}, u32[]{:S(2)}) %collective-permute-start.2) | collective-permute-done | bytes 1310752 | tf_op jit(solution)/shard_map/ppermute | solution.py:21
  97.3 2.5 %collective-permute-done.1.refs_2_ = bf16[640,1024]{1,0:T(8,128)(2,1)} collective-permute-done((bf16[640,1024]{1,0:T(8,128)(2,1)}, bf16[640,1024]{1,0:T(8,128)(2,1)}, u32[]{:S(2)}, u32[]{:S(2)}) %collective-permute-start.1) | collective-permute-done | bytes 1310752 | tf_op jit(solution)/shard_map/ppermute | solution.py:17
  99.8 3.4 %collective-permute-done.refs_1_ = bf16[640,1024]{1,0:T(8,128)(2,1)} collective-permute-done((bf16[640,1024]{1,0:T(8,128)(2,1)}, bf16[640,1024]{1,0:T(8,128)(2,1)}, u32[]{:S(2)}, u32[]{:S(2)}) %collective-permute-start) | collective-permute-done | bytes 1310752 | tf_op jit(solution)/shard_map/ppermute | solution.py:13
  103.2 0.0 collective-permute-start.3
  103.2 0.8 collective-permute-start.5
  104.0 3.2 %collective-permute-start.4 = (bf16[640,1024]{1,0:T(8,128)(2,1)}, bf16[640,1024]{1,0:T(8,128)(2,1)}, u32[]{:S(2)}, u32[]{:S(2)}) collective-permute-start(bf16[640,1024]{1,0:T(8,128)(2,1)} %collective-permute-done.1.refs_2_), channel_id=1, source_target_pairs={{0,6},{1,7},{2,0},{3,1},{4,2},{5,3},{6,4},{7,5},{8,14},{9,15},{10,... | collective-permute-start | bytes 3932168 | tf_op jit(solution)/shard_map/ppermute | solution.py:17
  107.2 0.1 pad_add_fusion.refs_0_
  107.3 3.1 %constant_dynamic-slice_fusion.refs_3_ = bf16[1024,1024]{1,0:T(8,128)(2,1)} fusion(bf16[8192,1024]{1,0:T(8,128)(2,1)} %refs_4_.3, s32[]{:T(128)S(6)} %select_n.52), kind=kLoop, calls=%fused_computation.50 | loop fusion | bytes 4194308 | tf_op jit(solution)/shard_map/dynamic_slice | solution.py:245
  110.4 8.5 %shard_map.116.refs_5_ = f32[640,1024]{1,0:T(8,128)S(1)} custom-call(s32[3]{0:T(128)S(1)} %pad_add_fusion.refs_0_, bf16[640,1024]{1,0:T(8,128)(2,1)} %collective-permute-done.refs_1_, bf16[640,1024]{1,0:T(8,128)(2,1)} %collective-permute-done.1.refs_2_, bf16[640,1024]{1,0:T(8,128)(2,1)} %collective-permute-done.2.refs_3_, bf16[8192,1024]{1,0:T(8,128)(2,1)} %refs_4_.3, ...), custom_call_target="tpu_custom_call" | custom-call | flops 4026531840 | bytes 6291456 | tf_op jit(solution)/shard_map/pallas_call | solution.py:91
  118.9 1.5 copy-done.1
  120.4 13.2 %collective-permute-done.3.refs_0_.refs_1_ = bf16[640,1024]{1,0:T(8,128)(2,1)} collective-permute-done((bf16[640,1024]{1,0:T(8,128)(2,1)}, bf16[640,1024]{1,0:T(8,128)(2,1)}, u32[]{:S(2)}, u32[]{:S(2)}) %collective-permute-start.3) | collective-permute-done | bytes 1310752 | tf_op jit(solution)/shard_map/ppermute | solution.py:13
  133.5 0.3 collective-permute-done.5.refs_1_.refs_3_
  133.8 0.0 collective-permute-done.4.refs_2_
  133.8 40.8 %shard_map.117 = (bf16[224,1024]{1,0:T(8,128)(2,1)}, bf16[224,1024]{1,0:T(8,128)(2,1)}, bf16[192,1024]{1,0:T(8,128)(2,1)}) custom-call(bf16[640,1024]{1,0:T(8,128)(2,1)} %collective-permute-done.3.refs_0_.refs_1_, bf16[640,1024]{1,0:T(8,128)(2,1)} %collective-permute-done.5.refs_1_.refs_3_, bf16[640,1024]{1,0:T(8,128)(2,1)} %collective-permute-done.4.refs_2_), custom_call_target="tpu_custom_call" | custom-call | bytes 3145728 | tf_op jit(solution)/shard_map/pallas_call | solution.py:122
  174.7 2.3 %collective-permute-start.8 = (bf16[192,1024]{1,0:T(8,128)(2,1)}, bf16[192,1024]{1,0:T(8,128)(2,1)S(1)}, u32[]{:S(2)}, u32[]{:S(2)}) collective-permute-start(bf16[192,1024]{1,0:T(8,128)(2,1)} %get-tuple-element.61), channel_id=1, source_target_pairs={{0,1},{1,0},{2,3},{3,2},{4,5},{5,4},{6,7},{7,6},{8,9},{9,8},{10,11... | collective-permute-start | bytes 1179656 | tf_op jit(solution)/shard_map/ppermute | solution.py:21
  177.0 0.0 collective-permute-start.6
  177.0 3.7 %collective-permute-start.7 = (bf16[224,1024]{1,0:T(8,128)(2,1)}, bf16[224,1024]{1,0:T(8,128)(2,1)S(1)}, u32[]{:S(2)}, u32[]{:S(2)}) collective-permute-start(bf16[224,1024]{1,0:T(8,128)(2,1)} %get-tuple-element.60), channel_id=1, source_target_pairs={{0,6},{1,7},{2,0},{3,1},{4,2},{5,3},{6,4},{7,5},{8,14},{9,15},{10,... | collective-permute-start | bytes 1376264 | tf_op jit(solution)/shard_map/ppermute | solution.py:17
  180.7 0.1 pad_add_fusion.1.refs_0_
  180.7 8.6 %shard_map.118.refs_4_ = f32[640,1024]{1,0:T(8,128)S(1)} custom-call(s32[3]{0:T(128)S(1)} %pad_add_fusion.1.refs_0_, bf16[640,1024]{1,0:T(8,128)(2,1)} %collective-permute-done.3.refs_0_.refs_1_, bf16[640,1024]{1,0:T(8,128)(2,1)} %collective-permute-done.4.refs_2_, bf16[640,1024]{1,0:T(8,128)(2,1)} %collective-permute-done.5.refs_1_.refs_3_, ...), custom_call_target="tpu_custom_call" | custom-call | flops 4026531840 | bytes 6291456 | tf_op jit(solution)/shard_map/pallas_call | solution.py:91
  189.4 0.0 collective-permute-done.8.refs_2_
  189.4 0.0 collective-permute-done.6.refs_0_
  189.4 0.0 collective-permute-done.7.refs_1_
  189.4 2.5 %shard_map.119 = (bf16[512,1024]{1,0:T(8,128)(2,1)}, bf16[128,1024]{1,0:T(8,128)(2,1)S(1)}) custom-call(bf16[224,1024]{1,0:T(8,128)(2,1)S(1)} %collective-permute-done.6.refs_0_, bf16[224,1024]{1,0:T(8,128)(2,1)S(1)} %collective-permute-done.7.refs_1_, bf16[192,1024]{1,0:T(8,128)(2,1)S(1)} %collective-permute-done.8.refs_2_, ...), custom_call_target="tpu_custom_call" | custom-call | flops 1342177280 | bytes 2097152 | tf_op jit(solution)/shard_map/pallas_call | solution.py:83
  191.9 0.8 reshape.105
  (19 shorter events, 0.1 us)
Async XLA Ops:
  0.6 47.3 %copy-start = (bf16[32,4,4,256]{3,2,1,0:T(4,128)(2,1)S(1)}, bf16[32,4,4,256]{3,2,1,0:T(4,128)(2,1)}, u32[]{:S(2)}) copy-start(bf16[32,4,4,256]{3,2,1,0:T(4,128)(2,1)} %param.16) | copy-start | bytes 786436
  0.6 5.4 %copy-start.9 = (bf16[512,4,256]{2,1,0:T(4,128)(2,1)S(1)}, bf16[512,4,256]{2,1,0:T(4,128)(2,1)}, u32[]{:S(2)}) copy-start(bf16[512,4,256]{2,1,0:T(4,128)(2,1)} %param.12) | copy-start | bytes 3145732
  8.1 5.8 %copy-start.6 = (bf16[512,4,256]{2,1,0:T(4,128)(2,1)S(1)}, bf16[512,4,256]{2,1,0:T(4,128)(2,1)}, u32[]{:S(2)}) copy-start(bf16[512,4,256]{2,1,0:T(4,128)(2,1)} %param.10) | copy-start | bytes 3145732
  8.1 6.8 %copy-start.7 = (bf16[512,4,256]{2,1,0:T(4,128)(2,1)S(1)}, bf16[512,4,256]{2,1,0:T(4,128)(2,1)}, u32[]{:S(2)}) copy-start(bf16[512,4,256]{2,1,0:T(4,128)(2,1)} %param.11) | copy-start | bytes 3145732
  8.1 29.5 %all-to-all-start = ((bf16[16,208,256]{2,1,0:T(8,128)(2,1)}), bf16[16,208,256]{2,1,0:T(8,128)(2,1)}, u32[]{:S(2)}, u32[]{:S(2)}) async-start(bf16[16,208,256]{2,1,0:T(8,128)(2,1)} %pad_maximum_fusion), calls=%async_computation | async-start | bytes 3407872 | tf_op jit(solution)/shard_map/all_to_all | solution.py:310
  37.6 10.1 %copy-start.8 = (f32[4,4,32]{2,1,0:T(4,128)S(1)}, f32[4,4,32]{2,1,0:T(4,128)}, u32[]{:S(2)}) copy-start(f32[4,4,32]{2,1,0:T(4,128)} %param.18) | copy-start | bytes 6148
  42.0 0.9 copy-start.5
  42.9 18.1 %all-to-all-start.1 = ((bf16[16,96,256]{2,1,0:T(8,128)(2,1)}), bf16[16,96,256]{2,1,0:T(8,128)(2,1)}, u32[]{:S(2)}, u32[]{:S(2)}) async-start(bf16[16,96,256]{2,1,0:T(8,128)(2,1)} %copy-done.5), calls=%async_computation.1 | async-start | bytes 1572864 | tf_op jit(solution)/shard_map/all_to_all | solution.py:325
  61.0 1.0 copy-start.4
  65.0 32.2 %collective-permute-start.2 = (bf16[640,1024]{1,0:T(8,128)(2,1)}, bf16[640,1024]{1,0:T(8,128)(2,1)}, u32[]{:S(2)}, u32[]{:S(2)}) collective-permute-start(bf16[640,1024]{1,0:T(8,128)(2,1)} %shard_map.114.refs_1_), channel_id=1, source_target_pairs={{0,1},{1,0},{2,3},{3,2},{4,5},{5,4},{6,7},{7,6},{8,9},{9,8},{10,11... | collective-permute-start | bytes 3932168 | tf_op jit(solution)/shard_map/ppermute | solution.py:21
  67.9 31.9 %collective-permute-start.1 = (bf16[640,1024]{1,0:T(8,128)(2,1)}, bf16[640,1024]{1,0:T(8,128)(2,1)}, u32[]{:S(2)}, u32[]{:S(2)}) collective-permute-start(bf16[640,1024]{1,0:T(8,128)(2,1)} %shard_map.114.refs_1_), channel_id=1, source_target_pairs={{0,6},{1,7},{2,0},{3,1},{4,2},{5,3},{6,4},{7,5},{8,14},{9,15},{10,... | collective-permute-start | bytes 3932168 | tf_op jit(solution)/shard_map/ppermute | solution.py:17
  71.9 31.3 %collective-permute-start = (bf16[640,1024]{1,0:T(8,128)(2,1)}, bf16[640,1024]{1,0:T(8,128)(2,1)}, u32[]{:S(2)}, u32[]{:S(2)}) collective-permute-start(bf16[640,1024]{1,0:T(8,128)(2,1)} %shard_map.114.refs_1_), channel_id=1, source_target_pairs={{0,2},{1,3},{2,4},{3,5},{4,6},{5,7},{6,0},{7,1},{8,10},{9,11},{10,... | collective-permute-start | bytes 3932168 | tf_op jit(solution)/shard_map/ppermute | solution.py:13
  103.2 30.4 %collective-permute-start.3 = (bf16[640,1024]{1,0:T(8,128)(2,1)}, bf16[640,1024]{1,0:T(8,128)(2,1)}, u32[]{:S(2)}, u32[]{:S(2)}) collective-permute-start(bf16[640,1024]{1,0:T(8,128)(2,1)} %collective-permute-done.2.refs_3_), channel_id=1, source_target_pairs={{0,2},{1,3},{2,4},{3,5},{4,6},{5,7},{6,0},{7,1},{8,10},{9,11},{10,... | collective-permute-start | bytes 3932168 | tf_op jit(solution)/shard_map/ppermute | solution.py:13
  103.2 30.7 %collective-permute-start.5 = (bf16[640,1024]{1,0:T(8,128)(2,1)}, bf16[640,1024]{1,0:T(8,128)(2,1)}, u32[]{:S(2)}, u32[]{:S(2)}) collective-permute-start(bf16[640,1024]{1,0:T(8,128)(2,1)} %collective-permute-done.1.refs_2_), channel_id=1, source_target_pairs={{0,1},{1,0},{2,3},{3,2},{4,5},{5,4},{6,7},{7,6},{8,9},{9,8},{10,11... | collective-permute-start | bytes 3932168 | tf_op jit(solution)/shard_map/ppermute | solution.py:21
  104.0 29.9 %collective-permute-start.4 = (bf16[640,1024]{1,0:T(8,128)(2,1)}, bf16[640,1024]{1,0:T(8,128)(2,1)}, u32[]{:S(2)}, u32[]{:S(2)}) collective-permute-start(bf16[640,1024]{1,0:T(8,128)(2,1)} %collective-permute-done.1.refs_2_), channel_id=1, source_target_pairs={{0,6},{1,7},{2,0},{3,1},{4,2},{5,3},{6,4},{7,5},{8,14},{9,15},{10,... | collective-permute-start | bytes 3932168 | tf_op jit(solution)/shard_map/ppermute | solution.py:17
  118.9 1.5 copy-start.1
  133.5 47.2 %copy-start.2 = (f32[640,1024]{1,0:T(8,128)S(1)}, f32[640,1024]{1,0:T(8,128)}, u32[]{:S(2)}) copy-start(f32[640,1024]{1,0:T(8,128)} %copy-done.1) | copy-start | bytes 7864324
  174.7 14.7 %collective-permute-start.8 = (bf16[192,1024]{1,0:T(8,128)(2,1)}, bf16[192,1024]{1,0:T(8,128)(2,1)S(1)}, u32[]{:S(2)}, u32[]{:S(2)}) collective-permute-start(bf16[192,1024]{1,0:T(8,128)(2,1)} %get-tuple-element.61), channel_id=1, source_target_pairs={{0,1},{1,0},{2,3},{3,2},{4,5},{5,4},{6,7},{7,6},{8,9},{9,8},{10,11... | collective-permute-start | bytes 1179656 | tf_op jit(solution)/shard_map/ppermute | solution.py:21
  177.0 12.4 %collective-permute-start.6 = (bf16[224,1024]{1,0:T(8,128)(2,1)}, bf16[224,1024]{1,0:T(8,128)(2,1)S(1)}, u32[]{:S(2)}, u32[]{:S(2)}) collective-permute-start(bf16[224,1024]{1,0:T(8,128)(2,1)} %get-tuple-element.59), channel_id=1, source_target_pairs={{0,2},{1,3},{2,4},{3,5},{4,6},{5,7},{6,0},{7,1},{8,10},{9,11},{10,... | collective-permute-start | bytes 1376264 | tf_op jit(solution)/shard_map/ppermute | solution.py:13
  177.0 12.4 %collective-permute-start.7 = (bf16[224,1024]{1,0:T(8,128)(2,1)}, bf16[224,1024]{1,0:T(8,128)(2,1)S(1)}, u32[]{:S(2)}, u32[]{:S(2)}) collective-permute-start(bf16[224,1024]{1,0:T(8,128)(2,1)} %get-tuple-element.60), channel_id=1, source_target_pairs={{0,6},{1,7},{2,0},{3,1},{4,2},{5,3},{6,4},{7,5},{8,14},{9,15},{10,... | collective-permute-start | bytes 1376264 | tf_op jit(solution)/shard_map/ppermute | solution.py:17
  180.7 8.7 %copy-start.3 = (bf16[1024,1024]{1,0:T(8,128)(2,1)S(1)}, bf16[1024,1024]{1,0:T(8,128)(2,1)}, u32[]{:S(2)}) copy-start(bf16[1024,1024]{1,0:T(8,128)(2,1)} %constant_dynamic-slice_fusion.refs_3_) | copy-start | bytes 6291460

commit v5 on v4

--- a/solution.py
+++ b/solution.py
@@ -122,7 +122,7 @@
     return pl.pallas_call(
         body,
         in_specs=[pl.BlockSpec(memory_space=pl.ANY)] * len(pieces),
-        out_specs=[pl.BlockSpec(memory_space=pl.ANY)] * len(pieces),
+        out_specs=[WHOLE] * len(pieces),
         out_shape=[jax.ShapeDtypeStruct((n, a.shape[1]), a.dtype) for a, _, n in pieces],
         scratch_shapes=[pltpu.SemaphoreType.DMA((len(pieces),))],
         cost_estimate=pl.CostEstimate(flops=0, bytes_accessed=3 << 20, transcendentals=0),
@@ -339,7 +339,6 @@
     own = jnp.einsum("rhtu,ruhe->rthe", own * step_gains, v_own.astype(F32))
     own = own.reshape(slots, heads * dim)
     kept = jnp.exp(step_logs).reshape(slots, heads)
-    got, own, kept = lax.optimization_barrier((got, own, kept))
 
     block = retain(queries, within, cum_late, got, slice_rows, own, kept)
     prompt_out, step_out = gathered_projection(block, tokens, w_out)

time: 193 us -> 155 us (0.80)
  Pallas kernels: 72.3 us -> 34 us
    pallas_call x1, Pallas kernels: 40.8 us -> 2.49 us  [cut(): pl.pallas_call(body, in_specs=[pl.BlockSpec(memory_space=pl.ANY)] * len(p...]
  transfers between devices with their start and end apart: 11 -> 11, of which waited for: 7 -> 7; matrix products, arithmetic and copies ran while one was open for 8% -> 10% of each run, Pallas kernels for 11% -> 14%
where the time goes in v5:
time: 155 us; the launch traced here: 154 us
  waiting for transfers between devices  64.8 us (42%)
  Pallas kernels  34 us (22%)
  starting transfers between devices  26.7 us (17%)
  local copies, waits for them, and re-layouts  13.4 us (9%)
  matrix products  8.59 us (6%)
  other arithmetic  5.76 us (4%)
    all_to_all x2, waiting for transfers between devices, shards(): got = lax.all_to_all(sent, 'ctx', 0, 0)  24.6 us
    pallas_call x3, Pallas kernels, project(): pl.pallas_call(body, in_specs=[pl.BlockSpec(memory_space=pltpu.SMEM)] + [...  21.6 us
    ppermute x3, waiting for transfers between devices, across(): return lax.ppermute(a, 'head', [(h, h ^ 1) for h in range(8)])  21.2 us
    ppermute x3, waiting for transfers between devices, up(): return lax.ppermute(a, 'head', [(h, (h + 2) % 8) for h in range(8)])  16.6 us
    ppermute x3, starting transfers between devices, down(): return lax.ppermute(a, 'head', [(h, (h - 2) % 8) for h in range(8)])  10.9 us
    all_to_all x2, starting transfers between devices, shards(): got = lax.all_to_all(sent, 'ctx', 0, 0)  10 us
    ppermute x3, starting transfers between devices, across(): return lax.ppermute(a, 'head', [(h, h ^ 1) for h in range(8)])  5.76 us
    dot_general x1, matrix products, shards(): jnp.einsum('hnm,mhe->nhe', weights, v_late, preferred_element_type=F32)  4.75 us
  transfers between devices with their start and end apart: 11, of which 7 were waited for; matrix products, arithmetic and copies ran while one was open for 10% of the time, Pallas kernels for 14%

profile of v5, /device:TPU:0, one launch (start us, length us, event | category | flops | bytes accessed | tf_op | source)
XLA Modules:
  0.0 154.2 jit_solution(14476178817323152917)
XLA Ops:
  0.6 0.0 copy-start
  0.6 0.0 copy-start.9
  0.7 0.8 convert_bitcast_fusion
  1.4 0.1 broadcast_in_dim.33
  1.5 0.1 convert_element_type.50
  1.6 1.0 fusion.8
  2.6 0.2 slice_reduce_fusion
  2.8 0.1 subtract_exponential_fusion
  2.9 0.2 copy.25
  3.1 1.0 copy.30
  4.0 0.1 pad_maximum_fusion.2
  4.1 0.1 broadcast_in_dim.32
  4.3 1.8 %multiply_convert_fusion.1 = bf16[512,4,256]{2,1,0:T(4,128)(2,1)S(1)} fusion(bf16[512,4,256]{2,1,0:T(4,128)(2,1)} %param.11, f32[512,4]{1,0:T(8,128)S(1)} %copy.25), kind=kLoop, calls=%fused_computation.1 | loop fusion | flops 1572864 | bytes 2105344 | tf_op jit(solution)/shard_map/convert_element_type | solution.py:287
  6.1 0.6 convolution_convert_fusion
  6.6 0.1 broadcast_in_dim.36
  6.7 1.3 pad_maximum_fusion
  8.1 5.8 %all-to-all-start = ((bf16[16,208,256]{2,1,0:T(8,128)(2,1)}), bf16[16,208,256]{2,1,0:T(8,128)(2,1)}, u32[]{:S(2)}, u32[]{:S(2)}) async-start(bf16[16,208,256]{2,1,0:T(8,128)(2,1)} %pad_maximum_fusion), calls=%async_computation | async-start | bytes 3407872 | tf_op jit(solution)/shard_map/all_to_all | solution.py:310
  13.9 0.0 copy-done.6
  13.9 0.2 copy.45
  14.1 0.8 iota_compare_fusion
  14.9 4.8 %fusion = f32[4,256,512]{2,1,0:T(8,128)} fusion(f32[4,512]{1,0:T(4,128)S(1)} %bitcast.37, pred[512,512]{1,0:T(8,128)(4,1)} %iota_compare_fusion, bf16[512,4,256]{2,1,0:T(4,128)(2,1)S(1)} %copy-done.7, bf16[512,4,256]{2,1,0:T(4,128)(2,1)S(1)} %copy-done.6, bf16[512,4,256]{2,1,0:T(4,128)(2,1)} %param.12), kind=kOutput, calls=%fused_computation.3 | convolution fusion | flops 1078984704 | bytes 5513216 | tf_op jit(solution)/shard_map/hnm,mhe->nhe/dot_general | solution.py:319
  19.6 1.9 %copy.43.in_ref = f32[512,1024]{1,0:T(8,128)S(1)} copy(f32[512,1024]{0,1:T(8,128)} %bitcast.40) | data formatting | bytes 4194304 | tf_op jit(solution)/shard_map/reshape | solution.py:320
  21.6 16.0 %all-to-all-done.got_ref = bf16[16,208,256]{2,1,0:T(8,128)(2,1)} async-done(((bf16[16,208,256]{2,1,0:T(8,128)(2,1)}), bf16[16,208,256]{2,1,0:T(8,128)(2,1)}, u32[]{:S(2)}, u32[]{:S(2)}) %all-to-all-start) | async-done | bytes 1703968 | tf_op jit(solution)/shard_map/all_to_all | solution.py:310
  37.6 4.4 %shard_map.113 = bf16[16,96,256]{2,1,0:T(8,128)(2,1)S(1)} custom-call(bf16[16,208,256]{2,1,0:T(8,128)(2,1)} %all-to-all-done.got_ref), custom_call_target="tpu_custom_call" | custom-call | flops 1073741824 | bytes 6291456 | tf_op jit(solution)/shard_map/pallas_call | solution.py:173
  42.0 0.0 copy-start.5
  42.0 0.9 copy-done.5
  42.9 4.3 %all-to-all-start.1 = ((bf16[16,96,256]{2,1,0:T(8,128)(2,1)}), bf16[16,96,256]{2,1,0:T(8,128)(2,1)}, u32[]{:S(2)}, u32[]{:S(2)}) async-start(bf16[16,96,256]{2,1,0:T(8,128)(2,1)} %copy-done.5), calls=%async_computation.1 | async-start | bytes 1572864 | tf_op jit(solution)/shard_map/all_to_all | solution.py:325
  47.2 0.5 iota_compare_fusion.4
  47.7 0.1 copy.37
  47.9 0.1 copy.33
  48.0 2.3 %convolution_bitcast_fusion = f32[32,4,4,256]{3,1,2,0:T(4,128)} fusion(bf16[32,4,4,256]{3,2,1,0:T(4,128)(2,1)S(1)} %copy-done, bf16[32,4,4,256]{3,2,1,0:T(4,128)(2,1)} %param.15, bf16[32,4,4,256]{3,2,1,0:T(4,128)(2,1)} %param.17, f32[32,4,4]{2,1,0:T(4,128)S(1)} %copy.33, pred[4,4]{1,0:T(4,128)(4,1)} %iota_compare_fusion.4), kind=kOutput, calls=%fused_computation.5 | convolution fusion | flops 2105344 | bytes 1312784 | tf_op jit(solution)/shard_map/rhtu,ruhe->rthe/dot_general | solution.py:339
  50.3 1.2 copy.36
  51.5 0.9 copy.46
  52.4 8.6 %all-to-all-done.1.got_ref = bf16[16,96,256]{2,1,0:T(8,128)(2,1)} async-done(((bf16[16,96,256]{2,1,0:T(8,128)(2,1)}), bf16[16,96,256]{2,1,0:T(8,128)(2,1)}, u32[]{:S(2)}, u32[]{:S(2)}) %all-to-all-start.1) | async-done | bytes 786464 | tf_op jit(solution)/shard_map/all_to_all | solution.py:325
  61.0 1.0 copy-done.4
  62.0 3.0 %shard_map.114.refs_1_ = bf16[640,1024]{1,0:T(8,128)(2,1)} custom-call(bf16[512,1024]{1,0:T(8,128)(2,1)S(1)} %bitcast.33, f32[512,1024]{1,0:T(8,128)S(1)} %copy.43.in_ref, f32[4,512]{1,0:T(4,128)S(1)} %bitcast.38, bf16[16,96,256]{2,1,0:T(8,128)(2,1)} %all-to-all-done.1.got_ref, f32[128,1024]{1,0:T(8,128)S(1)} %bitcast.34, f32[128,4]{1,0:T(8,128)S(1)} %bitcast.35), custom_call_target="tpu_custom_call" | custom-call | flops 268435456 | bytes 6291456 | tf_op jit(solution)/shard_map/pallas_call | solution.py:218
  65.0 2.8 %collective-permute-start.2 = (bf16[640,1024]{1,0:T(8,128)(2,1)}, bf16[640,1024]{1,0:T(8,128)(2,1)}, u32[]{:S(2)}, u32[]{:S(2)}) collective-permute-start(bf16[640,1024]{1,0:T(8,128)(2,1)} %shard_map.114.refs_1_), channel_id=1, source_target_pairs={{0,1},{1,0},{2,3},{3,2},{4,5},{5,4},{6,7},{7,6},{8,9},{9,8},{10,11... | collective-permute-start | bytes 3932168 | tf_op jit(solution)/shard_map/ppermute | solution.py:21
  67.9 4.0 %collective-permute-start.1 = (bf16[640,1024]{1,0:T(8,128)(2,1)}, bf16[640,1024]{1,0:T(8,128)(2,1)}, u32[]{:S(2)}, u32[]{:S(2)}) collective-permute-start(bf16[640,1024]{1,0:T(8,128)(2,1)} %shard_map.114.refs_1_), channel_id=1, source_target_pairs={{0,6},{1,7},{2,0},{3,1},{4,2},{5,3},{6,4},{7,5},{8,14},{9,15},{10,... | collective-permute-start | bytes 3932168 | tf_op jit(solution)/shard_map/ppermute | solution.py:17
  71.9 0.0 collective-permute-start
  71.9 4.5 %shard_map.115.refs_5_ = f32[640,1024]{1,0:T(8,128)S(1)} custom-call(s32[1]{0:T(128)} %bitcast.14.refs_0_, bf16[640,1024]{1,0:T(8,128)(2,1)} %shard_map.114.refs_1_, bf16[8192,1024]{1,0:T(8,128)(2,1)} %refs_4_.3), custom_call_target="tpu_custom_call" | custom-call | flops 1342177280 | bytes 2097152 | tf_op jit(solution)/shard_map/pallas_call | solution.py:91
  76.4 20.9 %collective-permute-done.2.refs_3_ = bf16[640,1024]{1,0:T(8,128)(2,1)} collective-permute-done((bf16[640,1024]{1,0:T(8,128)(2,1)}, bf16[640,1024]{1,0:T(8,128)(2,1)}, u32[]{:S(2)}, u32[]{:S(2)}) %collective-permute-start.2) | collective-permute-done | bytes 1310752 | tf_op jit(solution)/shard_map/ppermute | solution.py:21
  97.3 2.5 %collective-permute-done.1.refs_2_ = bf16[640,1024]{1,0:T(8,128)(2,1)} collective-permute-done((bf16[640,1024]{1,0:T(8,128)(2,1)}, bf16[640,1024]{1,0:T(8,128)(2,1)}, u32[]{:S(2)}, u32[]{:S(2)}) %collective-permute-start.1) | collective-permute-done | bytes 1310752 | tf_op jit(solution)/shard_map/ppermute | solution.py:17
  99.8 3.4 %collective-permute-done.refs_1_ = bf16[640,1024]{1,0:T(8,128)(2,1)} collective-permute-done((bf16[640,1024]{1,0:T(8,128)(2,1)}, bf16[640,1024]{1,0:T(8,128)(2,1)}, u32[]{:S(2)}, u32[]{:S(2)}) %collective-permute-start) | collective-permute-done | bytes 1310752 | tf_op jit(solution)/shard_map/ppermute | solution.py:13
  103.2 0.0 collective-permute-start.3
  103.2 0.8 collective-permute-start.5
  104.0 3.2 %collective-permute-start.4 = (bf16[640,1024]{1,0:T(8,128)(2,1)}, bf16[640,1024]{1,0:T(8,128)(2,1)}, u32[]{:S(2)}, u32[]{:S(2)}) collective-permute-start(bf16[640,1024]{1,0:T(8,128)(2,1)} %collective-permute-done.1.refs_2_), channel_id=1, source_target_pairs={{0,6},{1,7},{2,0},{3,1},{4,2},{5,3},{6,4},{7,5},{8,14},{9,15},{10,... | collective-permute-start | bytes 3932168 | tf_op jit(solution)/shard_map/ppermute | solution.py:17
  107.2 0.1 pad_add_fusion.refs_0_
  107.3 3.1 %constant_dynamic-slice_fusion.refs_3_ = bf16[1024,1024]{1,0:T(8,128)(2,1)} fusion(bf16[8192,1024]{1,0:T(8,128)(2,1)} %refs_4_.3, s32[]{:T(128)S(6)} %select_n.52), kind=kLoop, calls=%fused_computation.50 | loop fusion | bytes 4194308 | tf_op jit(solution)/shard_map/dynamic_slice | solution.py:245
  110.4 8.5 %shard_map.116.refs_5_ = f32[640,1024]{1,0:T(8,128)S(1)} custom-call(s32[3]{0:T(128)S(1)} %pad_add_fusion.refs_0_, bf16[640,1024]{1,0:T(8,128)(2,1)} %collective-permute-done.refs_1_, bf16[640,1024]{1,0:T(8,128)(2,1)} %collective-permute-done.1.refs_2_, bf16[640,1024]{1,0:T(8,128)(2,1)} %collective-permute-done.2.refs_3_, bf16[8192,1024]{1,0:T(8,128)(2,1)} %refs_4_.3, ...), custom_call_target="tpu_custom_call" | custom-call | flops 4026531840 | bytes 6291456 | tf_op jit(solution)/shard_map/pallas_call | solution.py:91
  118.9 1.5 copy-done.1
  120.4 13.2 %collective-permute-done.3.refs_0_.refs_1_ = bf16[640,1024]{1,0:T(8,128)(2,1)} collective-permute-done((bf16[640,1024]{1,0:T(8,128)(2,1)}, bf16[640,1024]{1,0:T(8,128)(2,1)}, u32[]{:S(2)}, u32[]{:S(2)}) %collective-permute-start.3) | collective-permute-done | bytes 1310752 | tf_op jit(solution)/shard_map/ppermute | solution.py:13
  133.5 0.3 collective-permute-done.5.refs_1_.refs_3_
  133.8 0.0 collective-permute-done.4.refs_2_
  133.8 2.5 %shard_map.117 = (bf16[224,1024]{1,0:T(8,128)(2,1)}, bf16[224,1024]{1,0:T(8,128)(2,1)}, bf16[192,1024]{1,0:T(8,128)(2,1)}) custom-call(bf16[640,1024]{1,0:T(8,128)(2,1)} %collective-permute-done.3.refs_0_.refs_1_, bf16[640,1024]{1,0:T(8,128)(2,1)} %collective-permute-done.5.refs_1_.refs_3_, bf16[640,1024]{1,0:T(8,128)(2,1)} %collective-permute-done.4.refs_2_), custom_call_target="tpu_custom_call" | custom-call | bytes 3145728 | tf_op jit(solution)/shard_map/pallas_call | solution.py:122
  136.3 2.1 %collective-permute-start.8 = (bf16[192,1024]{1,0:T(8,128)(2,1)}, bf16[192,1024]{1,0:T(8,128)(2,1)S(1)}, u32[]{:S(2)}, u32[]{:S(2)}) collective-permute-start(bf16[192,1024]{1,0:T(8,128)(2,1)} %get-tuple-element.55), channel_id=1, source_target_pairs={{0,1},{1,0},{2,3},{3,2},{4,5},{5,4},{6,7},{7,6},{8,9},{9,8},{10,11... | collective-permute-start | bytes 1179656 | tf_op jit(solution)/shard_map/ppermute | solution.py:21
  138.5 0.0 collective-permute-start.6
  138.5 3.7 %collective-permute-start.7 = (bf16[224,1024]{1,0:T(8,128)(2,1)}, bf16[224,1024]{1,0:T(8,128)(2,1)S(1)}, u32[]{:S(2)}, u32[]{:S(2)}) collective-permute-start(bf16[224,1024]{1,0:T(8,128)(2,1)} %get-tuple-element.54), channel_id=1, source_target_pairs={{0,6},{1,7},{2,0},{3,1},{4,2},{5,3},{6,4},{7,5},{8,14},{9,15},{10,... | collective-permute-start | bytes 1376264 | tf_op jit(solution)/shard_map/ppermute | solution.py:17
  142.2 0.1 pad_add_fusion.1.refs_0_
  142.3 8.6 %shard_map.118.refs_4_ = f32[640,1024]{1,0:T(8,128)S(1)} custom-call(s32[3]{0:T(128)S(1)} %pad_add_fusion.1.refs_0_, bf16[640,1024]{1,0:T(8,128)(2,1)} %collective-permute-done.3.refs_0_.refs_1_, bf16[640,1024]{1,0:T(8,128)(2,1)} %collective-permute-done.4.refs_2_, bf16[640,1024]{1,0:T(8,128)(2,1)} %collective-permute-done.5.refs_1_.refs_3_, ...), custom_call_target="tpu_custom_call" | custom-call | flops 4026531840 | bytes 6291456 | tf_op jit(solution)/shard_map/pallas_call | solution.py:91
  150.9 0.0 collective-permute-done.8.refs_2_
  150.9 0.0 collective-permute-done.6.refs_0_
  150.9 0.0 collective-permute-done.7.refs_1_
  150.9 2.5 %shard_map.119 = (bf16[512,1024]{1,0:T(8,128)(2,1)}, bf16[128,1024]{1,0:T(8,128)(2,1)S(1)}) custom-call(bf16[224,1024]{1,0:T(8,128)(2,1)S(1)} %collective-permute-done.6.refs_0_, bf16[224,1024]{1,0:T(8,128)(2,1)S(1)} %collective-permute-done.7.refs_1_, bf16[192,1024]{1,0:T(8,128)(2,1)S(1)} %collective-permute-done.8.refs_2_, ...), custom_call_target="tpu_custom_call" | custom-call | flops 1342177280 | bytes 2097152 | tf_op jit(solution)/shard_map/pallas_call | solution.py:83
  153.4 0.8 reshape.105
  (19 shorter events, 0.1 us)
Async XLA Ops:
  0.6 47.3 %copy-start = (bf16[32,4,4,256]{3,2,1,0:T(4,128)(2,1)S(1)}, bf16[32,4,4,256]{3,2,1,0:T(4,128)(2,1)}, u32[]{:S(2)}) copy-start(bf16[32,4,4,256]{3,2,1,0:T(4,128)(2,1)} %param.16) | copy-start | bytes 786436
  0.6 5.4 %copy-start.9 = (bf16[512,4,256]{2,1,0:T(4,128)(2,1)S(1)}, bf16[512,4,256]{2,1,0:T(4,128)(2,1)}, u32[]{:S(2)}) copy-start(bf16[512,4,256]{2,1,0:T(4,128)(2,1)} %param.12) | copy-start | bytes 3145732
  8.1 5.8 %copy-start.6 = (bf16[512,4,256]{2,1,0:T(4,128)(2,1)S(1)}, bf16[512,4,256]{2,1,0:T(4,128)(2,1)}, u32[]{:S(2)}) copy-start(bf16[512,4,256]{2,1,0:T(4,128)(2,1)} %param.10) | copy-start | bytes 3145732
  8.1 6.8 %copy-start.7 = (bf16[512,4,256]{2,1,0:T(4,128)(2,1)S(1)}, bf16[512,4,256]{2,1,0:T(4,128)(2,1)}, u32[]{:S(2)}) copy-start(bf16[512,4,256]{2,1,0:T(4,128)(2,1)} %param.11) | copy-start | bytes 3145732
  8.1 29.5 %all-to-all-start = ((bf16[16,208,256]{2,1,0:T(8,128)(2,1)}), bf16[16,208,256]{2,1,0:T(8,128)(2,1)}, u32[]{:S(2)}, u32[]{:S(2)}) async-start(bf16[16,208,256]{2,1,0:T(8,128)(2,1)} %pad_maximum_fusion), calls=%async_computation | async-start | bytes 3407872 | tf_op jit(solution)/shard_map/all_to_all | solution.py:310
  37.6 10.1 %copy-start.8 = (f32[4,4,32]{2,1,0:T(4,128)S(1)}, f32[4,4,32]{2,1,0:T(4,128)}, u32[]{:S(2)}) copy-start(f32[4,4,32]{2,1,0:T(4,128)} %param.18) | copy-start | bytes 6148
  42.0 0.9 copy-start.5
  42.9 18.1 %all-to-all-start.1 = ((bf16[16,96,256]{2,1,0:T(8,128)(2,1)}), bf16[16,96,256]{2,1,0:T(8,128)(2,1)}, u32[]{:S(2)}, u32[]{:S(2)}) async-start(bf16[16,96,256]{2,1,0:T(8,128)(2,1)} %copy-done.5), calls=%async_computation.1 | async-start | bytes 1572864 | tf_op jit(solution)/shard_map/all_to_all | solution.py:325
  61.0 1.0 copy-start.4
  65.0 32.2 %collective-permute-start.2 = (bf16[640,1024]{1,0:T(8,128)(2,1)}, bf16[640,1024]{1,0:T(8,128)(2,1)}, u32[]{:S(2)}, u32[]{:S(2)}) collective-permute-start(bf16[640,1024]{1,0:T(8,128)(2,1)} %shard_map.114.refs_1_), channel_id=1, source_target_pairs={{0,1},{1,0},{2,3},{3,2},{4,5},{5,4},{6,7},{7,6},{8,9},{9,8},{10,11... | collective-permute-start | bytes 3932168 | tf_op jit(solution)/shard_map/ppermute | solution.py:21
  67.9 31.9 %collective-permute-start.1 = (bf16[640,1024]{1,0:T(8,128)(2,1)}, bf16[640,1024]{1,0:T(8,128)(2,1)}, u32[]{:S(2)}, u32[]{:S(2)}) collective-permute-start(bf16[640,1024]{1,0:T(8,128)(2,1)} %shard_map.114.refs_1_), channel_id=1, source_target_pairs={{0,6},{1,7},{2,0},{3,1},{4,2},{5,3},{6,4},{7,5},{8,14},{9,15},{10,... | collective-permute-start | bytes 3932168 | tf_op jit(solution)/shard_map/ppermute | solution.py:17
  71.9 31.3 %collective-permute-start = (bf16[640,1024]{1,0:T(8,128)(2,1)}, bf16[640,1024]{1,0:T(8,128)(2,1)}, u32[]{:S(2)}, u32[]{:S(2)}) collective-permute-start(bf16[640,1024]{1,0:T(8,128)(2,1)} %shard_map.114.refs_1_), channel_id=1, source_target_pairs={{0,2},{1,3},{2,4},{3,5},{4,6},{5,7},{6,0},{7,1},{8,10},{9,11},{10,... | collective-permute-start | bytes 3932168 | tf_op jit(solution)/shard_map/ppermute | solution.py:13
  103.2 30.4 %collective-permute-start.3 = (bf16[640,1024]{1,0:T(8,128)(2,1)}, bf16[640,1024]{1,0:T(8,128)(2,1)}, u32[]{:S(2)}, u32[]{:S(2)}) collective-permute-start(bf16[640,1024]{1,0:T(8,128)(2,1)} %collective-permute-done.2.refs_3_), channel_id=1, source_target_pairs={{0,2},{1,3},{2,4},{3,5},{4,6},{5,7},{6,0},{7,1},{8,10},{9,11},{10,... | collective-permute-start | bytes 3932168 | tf_op jit(solution)/shard_map/ppermute | solution.py:13
  103.2 30.7 %collective-permute-start.5 = (bf16[640,1024]{1,0:T(8,128)(2,1)}, bf16[640,1024]{1,0:T(8,128)(2,1)}, u32[]{:S(2)}, u32[]{:S(2)}) collective-permute-start(bf16[640,1024]{1,0:T(8,128)(2,1)} %collective-permute-done.1.refs_2_), channel_id=1, source_target_pairs={{0,1},{1,0},{2,3},{3,2},{4,5},{5,4},{6,7},{7,6},{8,9},{9,8},{10,11... | collective-permute-start | bytes 3932168 | tf_op jit(solution)/shard_map/ppermute | solution.py:21
  104.0 29.9 %collective-permute-start.4 = (bf16[640,1024]{1,0:T(8,128)(2,1)}, bf16[640,1024]{1,0:T(8,128)(2,1)}, u32[]{:S(2)}, u32[]{:S(2)}) collective-permute-start(bf16[640,1024]{1,0:T(8,128)(2,1)} %collective-permute-done.1.refs_2_), channel_id=1, source_target_pairs={{0,6},{1,7},{2,0},{3,1},{4,2},{5,3},{6,4},{7,5},{8,14},{9,15},{10,... | collective-permute-start | bytes 3932168 | tf_op jit(solution)/shard_map/ppermute | solution.py:17
  118.9 1.5 copy-start.1
  133.5 8.7 %copy-start.2 = (f32[640,1024]{1,0:T(8,128)S(1)}, f32[640,1024]{1,0:T(8,128)}, u32[]{:S(2)}) copy-start(f32[640,1024]{1,0:T(8,128)} %copy-done.1) | copy-start | bytes 7864324
  136.3 14.6 %collective-permute-start.8 = (bf16[192,1024]{1,0:T(8,128)(2,1)}, bf16[192,1024]{1,0:T(8,128)(2,1)S(1)}, u32[]{:S(2)}, u32[]{:S(2)}) collective-permute-start(bf16[192,1024]{1,0:T(8,128)(2,1)} %get-tuple-element.55), channel_id=1, source_target_pairs={{0,1},{1,0},{2,3},{3,2},{4,5},{5,4},{6,7},{7,6},{8,9},{9,8},{10,11... | collective-permute-start | bytes 1179656 | tf_op jit(solution)/shard_map/ppermute | solution.py:21
  138.5 12.4 %collective-permute-start.6 = (bf16[224,1024]{1,0:T(8,128)(2,1)}, bf16[224,1024]{1,0:T(8,128)(2,1)S(1)}, u32[]{:S(2)}, u32[]{:S(2)}) collective-permute-start(bf16[224,1024]{1,0:T(8,128)(2,1)} %get-tuple-element.53), channel_id=1, source_target_pairs={{0,2},{1,3},{2,4},{3,5},{4,6},{5,7},{6,0},{7,1},{8,10},{9,11},{10,... | collective-permute-start | bytes 1376264 | tf_op jit(solution)/shard_map/ppermute | solution.py:13
  138.5 12.4 %collective-permute-start.7 = (bf16[224,1024]{1,0:T(8,128)(2,1)}, bf16[224,1024]{1,0:T(8,128)(2,1)S(1)}, u32[]{:S(2)}, u32[]{:S(2)}) collective-permute-start(bf16[224,1024]{1,0:T(8,128)(2,1)} %get-tuple-element.54), channel_id=1, source_target_pairs={{0,6},{1,7},{2,0},{3,1},{4,2},{5,3},{6,4},{7,5},{8,14},{9,15},{10,... | collective-permute-start | bytes 1376264 | tf_op jit(solution)/shard_map/ppermute | solution.py:17
  142.2 8.7 %copy-start.3 = (bf16[1024,1024]{1,0:T(8,128)(2,1)S(1)}, bf16[1024,1024]{1,0:T(8,128)(2,1)}, u32[]{:S(2)}) copy-start(bf16[1024,1024]{1,0:T(8,128)(2,1)} %constant_dynamic-slice_fusion.refs_3_) | copy-start | bytes 6291460

commit v6 on v5

--- a/solution.py
+++ b/solution.py
@@ -77,7 +77,7 @@
         out = [jax.ShapeDtypeStruct((r, columns), BF) for r in (split, rows - split)]
     flops = sum(2 * t[3] * width * columns for t in terms)
     cost = pl.CostEstimate(
-        flops=flops, bytes_accessed=max(n_slot, 1) * 2 * width * columns, transcendentals=0
+        flops=flops >> 10, bytes_accessed=1 << 10, transcendentals=0
     )
     if heads is None:
         return pl.pallas_call(
@@ -105,30 +105,6 @@
     )(jnp.stack(heads).astype(jnp.int32), *srcs, w, *old)
 
 
-def cut(pieces):
-    def body(*refs):
-        k = len(pieces)
-        copies = [
-            pltpu.make_async_copy(
-                refs[i].at[pl.ds(start, n), :], refs[k + i], refs[2 * k].at[i]
-            )
-            for i, (_, start, n) in enumerate(pieces)
-        ]
-        for copy in copies:
-            copy.start()
-        for copy in copies:
-            copy.wait()
-
-    return pl.pallas_call(
-        body,
-        in_specs=[pl.BlockSpec(memory_space=pl.ANY)] * len(pieces),
-        out_specs=[WHOLE] * len(pieces),
-        out_shape=[jax.ShapeDtypeStruct((n, a.shape[1]), a.dtype) for a, _, n in pieces],
-        scratch_shapes=[pltpu.SemaphoreType.DMA((len(pieces),))],
-        cost_estimate=pl.CostEstimate(flops=0, bytes_accessed=3 << 20, transcendentals=0),
-    )(*[a for a, _, _ in pieces])
-
-
 NT = (((1,), (1,)), ((), ()))
 
 
@@ -191,7 +167,10 @@
     slots, heads = kept.shape
     per_head = sections // heads
 
-    def body(q_ref, in_ref, l_ref, got_ref, own_ref, k_ref, o_ref, own_held, arrived):
+    n = tokens + slots
+    upper = n // 2
+
+    def body(q_ref, in_ref, l_ref, got_ref, own_ref, k_ref, o_ref, t_ref, b_ref, own_held, arrived):
         fetch = pltpu.make_async_copy(own_ref, own_held, arrived)
         fetch.start()
         gains = jnp.exp(l_ref[...])
@@ -212,14 +191,16 @@
             read = jnp.concatenate(parts, axis=0).T
             mixed = k_ref[:, h : h + 1] * read + own_held[:, cols]
             o_ref[tokens:, cols] = mixed.astype(BF)
+        t_ref[...] = o_ref[:upper, :]
+        b_ref[...] = o_ref[upper:, :]
 
     specs = [WHOLE] * 6
     specs[4] = pl.BlockSpec(memory_space=pl.ANY)
     return pl.pallas_call(
         body,
         in_specs=specs,
-        out_specs=WHOLE,
-        out_shape=jax.ShapeDtypeStruct((tokens + slots, width), BF),
+        out_specs=[WHOLE] * 3,
+        out_shape=[jax.ShapeDtypeStruct((r, width), BF) for r in (n, upper, n - upper)],
         scratch_shapes=[pltpu.VMEM(own.shape, F32), pltpu.SemaphoreType.DMA],
         compiler_params=pltpu.CompilerParams(vmem_limit_bytes=12 << 20),
         cost_estimate=pl.CostEstimate(
@@ -228,40 +209,47 @@
     )(queries, within, logs, got, own, kept)
 
 
-def gathered_projection(block, split, w):
+def gathered_projection(blocks, split, w):
     me = lax.axis_index("head")
     z, x = me // 2, me % 2
     here, far = lambda d: ((z + d) % 4) * 2 + x, lambda d: ((z + d) % 4) * 2 + 1 - x
-    n = block.shape[0]
-    third = -(-n // 48) * 16
-    whole = lambda s: (s, s, 0, n, 0)
-
-    a1, a2, a3 = up(block), down(block), across(block)
-    (total,) = project(n, [block], [whole(0)], [me], w)
-    a1, a2, a3, total = lax.optimization_barrier((a1, a2, a3, total))
-
-    b1, b2, b3 = up(a3), down(a2), across(a2)
+    block, top, bottom = blocks
+    n, h = block.shape[0], top.shape[0]
     width = block.shape[1]
+    whole = lambda slot, i: [(slot, i, 0, n, 0)]
+    halves = lambda slot, i: [(slot, i, 0, h, 0), (slot, i + 1, 0, n - h, h)]
+
+    down_top, down_bottom = down(top), down(bottom)
+    from_below, from_side = up(block), across(block)
+    (total,) = project(n, [block], whole(0, 0), [me], w)
+
+    down_top, total = lax.optimization_barrier((down_top, total))
+    side_below = up(after(from_side, down_bottom))
+    side_top, far_bottom = across(down_top), down(down_bottom)
+    side_bottom, far_top = across(after(down_bottom, from_below)), down(after(down_top, from_below))
+    (total,) = project(
+        total,
+        [from_below, down_top, down_bottom, from_side],
+        whole(0, 0) + halves(1, 1) + whole(2, 3),
+        [here(-1), here(1), far(0)],
+        w,
+    )
+
+    side_top, total = lax.optimization_barrier((side_top, total))
+    last_top = down(side_top)
+    last_bottom = across(far_bottom)
     w_last = lax.dynamic_slice_in_dim(after(w, total), far(2) * width, width, 0)
     (total,) = project(
-        total, [a1, a2, a3], [whole(s) for s in range(3)], [here(-1), here(1), far(0)], w
-    )
-    b1, b2, b3, total, w_last = lax.optimization_barrier((b1, b2, b3, total, w_last))
-
-    c1, c2, c3 = cut([(b1, 0, third), (b3, third, third), (b2, 2 * third, n - 2 * third)])
-    c1, c2, c3 = up(c1), down(c2), across(c3)
-    (total,) = project(
-        total, [b1, b2, b3], [whole(s) for s in range(3)], [far(-1), here(2), far(1)], w
-    )
-    c1, c2, c3, total = lax.optimization_barrier((c1, c2, c3, total))
-    return project(
         total,
-        [c1, c2, c3],
-        [(0, i, 0, c.shape[0], i * third) for i, c in enumerate((c1, c2, c3))],
-        None,
-        w_last,
-        split,
-    )
+        [side_below, far_top, far_bottom, side_top, side_bottom],
+        whole(0, 0) + halves(1, 1) + halves(2, 3),
+        [far(-1), here(2), far(1)],
+        w,
+    )
+    last_top, last_bottom, total, w_last = lax.optimization_barrier(
+        (last_top, last_bottom, total, w_last)
+    )
+    return project(total, [last_top, last_bottom], halves(0, 0), None, w_last, split)
 
 
 def shards(
@@ -340,8 +328,8 @@
     own = own.reshape(slots, heads * dim)
     kept = jnp.exp(step_logs).reshape(slots, heads)
 
-    block = retain(queries, within, cum_late, got, slice_rows, own, kept)
-    prompt_out, step_out = gathered_projection(block, tokens, w_out)
+    blocks = retain(queries, within, cum_late, got, slice_rows, own, kept)
+    prompt_out, step_out = gathered_projection(blocks, tokens, w_out)
     return prompt_out, step_out.reshape(rows, steps, w_out.shape[1])
 
 

time: 155 us -> 149 us (0.961)
  waiting for transfers between devices: 64.8 us -> 57.4 us
  starting transfers between devices: 26.7 us -> 32.7 us
  Pallas kernels: 34 us -> 31.1 us
    ppermute x3 -> x5, waiting for transfers between devices: 2.5 us -> 21 us  [down(): return lax.ppermute(a, 'head', [(h, (h - 2) % 8) for h in range(8)])]
    ppermute x3 -> x2, waiting for transfers between devices: 16.6 us -> 0.01 us  [up(): return lax.ppermute(a, 'head', [(h, (h + 2) % 8) for h in range(8)])]
    ppermute x3 -> x4, waiting for transfers between devices: 21.2 us -> 11.8 us  [across(): return lax.ppermute(a, 'head', [(h, h ^ 1) for h in range(8)])]
    ppermute x3 -> x2, starting transfers between devices: 0.01 us -> 3.83 us  [up(): return lax.ppermute(a, 'head', [(h, (h + 2) % 8) for h in range(8)])]
    pallas_call x2 -> x1, Pallas kernels: 5.52 us -> 3.39 us  [retain(): pl.pallas_call(body, in_specs=specs, out_specs=[WHOLE] * 3, out_shape=[ja...]
    unnamed x22 -> x20, local copies, waits for them, and re-layouts: 4.56 us -> 5.78 us
    ppermute x3 -> x4, starting transfers between devices: 5.76 us -> 6.93 us  [across(): return lax.ppermute(a, 'head', [(h, h ^ 1) for h in range(8)])]
    ppermute x3 -> x5, starting transfers between devices: 10.9 us -> 11.9 us  [down(): return lax.ppermute(a, 'head', [(h, (h - 2) % 8) for h in range(8)])]
  transfers between devices with their start and end apart: 11 -> 13, of which waited for: 7 -> 8; matrix products, arithmetic and copies ran while one was open for 10% -> 10% of each run, Pallas kernels for 14% -> 14%
where the time goes in v6:
time: 149 us
  waiting for transfers between devices  57.4 us (39%)
  starting transfers between devices  32.7 us (22%)
  Pallas kernels  31.1 us (21%)
  local copies, waits for them, and re-layouts  13.4 us (9%)
  matrix products  8.54 us (6%)
  other arithmetic  4.48 us (3%)
    all_to_all x2, waiting for transfers between devices, shards(): got = lax.all_to_all(sent, 'ctx', 0, 0)  24.6 us
    ppermute x5, waiting for transfers between devices, down(): return lax.ppermute(a, 'head', [(h, (h - 2) % 8) for h in range(8)])  21 us
    pallas_call x3, Pallas kernels, project(): pl.pallas_call(body, in_specs=[pl.BlockSpec(memory_space=pltpu.SMEM)] + [...  20.9 us
    ppermute x5, starting transfers between devices, down(): return lax.ppermute(a, 'head', [(h, (h - 2) % 8) for h in range(8)])  11.9 us
    ppermute x4, waiting for transfers between devices, across(): return lax.ppermute(a, 'head', [(h, h ^ 1) for h in range(8)])  11.8 us
    all_to_all x2, starting transfers between devices, shards(): got = lax.all_to_all(sent, 'ctx', 0, 0)  10 us
    ppermute x4, starting transfers between devices, across(): return lax.ppermute(a, 'head', [(h, h ^ 1) for h in range(8)])  6.93 us
    unnamed x20, local copies, waits for them, and re-layouts  5.78 us
  transfers between devices with their start and end apart: 13, of which 8 were waited for; matrix products, arithmetic and copies ran while one was open for 10% of the time, Pallas kernels for 14%

profile of v6, /device:TPU:0, one launch (start us, length us, event | category | flops | bytes accessed | tf_op | source)
XLA Modules:
  0.0 148.6 jit_solution(4508960597249270127)
XLA Ops:
  0.6 0.0 copy-start
  0.6 1.0 copy.30
  1.7 0.7 convert_bitcast_fusion
  2.3 0.1 broadcast_in_dim.33
  2.4 0.1 convert_element_type.50
  2.5 1.0 fusion.8
  3.5 0.2 slice_reduce_fusion
  3.7 0.1 subtract_exponential_fusion
  3.8 0.2 copy.25
  4.0 0.0 copy-start.8
  4.0 0.1 pad_maximum_fusion.2
  4.1 0.1 broadcast_in_dim.32
  4.2 1.8 %multiply_convert_fusion.1 = bf16[512,4,256]{2,1,0:T(4,128)(2,1)S(1)} fusion(bf16[512,4,256]{2,1,0:T(4,128)(2,1)} %param.11, f32[512,4]{1,0:T(8,128)S(1)} %copy.25), kind=kLoop, calls=%fused_computation.1 | loop fusion | flops 1572864 | bytes 2105344 | tf_op jit(solution)/shard_map/convert_element_type | solution.py:275
  6.0 0.6 convolution_convert_fusion
  6.6 0.1 broadcast_in_dim.36
  6.7 1.3 pad_maximum_fusion
  8.0 5.8 %all-to-all-start = ((bf16[16,208,256]{2,1,0:T(8,128)(2,1)}), bf16[16,208,256]{2,1,0:T(8,128)(2,1)}, u32[]{:S(2)}, u32[]{:S(2)}) async-start(bf16[16,208,256]{2,1,0:T(8,128)(2,1)} %pad_maximum_fusion), calls=%async_computation | async-start | bytes 3407872 | tf_op jit(solution)/shard_map/all_to_all | solution.py:298
  13.8 0.1 iota_compare_fusion
  13.9 4.7 %fusion = f32[4,256,512]{2,1,0:T(8,128)} fusion(f32[4,512]{1,0:T(4,128)S(1)} %bitcast.37, pred[512,512]{1,0:T(8,128)(4,1)S(1)} %iota_compare_fusion, bf16[512,4,256]{2,1,0:T(4,128)(2,1)S(1)} %copy-done.5, bf16[512,4,256]{2,1,0:T(4,128)(2,1)S(1)} %copy-done.6, bf16[512,4,256]{2,1,0:T(4,128)(2,1)} %param.12), kind=kOutput, calls=%fused_computation.3 | convolution fusion | flops 1078984704 | bytes 5513216 | tf_op jit(solution)/shard_map/hnm,mhe->nhe/dot_general | solution.py:307
  18.6 1.9 %copy.43.in_ref = f32[512,1024]{1,0:T(8,128)S(1)} copy(f32[512,1024]{0,1:T(8,128)} %bitcast.40) | data formatting | bytes 4194304 | tf_op jit(solution)/shard_map/reshape | solution.py:308
  20.6 1.4 copy.45
  22.0 15.5 %all-to-all-done.got_ref = bf16[16,208,256]{2,1,0:T(8,128)(2,1)} async-done(((bf16[16,208,256]{2,1,0:T(8,128)(2,1)}), bf16[16,208,256]{2,1,0:T(8,128)(2,1)}, u32[]{:S(2)}, u32[]{:S(2)}) %all-to-all-start) | async-done | bytes 1703968 | tf_op jit(solution)/shard_map/all_to_all | solution.py:298
  37.6 4.4 %shard_map.113 = bf16[16,96,256]{2,1,0:T(8,128)(2,1)S(1)} custom-call(bf16[16,208,256]{2,1,0:T(8,128)(2,1)} %all-to-all-done.got_ref), custom_call_target="tpu_custom_call" | custom-call | flops 1073741824 | bytes 6291456 | tf_op jit(solution)/shard_map/pallas_call | solution.py:149
  42.0 0.0 copy-start.4
  42.0 0.9 copy-done.4
  42.9 4.3 %all-to-all-start.1 = ((bf16[16,96,256]{2,1,0:T(8,128)(2,1)}), bf16[16,96,256]{2,1,0:T(8,128)(2,1)}, u32[]{:S(2)}, u32[]{:S(2)}) async-start(bf16[16,96,256]{2,1,0:T(8,128)(2,1)} %copy-done.4), calls=%async_computation.1 | async-start | bytes 1572864 | tf_op jit(solution)/shard_map/all_to_all | solution.py:313
  47.2 0.1 copy.33
  47.3 2.3 %convolution_bitcast_fusion = f32[32,4,4,256]{3,1,2,0:T(4,128)} fusion(bf16[32,4,4,256]{3,2,1,0:T(4,128)(2,1)S(1)} %copy-done, bf16[32,4,4,256]{3,2,1,0:T(4,128)(2,1)} %param.15, bf16[32,4,4,256]{3,2,1,0:T(4,128)(2,1)} %param.17, f32[32,4,4]{2,1,0:T(4,128)S(1)} %copy.33, pred[4,4]{1,0:T(4,128)(4,1)S(1)} %iota_compare_fusion.4), kind=kOutput, calls=%fused_computation.5 | convolution fusion | flops 2105344 | bytes 1312784 | tf_op jit(solution)/shard_map/rhtu,ruhe->rthe/dot_general | solution.py:327
  49.6 1.2 copy.36
  50.8 0.9 copy.46
  51.7 0.1 copy.37
  51.8 9.1 %all-to-all-done.1.got_ref = bf16[16,96,256]{2,1,0:T(8,128)(2,1)} async-done(((bf16[16,96,256]{2,1,0:T(8,128)(2,1)}), bf16[16,96,256]{2,1,0:T(8,128)(2,1)}, u32[]{:S(2)}, u32[]{:S(2)}) %all-to-all-start.1) | async-done | bytes 786464 | tf_op jit(solution)/shard_map/all_to_all | solution.py:313
  60.9 1.0 copy-done.3
  62.0 3.4 %shard_map.114 = (bf16[640,1024]{1,0:T(8,128)(2,1)}, bf16[320,1024]{1,0:T(8,128)(2,1)}, bf16[320,1024]{1,0:T(8,128)(2,1)}) custom-call(bf16[512,1024]{1,0:T(8,128)(2,1)S(1)} %bitcast.33, f32[512,1024]{1,0:T(8,128)S(1)} %copy.43.in_ref, f32[4,512]{1,0:T(4,128)S(1)} %bitcast.38, bf16[16,96,256]{2,1,0:T(8,128)(2,1)} %all-to-all-done.1.got_ref, ...), custom_call_target="tpu_custom_call" | custom-call | flops 268435456 | bytes 6291456 | tf_op jit(solution)/shard_map/pallas_call | solution.py:199
  65.4 2.8 %collective-permute-start.4 = (bf16[640,1024]{1,0:T(8,128)(2,1)}, bf16[640,1024]{1,0:T(8,128)(2,1)}, u32[]{:S(2)}, u32[]{:S(2)}) collective-permute-start(bf16[640,1024]{1,0:T(8,128)(2,1)} %get-tuple-element.44.refs_1_), channel_id=1, source_target_pairs={{0,1},{1,0},{2,3},{3,2},{4,5},{5,4},{6,7},{7,6},{8,9},{9,8},{10,11... | collective-permute-start | bytes 3932168 | tf_op jit(solution)/shard_map/ppermute | solution.py:21
  68.2 1.9 %collective-permute-start.2 = (bf16[640,1024]{1,0:T(8,128)(2,1)}, bf16[640,1024]{1,0:T(8,128)(2,1)}, u32[]{:S(2)}, u32[]{:S(2)}) collective-permute-start(bf16[640,1024]{1,0:T(8,128)(2,1)} %get-tuple-element.44.refs_1_), channel_id=1, source_target_pairs={{0,2},{1,3},{2,4},{3,5},{4,6},{5,7},{6,0},{7,1},{8,10},{9,11},{10,... | collective-permute-start | bytes 3932168 | tf_op jit(solution)/shard_map/ppermute | solution.py:13
  70.1 2.2 %collective-permute-start.3 = (bf16[320,1024]{1,0:T(8,128)(2,1)}, bf16[320,1024]{1,0:T(8,128)(2,1)S(1)}, u32[]{:S(2)}, u32[]{:S(2)}) collective-permute-start(bf16[320,1024]{1,0:T(8,128)(2,1)} %get-tuple-element.46), channel_id=1, source_target_pairs={{0,6},{1,7},{2,0},{3,1},{4,2},{5,3},{6,4},{7,5},{8,14},{9,15},{10,... | collective-permute-start | bytes 1966088 | tf_op jit(solution)/shard_map/ppermute | solution.py:17
  72.2 2.0 %collective-permute-start = (bf16[320,1024]{1,0:T(8,128)(2,1)}, bf16[320,1024]{1,0:T(8,128)(2,1)}, u32[]{:S(2)}, u32[]{:S(2)}) collective-permute-start(bf16[320,1024]{1,0:T(8,128)(2,1)} %get-tuple-element.43), channel_id=1, source_target_pairs={{0,6},{1,7},{2,0},{3,1},{4,2},{5,3},{6,4},{7,5},{8,14},{9,15},{10,... | collective-permute-start | bytes 1966088 | tf_op jit(solution)/shard_map/ppermute | solution.py:17
  74.3 4.4 %shard_map.115.refs_6_ = f32[640,1024]{1,0:T(8,128)S(1)} custom-call(s32[1]{0:T(128)} %bitcast.14.refs_0_, bf16[640,1024]{1,0:T(8,128)(2,1)} %get-tuple-element.44.refs_1_, bf16[8192,1024]{1,0:T(8,128)(2,1)} %refs_6_.1), custom_call_target="tpu_custom_call" | custom-call | flops 1310720 | bytes 1024 | tf_op jit(solution)/shard_map/pallas_call | solution.py:91
  78.7 9.3 %collective-permute-done.3.refs_3_ = bf16[320,1024]{1,0:T(8,128)(2,1)S(1)} collective-permute-done((bf16[320,1024]{1,0:T(8,128)(2,1)}, bf16[320,1024]{1,0:T(8,128)(2,1)S(1)}, u32[]{:S(2)}, u32[]{:S(2)}) %collective-permute-start.3) | collective-permute-done | bytes 655392 | tf_op jit(solution)/shard_map/ppermute | solution.py:17
  88.0 9.6 %collective-permute-done.4.refs_4_ = bf16[640,1024]{1,0:T(8,128)(2,1)} collective-permute-done((bf16[640,1024]{1,0:T(8,128)(2,1)}, bf16[640,1024]{1,0:T(8,128)(2,1)}, u32[]{:S(2)}, u32[]{:S(2)}) %collective-permute-start.4) | collective-permute-done | bytes 1310752 | tf_op jit(solution)/shard_map/ppermute | solution.py:21
  97.6 1.9 %collective-permute-start.8 = (bf16[640,1024]{1,0:T(8,128)(2,1)}, bf16[640,1024]{1,0:T(8,128)(2,1)}, u32[]{:S(2)}, u32[]{:S(2)}) collective-permute-start(bf16[640,1024]{1,0:T(8,128)(2,1)} %collective-permute-done.4.refs_4_), channel_id=1, source_target_pairs={{0,2},{1,3},{2,4},{3,5},{4,6},{5,7},{6,0},{7,1},{8,10},{9,11},{10,... | collective-permute-start | bytes 3932168 | tf_op jit(solution)/shard_map/ppermute | solution.py:13
  99.5 0.8 collective-permute-done.refs_2_
  100.3 1.9 %collective-permute-start.1 = (bf16[320,1024]{1,0:T(8,128)(2,1)}, bf16[320,1024]{1,0:T(8,128)(2,1)}, u32[]{:S(2)}, u32[]{:S(2)}) collective-permute-start(bf16[320,1024]{1,0:T(8,128)(2,1)} %collective-permute-done.refs_2_), channel_id=1, source_target_pairs={{0,1},{1,0},{2,3},{3,2},{4,5},{5,4},{6,7},{7,6},{8,9},{9,8},{10,11... | collective-permute-start | bytes 1966088 | tf_op jit(solution)/shard_map/ppermute | solution.py:21
  102.2 2.3 %collective-permute-start.6 = (bf16[320,1024]{1,0:T(8,128)(2,1)S(1)}, bf16[320,1024]{1,0:T(8,128)(2,1)}, u32[]{:S(2)}, u32[]{:S(2)}) collective-permute-start(bf16[320,1024]{1,0:T(8,128)(2,1)S(1)} %collective-permute-done.3.refs_3_), channel_id=1, source_target_pairs={{0,6},{1,7},{2,0},{3,1},{4,2},{5,3},{6,4},{7,5},{8,14},{9,15},{10,... | collective-permute-start | bytes 1966088 | tf_op jit(solution)/shard_map/ppermute | solution.py:17
  104.6 0.1 pad_add_fusion.refs_0_
  104.6 0.0 collective-permute-done.2.refs_1_
  104.6 1.9 %collective-permute-start.9 = (bf16[320,1024]{1,0:T(8,128)(2,1)}, bf16[320,1024]{1,0:T(8,128)(2,1)}, u32[]{:S(2)}, u32[]{:S(2)}) collective-permute-start(bf16[320,1024]{1,0:T(8,128)(2,1)} %collective-permute-done.refs_2_), channel_id=1, source_target_pairs={{0,6},{1,7},{2,0},{3,1},{4,2},{5,3},{6,4},{7,5},{8,14},{9,15},{10,... | collective-permute-start | bytes 1966088 | tf_op jit(solution)/shard_map/ppermute | solution.py:17
  106.5 1.5 collective-permute-start.10
  108.0 8.1 %shard_map.116.refs_7_ = f32[640,1024]{1,0:T(8,128)S(1)} custom-call(s32[3]{0:T(128)S(1)} %pad_add_fusion.refs_0_, bf16[640,1024]{1,0:T(8,128)(2,1)} %collective-permute-done.2.refs_1_, bf16[320,1024]{1,0:T(8,128)(2,1)} %collective-permute-done.refs_2_, bf16[320,1024]{1,0:T(8,128)(2,1)S(1)} %collective-permute-done.3.refs_3_, ...), custom_call_target="tpu_custom_call" | custom-call | flops 3932160 | bytes 1024 | tf_op jit(solution)/shard_map/pallas_call | solution.py:91
  116.1 1.5 %copy-done.1 = f32[640,1024]{1,0:T(8,128)} copy-done((f32[640,1024]{1,0:T(8,128)}, f32[640,1024]{1,0:T(8,128)S(1)}, u32[]{:S(2)}) %copy-start.1) | copy-done | bytes 2621464
  117.6 2.2 %collective-permute-done.1.refs_4_ = bf16[320,1024]{1,0:T(8,128)(2,1)} collective-permute-done((bf16[320,1024]{1,0:T(8,128)(2,1)}, bf16[320,1024]{1,0:T(8,128)(2,1)}, u32[]{:S(2)}, u32[]{:S(2)}) %collective-permute-start.1) | collective-permute-done | bytes 655392 | tf_op jit(solution)/shard_map/ppermute | solution.py:21
  119.8 3.5 %collective-permute-start.5 = (bf16[320,1024]{1,0:T(8,128)(2,1)}, bf16[320,1024]{1,0:T(8,128)(2,1)S(1)}, u32[]{:S(2)}, u32[]{:S(2)}) collective-permute-start(bf16[320,1024]{1,0:T(8,128)(2,1)} %collective-permute-done.1.refs_4_), channel_id=1, source_target_pairs={{0,6},{1,7},{2,0},{3,1},{4,2},{5,3},{6,4},{7,5},{8,14},{9,15},{10,... | collective-permute-start | bytes 1966088 | tf_op jit(solution)/shard_map/ppermute | solution.py:17
  123.3 0.0 collective-permute-done.6.refs_3_
  123.3 0.8 collective-permute-start.7
  124.1 0.1 pad_add_fusion.1.refs_0_
  124.1 1.9 %constant_dynamic-slice_fusion.refs_2_ = bf16[1024,1024]{1,0:T(8,128)(2,1)S(1)} fusion(bf16[8192,1024]{1,0:T(8,128)(2,1)} %refs_6_.1, s32[]{:T(128)S(6)} %select_n.52), kind=kLoop, calls=%fused_computation.50 | loop fusion | bytes 4194308 | tf_op jit(solution)/shard_map/dynamic_slice | solution.py:241
  126.1 8.0 %collective-permute-done.9.refs_2_ = bf16[320,1024]{1,0:T(8,128)(2,1)} collective-permute-done((bf16[320,1024]{1,0:T(8,128)(2,1)}, bf16[320,1024]{1,0:T(8,128)(2,1)}, u32[]{:S(2)}, u32[]{:S(2)}) %collective-permute-start.9) | collective-permute-done | bytes 655392 | tf_op jit(solution)/shard_map/ppermute | solution.py:17
  134.1 0.0 collective-permute-done.10.refs_5_
  134.1 8.3 %shard_map.117.refs_3_ = f32[640,1024]{1,0:T(8,128)S(1)} custom-call(s32[3]{0:T(128)S(1)} %pad_add_fusion.1.refs_0_, bf16[640,1024]{1,0:T(8,128)(2,1)} %collective-permute-done.8.refs_1_, bf16[320,1024]{1,0:T(8,128)(2,1)} %collective-permute-done.9.refs_2_, bf16[320,1024]{1,0:T(8,128)(2,1)} %collective-permute-done.6.refs_3_, ...), custom_call_target="tpu_custom_call" | custom-call | flops 3932160 | bytes 1024 | tf_op jit(solution)/shard_map/pallas_call | solution.py:91
  142.4 2.9 %collective-permute-done.5.refs_0_ = bf16[320,1024]{1,0:T(8,128)(2,1)S(1)} collective-permute-done((bf16[320,1024]{1,0:T(8,128)(2,1)}, bf16[320,1024]{1,0:T(8,128)(2,1)S(1)}, u32[]{:S(2)}, u32[]{:S(2)}) %collective-permute-start.5) | collective-permute-done | bytes 655392 | tf_op jit(solution)/shard_map/ppermute | solution.py:17
  145.3 0.0 collective-permute-done.7.refs_1_
  145.3 2.5 %shard_map.118 = (bf16[512,1024]{1,0:T(8,128)(2,1)}, bf16[128,1024]{1,0:T(8,128)(2,1)S(1)}) custom-call(bf16[320,1024]{1,0:T(8,128)(2,1)S(1)} %collective-permute-done.5.refs_0_, bf16[320,1024]{1,0:T(8,128)(2,1)S(1)} %collective-permute-done.7.refs_1_, bf16[1024,1024]{1,0:T(8,128)(2,1)S(1)} %constant_dynamic-slice_fusion.refs_2_, ...), custom_call_target="tpu_custom_call" | custom-call | flops 1310720 | bytes 1024 | tf_op jit(solution)/shard_map/pallas_call | solution.py:83
  147.8 0.8 reshape.105
  (20 shorter events, 0.2 us)
Async XLA Ops:
  0.6 46.7 %copy-start = (bf16[32,4,4,256]{3,2,1,0:T(4,128)(2,1)S(1)}, bf16[32,4,4,256]{3,2,1,0:T(4,128)(2,1)}, u32[]{:S(2)}) copy-start(bf16[32,4,4,256]{3,2,1,0:T(4,128)(2,1)} %param.16) | copy-start | bytes 786436
  4.0 2.1 %copy-start.8 = (bf16[512,4,256]{2,1,0:T(4,128)(2,1)S(1)}, bf16[512,4,256]{2,1,0:T(4,128)(2,1)}, u32[]{:S(2)}) copy-start(bf16[512,4,256]{2,1,0:T(4,128)(2,1)} %param.12) | copy-start | bytes 3145732
  8.0 5.9 %copy-start.5 = (bf16[512,4,256]{2,1,0:T(4,128)(2,1)S(1)}, bf16[512,4,256]{2,1,0:T(4,128)(2,1)}, u32[]{:S(2)}) copy-start(bf16[512,4,256]{2,1,0:T(4,128)(2,1)} %param.11) | copy-start | bytes 3145732
  8.0 5.9 %copy-start.6 = (bf16[512,4,256]{2,1,0:T(4,128)(2,1)S(1)}, bf16[512,4,256]{2,1,0:T(4,128)(2,1)}, u32[]{:S(2)}) copy-start(bf16[512,4,256]{2,1,0:T(4,128)(2,1)} %param.10) | copy-start | bytes 3145732
  8.0 29.5 %all-to-all-start = ((bf16[16,208,256]{2,1,0:T(8,128)(2,1)}), bf16[16,208,256]{2,1,0:T(8,128)(2,1)}, u32[]{:S(2)}, u32[]{:S(2)}) async-start(bf16[16,208,256]{2,1,0:T(8,128)(2,1)} %pad_maximum_fusion), calls=%async_computation | async-start | bytes 3407872 | tf_op jit(solution)/shard_map/all_to_all | solution.py:298
  37.6 9.6 %copy-start.7 = (f32[4,4,32]{2,1,0:T(4,128)S(1)}, f32[4,4,32]{2,1,0:T(4,128)}, u32[]{:S(2)}) copy-start(f32[4,4,32]{2,1,0:T(4,128)} %param.18) | copy-start | bytes 6148
  42.0 0.9 copy-start.4
  42.9 18.1 %all-to-all-start.1 = ((bf16[16,96,256]{2,1,0:T(8,128)(2,1)}), bf16[16,96,256]{2,1,0:T(8,128)(2,1)}, u32[]{:S(2)}, u32[]{:S(2)}) async-start(bf16[16,96,256]{2,1,0:T(8,128)(2,1)} %copy-done.4), calls=%async_computation.1 | async-start | bytes 1572864 | tf_op jit(solution)/shard_map/all_to_all | solution.py:313
  60.9 1.0 copy-start.3
  65.4 32.2 %collective-permute-start.4 = (bf16[640,1024]{1,0:T(8,128)(2,1)}, bf16[640,1024]{1,0:T(8,128)(2,1)}, u32[]{:S(2)}, u32[]{:S(2)}) collective-permute-start(bf16[640,1024]{1,0:T(8,128)(2,1)} %get-tuple-element.44.refs_1_), channel_id=1, source_target_pairs={{0,1},{1,0},{2,3},{3,2},{4,5},{5,4},{6,7},{7,6},{8,9},{9,8},{10,11... | collective-permute-start | bytes 3932168 | tf_op jit(solution)/shard_map/ppermute | solution.py:21
  68.2 36.5 %collective-permute-start.2 = (bf16[640,1024]{1,0:T(8,128)(2,1)}, bf16[640,1024]{1,0:T(8,128)(2,1)}, u32[]{:S(2)}, u32[]{:S(2)}) collective-permute-start(bf16[640,1024]{1,0:T(8,128)(2,1)} %get-tuple-element.44.refs_1_), channel_id=1, source_target_pairs={{0,2},{1,3},{2,4},{3,5},{4,6},{5,7},{6,0},{7,1},{8,10},{9,11},{10,... | collective-permute-start | bytes 3932168 | tf_op jit(solution)/shard_map/ppermute | solution.py:13
  70.1 17.9 %collective-permute-start.3 = (bf16[320,1024]{1,0:T(8,128)(2,1)}, bf16[320,1024]{1,0:T(8,128)(2,1)S(1)}, u32[]{:S(2)}, u32[]{:S(2)}) collective-permute-start(bf16[320,1024]{1,0:T(8,128)(2,1)} %get-tuple-element.46), channel_id=1, source_target_pairs={{0,6},{1,7},{2,0},{3,1},{4,2},{5,3},{6,4},{7,5},{8,14},{9,15},{10,... | collective-permute-start | bytes 1966088 | tf_op jit(solution)/shard_map/ppermute | solution.py:17
  72.2 28.1 %collective-permute-start = (bf16[320,1024]{1,0:T(8,128)(2,1)}, bf16[320,1024]{1,0:T(8,128)(2,1)}, u32[]{:S(2)}, u32[]{:S(2)}) collective-permute-start(bf16[320,1024]{1,0:T(8,128)(2,1)} %get-tuple-element.43), channel_id=1, source_target_pairs={{0,6},{1,7},{2,0},{3,1},{4,2},{5,3},{6,4},{7,5},{8,14},{9,15},{10,... | collective-permute-start | bytes 1966088 | tf_op jit(solution)/shard_map/ppermute | solution.py:17
  97.6 36.5 %collective-permute-start.8 = (bf16[640,1024]{1,0:T(8,128)(2,1)}, bf16[640,1024]{1,0:T(8,128)(2,1)}, u32[]{:S(2)}, u32[]{:S(2)}) collective-permute-start(bf16[640,1024]{1,0:T(8,128)(2,1)} %collective-permute-done.4.refs_4_), channel_id=1, source_target_pairs={{0,2},{1,3},{2,4},{3,5},{4,6},{5,7},{6,0},{7,1},{8,10},{9,11},{10,... | collective-permute-start | bytes 3932168 | tf_op jit(solution)/shard_map/ppermute | solution.py:13
  100.3 19.5 %collective-permute-start.1 = (bf16[320,1024]{1,0:T(8,128)(2,1)}, bf16[320,1024]{1,0:T(8,128)(2,1)}, u32[]{:S(2)}, u32[]{:S(2)}) collective-permute-start(bf16[320,1024]{1,0:T(8,128)(2,1)} %collective-permute-done.refs_2_), channel_id=1, source_target_pairs={{0,1},{1,0},{2,3},{3,2},{4,5},{5,4},{6,7},{7,6},{8,9},{9,8},{10,11... | collective-permute-start | bytes 1966088 | tf_op jit(solution)/shard_map/ppermute | solution.py:21
  102.2 21.1 %collective-permute-start.6 = (bf16[320,1024]{1,0:T(8,128)(2,1)S(1)}, bf16[320,1024]{1,0:T(8,128)(2,1)}, u32[]{:S(2)}, u32[]{:S(2)}) collective-permute-start(bf16[320,1024]{1,0:T(8,128)(2,1)S(1)} %collective-permute-done.3.refs_3_), channel_id=1, source_target_pairs={{0,6},{1,7},{2,0},{3,1},{4,2},{5,3},{6,4},{7,5},{8,14},{9,15},{10,... | collective-permute-start | bytes 1966088 | tf_op jit(solution)/shard_map/ppermute | solution.py:17
  104.6 29.4 %collective-permute-start.9 = (bf16[320,1024]{1,0:T(8,128)(2,1)}, bf16[320,1024]{1,0:T(8,128)(2,1)}, u32[]{:S(2)}, u32[]{:S(2)}) collective-permute-start(bf16[320,1024]{1,0:T(8,128)(2,1)} %collective-permute-done.refs_2_), channel_id=1, source_target_pairs={{0,6},{1,7},{2,0},{3,1},{4,2},{5,3},{6,4},{7,5},{8,14},{9,15},{10,... | collective-permute-start | bytes 1966088 | tf_op jit(solution)/shard_map/ppermute | solution.py:17
  106.5 27.6 %collective-permute-start.10 = (bf16[320,1024]{1,0:T(8,128)(2,1)S(1)}, bf16[320,1024]{1,0:T(8,128)(2,1)}, u32[]{:S(2)}, u32[]{:S(2)}) collective-permute-start(bf16[320,1024]{1,0:T(8,128)(2,1)S(1)} %collective-permute-done.3.refs_3_), channel_id=1, source_target_pairs={{0,1},{1,0},{2,3},{3,2},{4,5},{5,4},{6,7},{7,6},{8,9},{9,8},{10,11... | collective-permute-start | bytes 1966088 | tf_op jit(solution)/shard_map/ppermute | solution.py:21
  116.1 1.5 %copy-start.1 = (f32[640,1024]{1,0:T(8,128)}, f32[640,1024]{1,0:T(8,128)S(1)}, u32[]{:S(2)}) copy-start(f32[640,1024]{1,0:T(8,128)S(1)} %shard_map.116.refs_7_) | copy-start | bytes 7864324
  119.8 25.5 %collective-permute-start.5 = (bf16[320,1024]{1,0:T(8,128)(2,1)}, bf16[320,1024]{1,0:T(8,128)(2,1)S(1)}, u32[]{:S(2)}, u32[]{:S(2)}) collective-permute-start(bf16[320,1024]{1,0:T(8,128)(2,1)} %collective-permute-done.1.refs_4_), channel_id=1, source_target_pairs={{0,6},{1,7},{2,0},{3,1},{4,2},{5,3},{6,4},{7,5},{8,14},{9,15},{10,... | collective-permute-start | bytes 1966088 | tf_op jit(solution)/shard_map/ppermute | solution.py:17
  123.3 22.0 %collective-permute-start.7 = (bf16[320,1024]{1,0:T(8,128)(2,1)}, bf16[320,1024]{1,0:T(8,128)(2,1)S(1)}, u32[]{:S(2)}, u32[]{:S(2)}) collective-permute-start(bf16[320,1024]{1,0:T(8,128)(2,1)} %collective-permute-done.6.refs_3_), channel_id=1, source_target_pairs={{0,1},{1,0},{2,3},{3,2},{4,5},{5,4},{6,7},{7,6},{8,9},{9,8},{10,11... | collective-permute-start | bytes 1966088 | tf_op jit(solution)/shard_map/ppermute | solution.py:21
  124.1 9.9 %copy-start.2 = (f32[640,1024]{1,0:T(8,128)S(1)}, f32[640,1024]{1,0:T(8,128)}, u32[]{:S(2)}) copy-start(f32[640,1024]{1,0:T(8,128)} %copy-done.1) | copy-start | bytes 7864324

commit v7 on v6

--- a/solution.py
+++ b/solution.py
@@ -25,7 +25,7 @@
     return lax.optimization_barrier((values, others))[0]
 
 
-def project(total, srcs, terms, heads, w, split=None):
+def project(total, srcs, terms, heads, w, split=None, steps=None):
     width, columns = srcs[0].shape[1], w.shape[1]
     n_slot = 0 if heads is None else len(heads)
     old = [] if isinstance(total, int) else [total]
@@ -48,7 +48,9 @@
                 out_refs[0][a0 : a0 + top, :] = part[:top].astype(BF)
             if top < n:
                 below = a0 + top - split
-                out_refs[1][below : below + n - top, :] = part[top:].astype(BF)
+                first, some = below // steps, (n - top) // steps
+                rest = part[top:].reshape(some, steps, columns)
+                out_refs[1][first : first + some] = rest.astype(BF)
 
     def body(*refs):
         if heads is None:
@@ -74,7 +76,8 @@
     if split is None:
         out = [jax.ShapeDtypeStruct((rows, columns), F32)]
     else:
-        out = [jax.ShapeDtypeStruct((r, columns), BF) for r in (split, rows - split)]
+        shapes = (split, columns), ((rows - split) // steps, steps, columns)
+        out = [jax.ShapeDtypeStruct(shape, BF) for shape in shapes]
     flops = sum(2 * t[3] * width * columns for t in terms)
     cost = pl.CostEstimate(
         flops=flops >> 10, bytes_accessed=1 << 10, transcendentals=0
@@ -108,6 +111,43 @@
 NT = (((1,), (1,)), ((), ()))
 
 
+def first_parcels(own_state, parts, named, queries):
+    heads, dim, _ = own_state.shape
+    slots, rows = queries.shape[1], named.shape[1]
+    count = lax.axis_size("ctx")
+    per_head = count // heads
+    slice_rows = heads * dim // count
+
+    def body(s_ref, p_ref, n_ref, q_ref, o_ref):
+        row = lax.broadcasted_iota(jnp.int32, (rows, slots), 0)
+        lane = lax.broadcasted_iota(jnp.int32, (rows, slots), 1)
+        first = row * (slots // rows)
+        mine = (lane >= first) & (lane < first + slots // rows)
+        sections = jnp.broadcast_to(n_ref[...].astype(F32), (8, rows)).astype(BF)
+        sections = jnp.dot(sections, mine.astype(BF), preferred_element_type=F32)[:1]
+        sections = jnp.concatenate([sections, jnp.zeros((1, dim - slots), F32)], axis=1)
+        line = lax.broadcasted_iota(jnp.int32, (16, dim), 0)
+        for h in range(heads):
+            header = jnp.where(line == 3, sections, 0.0)
+            for i in range(3):
+                header = jnp.where(line == i, p_ref[h : h + 1, i : i + 1], header)
+            header = header.astype(BF)
+            for k in range(per_head):
+                c = h * per_head + k
+                o_ref[c, :slice_rows, :] = s_ref[h, k * slice_rows : (k + 1) * slice_rows, :]
+                o_ref[c, slice_rows : slice_rows + 16, :] = header
+                o_ref[c, slice_rows + 16 :, :] = q_ref[h]
+
+    return pl.pallas_call(
+        body,
+        in_specs=[WHOLE] * 4,
+        out_specs=WHOLE,
+        out_shape=jax.ShapeDtypeStruct((count, slice_rows + 16 + slots, dim), BF),
+        compiler_params=pltpu.CompilerParams(vmem_limit_bytes=12 << 20),
+        cost_estimate=pl.CostEstimate(flops=0, bytes_accessed=3 << 20, transcendentals=0),
+    )(own_state, parts, named, queries)
+
+
 def scan_and_read(got, slice_rows, slots):
     sections, _, dim = got.shape
     head_rows, half = got.shape[1] - slice_rows - slots, slice_rows // 2
@@ -152,7 +192,7 @@
         out_specs=WHOLE,
         out_shape=jax.ShapeDtypeStruct((sections, slice_rows + half, dim), BF),
         scratch_shapes=[pltpu.VMEM((sections * slice_rows, dim), BF)],
-        compiler_params=pltpu.CompilerParams(vmem_limit_bytes=12 << 20),
+        compiler_params=pltpu.CompilerParams(vmem_limit_bytes=58 << 20),
         cost_estimate=pl.CostEstimate(
             flops=2 * sections * slots * sections * slice_rows * dim,
             bytes_accessed=6 << 20,
@@ -209,7 +249,7 @@
     )(queries, within, logs, got, own, kept)
 
 
-def gathered_projection(blocks, split, w):
+def gathered_projection(blocks, split, steps, w):
     me = lax.axis_index("head")
     z, x = me // 2, me % 2
     here, far = lambda d: ((z + d) % 4) * 2 + x, lambda d: ((z + d) % 4) * 2 + 1 - x
@@ -249,7 +289,7 @@
     last_top, last_bottom, total, w_last = lax.optimization_barrier(
         (last_top, last_bottom, total, w_last)
     )
-    return project(total, [last_top, last_bottom], halves(0, 0), None, w_last, split)
+    return project(total, [last_top, last_bottom], halves(0, 0), None, w_last, split, steps)
 
 
 def shards(
@@ -278,23 +318,9 @@
     slice_rows, slots = heads * dim // sections, rows * steps
     high = lax.reduce_precision(total_decay, 8, 7)
     middle = lax.reduce_precision(total_decay - high, 8, 7)
-    parts = jnp.stack([high, middle, total_decay - high - middle], axis=1).astype(BF)
-    parts = jnp.broadcast_to(parts[:, None, :, None], (heads, sections // heads, 3, dim))
-    named = jnp.broadcast_to(prompt_section, (rows, steps)).reshape(1, 1, slots).astype(BF)
-    named = jnp.pad(named, ((0, 0), (0, 0), (0, dim - slots)))
-    named = jnp.broadcast_to(named, (sections, 1, dim))
-    header = jnp.concatenate([parts.reshape(sections, 3, dim), named], axis=1)
-    header = jnp.pad(header, ((0, 0), (0, 12), (0, 0)))
+    parts = jnp.stack([high, middle, total_decay - high - middle], axis=1)
     asked = q_step.reshape(slots, heads, dim).transpose(1, 0, 2)
-    asked = jnp.broadcast_to(asked[:, None], (heads, sections // heads, slots, dim))
-    sent = jnp.concatenate(
-        [
-            own_state.astype(BF).reshape(sections, slice_rows, dim),
-            header,
-            asked.reshape(sections, slots, dim),
-        ],
-        axis=1,
-    )
+    sent = first_parcels(own_state.astype(BF), parts, prompt_section.reshape(1, rows), asked)
     got = lax.all_to_all(sent, "ctx", 0, 0)
 
     q_late, k_late, v_late, cum_late = after((q_prompt, k_prompt, v_prompt, cumlog), sent)
@@ -329,8 +355,7 @@
     kept = jnp.exp(step_logs).reshape(slots, heads)
 
     blocks = retain(queries, within, cum_late, got, slice_rows, own, kept)
-    prompt_out, step_out = gathered_projection(blocks, tokens, w_out)
-    return prompt_out, step_out.reshape(rows, steps, w_out.shape[1])
+    return tuple(gathered_projection(blocks, tokens, steps, w_out))
 
 
 def solution(mesh):

time: 149 us -> 147 us (0.987)
  Pallas kernels: 31.1 us -> 33.5 us
  local copies, waits for them, and re-layouts: 13.4 us -> 11.3 us
  other arithmetic: 4.48 us -> 2.39 us
where the time goes in v7:
time: 147 us
  waiting for transfers between devices  57.5 us (39%)
  Pallas kernels  33.5 us (23%)
  starting transfers between devices  32.6 us (22%)
  local copies, waits for them, and re-layouts  11.3 us (8%)
  matrix products  8.65 us (6%)
  other arithmetic  2.39 us (2%)
    all_to_all x2, waiting for transfers between devices, shards(): got = lax.all_to_all(sent, 'ctx', 0, 0)  24.6 us
    ppermute x5, waiting for transfers between devices, down(): return lax.ppermute(a, 'head', [(h, (h - 2) % 8) for h in range(8)])  21 us
    pallas_call x3, Pallas kernels, project(): pl.pallas_call(body, in_specs=[pl.BlockSpec(memory_space=pltpu.SMEM)] + [...  20.9 us
    ppermute x4, waiting for transfers between devices, across(): return lax.ppermute(a, 'head', [(h, h ^ 1) for h in range(8)])  11.9 us
    ppermute x5, starting transfers between devices, down(): return lax.ppermute(a, 'head', [(h, (h - 2) % 8) for h in range(8)])  11.8 us
    all_to_all x2, starting transfers between devices, shards(): got = lax.all_to_all(sent, 'ctx', 0, 0)  10.1 us
    ppermute x4, starting transfers between devices, across(): return lax.ppermute(a, 'head', [(h, h ^ 1) for h in range(8)])  7.04 us
    pallas_call x1, Pallas kernels, scan_and_read(): pl.pallas_call(body, in_specs=[WHOLE], out_specs=WHOLE, out_shape=jax.Sha...  5.25 us
  transfers between devices with their start and end apart: 13, of which 8 were waited for; matrix products, arithmetic and copies ran while one was open for 10% of the time, Pallas kernels for 14%

profile of v7, /device:TPU:0, one launch (start us, length us, event | category | flops | bytes accessed | tf_op | source)
XLA Modules:
  0.0 146.8 jit_solution(13817272129857261180)
XLA Ops:
  0.6 0.0 copy-start
  0.6 0.0 copy-start.8
  0.7 1.1 fusion.9
  1.7 0.2 fusion.24
  1.9 0.1 subtract_exponential_fusion
  2.0 0.2 copy.24
  2.2 1.0 copy.66
  3.2 1.8 %multiply_convert_fusion.1 = bf16[512,4,256]{2,1,0:T(4,128)(2,1)S(1)} fusion(bf16[512,4,256]{2,1,0:T(4,128)(2,1)} %param.11, f32[512,4]{1,0:T(8,128)S(1)} %copy.24), kind=kLoop, calls=%fused_computation.1 | loop fusion | flops 1572864 | bytes 2105344 | tf_op jit(solution)/shard_map/convert_element_type | solution.py:315
  4.9 0.0 copy-done.8
  4.9 0.0 copy-start.4
  4.9 0.6 fusion.1.s_ref
  5.5 0.1 pad_maximum_fusion.1.p_ref
  5.6 0.0 copy-done.4
  5.6 1.4 shard_map.113
  6.9 5.8 %all-to-all-start = ((bf16[16,208,256]{2,1,0:T(8,128)(2,1)}), bf16[16,208,256]{2,1,0:T(8,128)(2,1)}, u32[]{:S(2)}, u32[]{:S(2)}) async-start(bf16[16,208,256]{2,1,0:T(8,128)(2,1)} %shard_map.113), calls=%async_computation | async-start | bytes 3407872 | tf_op jit(solution)/shard_map/all_to_all | solution.py:324
  12.7 0.1 iota_compare_fusion
  12.8 0.0 copy-done.5
  12.8 0.0 copy-done.6
  12.8 4.7 %fusion = f32[4,256,512]{2,1,0:T(8,128)} fusion(f32[4,512]{1,0:T(4,128)S(1)} %bitcast.35, pred[512,512]{1,0:T(8,128)(4,1)S(1)} %iota_compare_fusion, bf16[512,4,256]{2,1,0:T(4,128)(2,1)S(1)} %copy-done.5, bf16[512,4,256]{2,1,0:T(4,128)(2,1)S(1)} %copy-done.6, bf16[512,4,256]{2,1,0:T(4,128)(2,1)} %param.12), kind=kOutput, calls=%fused_computation.2 | convolution fusion | flops 1078984704 | bytes 5513216 | tf_op jit(solution)/shard_map/hnm,mhe->nhe/dot_general | solution.py:333
  17.6 1.9 %copy.42.in_ref = f32[512,1024]{1,0:T(8,128)S(1)} copy(f32[512,1024]{0,1:T(8,128)} %bitcast.38) | data formatting | bytes 4194304 | tf_op jit(solution)/shard_map/reshape | solution.py:334
  19.5 1.4 copy.43
  20.9 15.5 %all-to-all-done.got_ref = bf16[16,208,256]{2,1,0:T(8,128)(2,1)} async-done(((bf16[16,208,256]{2,1,0:T(8,128)(2,1)}), bf16[16,208,256]{2,1,0:T(8,128)(2,1)}, u32[]{:S(2)}, u32[]{:S(2)}) %all-to-all-start) | async-done | bytes 1703968 | tf_op jit(solution)/shard_map/all_to_all | solution.py:324
  36.5 5.3 %shard_map.114 = bf16[16,96,256]{2,1,0:T(8,128)(2,1)} custom-call(bf16[16,208,256]{2,1,0:T(8,128)(2,1)} %all-to-all-done.got_ref), custom_call_target="tpu_custom_call" | custom-call | flops 1073741824 | bytes 6291456 | tf_op jit(solution)/shard_map/pallas_call | solution.py:189
  41.7 4.3 %all-to-all-start.1 = ((bf16[16,96,256]{2,1,0:T(8,128)(2,1)}), bf16[16,96,256]{2,1,0:T(8,128)(2,1)}, u32[]{:S(2)}, u32[]{:S(2)}) async-start(bf16[16,96,256]{2,1,0:T(8,128)(2,1)} %shard_map.114), calls=%async_computation.1 | async-start | bytes 1572864 | tf_op jit(solution)/shard_map/all_to_all | solution.py:339
  46.0 0.0 copy-done.7
  46.1 0.1 copy.31
  46.2 0.0 copy-done
  46.2 2.3 %convolution_bitcast_fusion = f32[32,4,4,256]{3,1,2,0:T(4,128)} fusion(bf16[32,4,4,256]{3,2,1,0:T(4,128)(2,1)S(1)} %copy-done, bf16[32,4,4,256]{3,2,1,0:T(4,128)(2,1)} %param.15, bf16[32,4,4,256]{3,2,1,0:T(4,128)(2,1)} %param.17, f32[32,4,4]{2,1,0:T(4,128)S(1)} %copy.31, pred[4,4]{1,0:T(4,128)(4,1)S(1)} %iota_compare_fusion.3), kind=kOutput, calls=%fused_computation.5 | convolution fusion | flops 2105344 | bytes 1312784 | tf_op jit(solution)/shard_map/rhtu,ruhe->rthe/dot_general | solution.py:353
  48.5 1.2 copy.34
  49.7 0.9 copy.44
  50.6 0.1 copy.35
  50.7 9.1 %all-to-all-done.1.got_ref = bf16[16,96,256]{2,1,0:T(8,128)(2,1)} async-done(((bf16[16,96,256]{2,1,0:T(8,128)(2,1)}), bf16[16,96,256]{2,1,0:T(8,128)(2,1)}, u32[]{:S(2)}, u32[]{:S(2)}) %all-to-all-start.1) | async-done | bytes 786464 | tf_op jit(solution)/shard_map/all_to_all | solution.py:339
  59.8 1.0 copy-done.3
  60.8 3.4 %shard_map.115 = (bf16[640,1024]{1,0:T(8,128)(2,1)}, bf16[320,1024]{1,0:T(8,128)(2,1)}, bf16[320,1024]{1,0:T(8,128)(2,1)}) custom-call(bf16[512,1024]{1,0:T(8,128)(2,1)S(1)} %bitcast.30, f32[512,1024]{1,0:T(8,128)S(1)} %copy.42.in_ref, f32[4,512]{1,0:T(4,128)S(1)} %bitcast.36, bf16[16,96,256]{2,1,0:T(8,128)(2,1)} %all-to-all-done.1.got_ref, ...), custom_call_target="tpu_custom_call" | custom-call | flops 268435456 | bytes 6291456 | tf_op jit(solution)/shard_map/pallas_call | solution.py:239
  64.2 2.9 %collective-permute-start.4 = (bf16[640,1024]{1,0:T(8,128)(2,1)}, bf16[640,1024]{1,0:T(8,128)(2,1)}, u32[]{:S(2)}, u32[]{:S(2)}) collective-permute-start(bf16[640,1024]{1,0:T(8,128)(2,1)} %get-tuple-element.42.refs_1_), channel_id=1, source_target_pairs={{0,1},{1,0},{2,3},{3,2},{4,5},{5,4},{6,7},{7,6},{8,9},{9,8},{10,11... | collective-permute-start | bytes 3932168 | tf_op jit(solution)/shard_map/ppermute | solution.py:21
  67.1 1.9 %collective-permute-start.2 = (bf16[640,1024]{1,0:T(8,128)(2,1)}, bf16[640,1024]{1,0:T(8,128)(2,1)}, u32[]{:S(2)}, u32[]{:S(2)}) collective-permute-start(bf16[640,1024]{1,0:T(8,128)(2,1)} %get-tuple-element.42.refs_1_), channel_id=1, source_target_pairs={{0,2},{1,3},{2,4},{3,5},{4,6},{5,7},{6,0},{7,1},{8,10},{9,11},{10,... | collective-permute-start | bytes 3932168 | tf_op jit(solution)/shard_map/ppermute | solution.py:13
  68.9 2.1 %collective-permute-start.3 = (bf16[320,1024]{1,0:T(8,128)(2,1)}, bf16[320,1024]{1,0:T(8,128)(2,1)S(1)}, u32[]{:S(2)}, u32[]{:S(2)}) collective-permute-start(bf16[320,1024]{1,0:T(8,128)(2,1)} %get-tuple-element.44), channel_id=1, source_target_pairs={{0,6},{1,7},{2,0},{3,1},{4,2},{5,3},{6,4},{7,5},{8,14},{9,15},{10,... | collective-permute-start | bytes 1966088 | tf_op jit(solution)/shard_map/ppermute | solution.py:17
  71.1 2.0 %collective-permute-start = (bf16[320,1024]{1,0:T(8,128)(2,1)}, bf16[320,1024]{1,0:T(8,128)(2,1)}, u32[]{:S(2)}, u32[]{:S(2)}) collective-permute-start(bf16[320,1024]{1,0:T(8,128)(2,1)} %get-tuple-element.41), channel_id=1, source_target_pairs={{0,6},{1,7},{2,0},{3,1},{4,2},{5,3},{6,4},{7,5},{8,14},{9,15},{10,... | collective-permute-start | bytes 1966088 | tf_op jit(solution)/shard_map/ppermute | solution.py:17
  73.1 4.4 %shard_map.116.refs_6_ = f32[640,1024]{1,0:T(8,128)S(1)} custom-call(s32[1]{0:T(128)} %bitcast.11.refs_0_, bf16[640,1024]{1,0:T(8,128)(2,1)} %get-tuple-element.42.refs_1_, bf16[8192,1024]{1,0:T(8,128)(2,1)} %refs_6_.1), custom_call_target="tpu_custom_call" | custom-call | flops 1310720 | bytes 1024 | tf_op jit(solution)/shard_map/pallas_call | solution.py:94
  77.5 9.3 %collective-permute-done.3.refs_3_ = bf16[320,1024]{1,0:T(8,128)(2,1)S(1)} collective-permute-done((bf16[320,1024]{1,0:T(8,128)(2,1)}, bf16[320,1024]{1,0:T(8,128)(2,1)S(1)}, u32[]{:S(2)}, u32[]{:S(2)}) %collective-permute-start.3) | collective-permute-done | bytes 655392 | tf_op jit(solution)/shard_map/ppermute | solution.py:17
  86.8 9.6 %collective-permute-done.4.refs_4_ = bf16[640,1024]{1,0:T(8,128)(2,1)} collective-permute-done((bf16[640,1024]{1,0:T(8,128)(2,1)}, bf16[640,1024]{1,0:T(8,128)(2,1)}, u32[]{:S(2)}, u32[]{:S(2)}) %collective-permute-start.4) | collective-permute-done | bytes 1310752 | tf_op jit(solution)/shard_map/ppermute | solution.py:21
  96.4 1.9 %collective-permute-start.8 = (bf16[640,1024]{1,0:T(8,128)(2,1)}, bf16[640,1024]{1,0:T(8,128)(2,1)}, u32[]{:S(2)}, u32[]{:S(2)}) collective-permute-start(bf16[640,1024]{1,0:T(8,128)(2,1)} %collective-permute-done.4.refs_4_), channel_id=1, source_target_pairs={{0,2},{1,3},{2,4},{3,5},{4,6},{5,7},{6,0},{7,1},{8,10},{9,11},{10,... | collective-permute-start | bytes 3932168 | tf_op jit(solution)/shard_map/ppermute | solution.py:13
  98.4 0.8 collective-permute-done.refs_2_
  99.2 1.9 %collective-permute-start.1 = (bf16[320,1024]{1,0:T(8,128)(2,1)}, bf16[320,1024]{1,0:T(8,128)(2,1)}, u32[]{:S(2)}, u32[]{:S(2)}) collective-permute-start(bf16[320,1024]{1,0:T(8,128)(2,1)} %collective-permute-done.refs_2_), channel_id=1, source_target_pairs={{0,1},{1,0},{2,3},{3,2},{4,5},{5,4},{6,7},{7,6},{8,9},{9,8},{10,11... | collective-permute-start | bytes 1966088 | tf_op jit(solution)/shard_map/ppermute | solution.py:21
  101.1 2.4 %collective-permute-start.6 = (bf16[320,1024]{1,0:T(8,128)(2,1)S(1)}, bf16[320,1024]{1,0:T(8,128)(2,1)}, u32[]{:S(2)}, u32[]{:S(2)}) collective-permute-start(bf16[320,1024]{1,0:T(8,128)(2,1)S(1)} %collective-permute-done.3.refs_3_), channel_id=1, source_target_pairs={{0,6},{1,7},{2,0},{3,1},{4,2},{5,3},{6,4},{7,5},{8,14},{9,15},{10,... | collective-permute-start | bytes 1966088 | tf_op jit(solution)/shard_map/ppermute | solution.py:17
  103.5 0.1 pad_add_fusion.refs_0_
  103.5 0.0 collective-permute-done.2.refs_1_
  103.5 1.8 %collective-permute-start.9 = (bf16[320,1024]{1,0:T(8,128)(2,1)}, bf16[320,1024]{1,0:T(8,128)(2,1)}, u32[]{:S(2)}, u32[]{:S(2)}) collective-permute-start(bf16[320,1024]{1,0:T(8,128)(2,1)} %collective-permute-done.refs_2_), channel_id=1, source_target_pairs={{0,6},{1,7},{2,0},{3,1},{4,2},{5,3},{6,4},{7,5},{8,14},{9,15},{10,... | collective-permute-start | bytes 1966088 | tf_op jit(solution)/shard_map/ppermute | solution.py:17
  105.3 1.5 collective-permute-start.10
  106.8 8.1 %shard_map.117.refs_7_ = f32[640,1024]{1,0:T(8,128)S(1)} custom-call(s32[3]{0:T(128)S(1)} %pad_add_fusion.refs_0_, bf16[640,1024]{1,0:T(8,128)(2,1)} %collective-permute-done.2.refs_1_, bf16[320,1024]{1,0:T(8,128)(2,1)} %collective-permute-done.refs_2_, bf16[320,1024]{1,0:T(8,128)(2,1)S(1)} %collective-permute-done.3.refs_3_, ...), custom_call_target="tpu_custom_call" | custom-call | flops 3932160 | bytes 1024 | tf_op jit(solution)/shard_map/pallas_call | solution.py:94
  115.0 1.5 %copy-done.1 = f32[640,1024]{1,0:T(8,128)} copy-done((f32[640,1024]{1,0:T(8,128)}, f32[640,1024]{1,0:T(8,128)S(1)}, u32[]{:S(2)}) %copy-start.1) | copy-done | bytes 2621464
  116.4 2.2 %collective-permute-done.1.refs_4_ = bf16[320,1024]{1,0:T(8,128)(2,1)} collective-permute-done((bf16[320,1024]{1,0:T(8,128)(2,1)}, bf16[320,1024]{1,0:T(8,128)(2,1)}, u32[]{:S(2)}, u32[]{:S(2)}) %collective-permute-start.1) | collective-permute-done | bytes 655392 | tf_op jit(solution)/shard_map/ppermute | solution.py:21
  118.7 3.4 %collective-permute-start.5 = (bf16[320,1024]{1,0:T(8,128)(2,1)}, bf16[320,1024]{1,0:T(8,128)(2,1)S(1)}, u32[]{:S(2)}, u32[]{:S(2)}) collective-permute-start(bf16[320,1024]{1,0:T(8,128)(2,1)} %collective-permute-done.1.refs_4_), channel_id=1, source_target_pairs={{0,6},{1,7},{2,0},{3,1},{4,2},{5,3},{6,4},{7,5},{8,14},{9,15},{10,... | collective-permute-start | bytes 1966088 | tf_op jit(solution)/shard_map/ppermute | solution.py:17
  122.1 0.0 collective-permute-done.6.refs_3_
  122.1 0.8 collective-permute-start.7
  122.9 0.1 pad_add_fusion.1.refs_0_
  123.0 1.9 %constant_dynamic-slice_fusion.refs_2_ = bf16[1024,1024]{1,0:T(8,128)(2,1)S(1)} fusion(bf16[8192,1024]{1,0:T(8,128)(2,1)} %refs_6_.1, s32[]{:T(128)S(6)} %select_n.52), kind=kLoop, calls=%fused_computation.44 | loop fusion | bytes 4194308 | tf_op jit(solution)/shard_map/dynamic_slice | solution.py:281
  124.9 8.0 %collective-permute-done.9.refs_2_ = bf16[320,1024]{1,0:T(8,128)(2,1)} collective-permute-done((bf16[320,1024]{1,0:T(8,128)(2,1)}, bf16[320,1024]{1,0:T(8,128)(2,1)}, u32[]{:S(2)}, u32[]{:S(2)}) %collective-permute-start.9) | collective-permute-done | bytes 655392 | tf_op jit(solution)/shard_map/ppermute | solution.py:17
  132.9 0.0 collective-permute-done.10.refs_5_
  132.9 0.0 collective-permute-done.8.refs_1_
  132.9 8.3 %shard_map.118.refs_3_ = f32[640,1024]{1,0:T(8,128)S(1)} custom-call(s32[3]{0:T(128)S(1)} %pad_add_fusion.1.refs_0_, bf16[640,1024]{1,0:T(8,128)(2,1)} %collective-permute-done.8.refs_1_, bf16[320,1024]{1,0:T(8,128)(2,1)} %collective-permute-done.9.refs_2_, bf16[320,1024]{1,0:T(8,128)(2,1)} %collective-permute-done.6.refs_3_, ...), custom_call_target="tpu_custom_call" | custom-call | flops 3932160 | bytes 1024 | tf_op jit(solution)/shard_map/pallas_call | solution.py:94
  141.3 2.9 %collective-permute-done.5.refs_0_ = bf16[320,1024]{1,0:T(8,128)(2,1)S(1)} collective-permute-done((bf16[320,1024]{1,0:T(8,128)(2,1)}, bf16[320,1024]{1,0:T(8,128)(2,1)S(1)}, u32[]{:S(2)}, u32[]{:S(2)}) %collective-permute-start.5) | collective-permute-done | bytes 655392 | tf_op jit(solution)/shard_map/ppermute | solution.py:17
  144.2 0.0 collective-permute-done.7.refs_1_
  144.2 2.6 %shard_map.119 = (bf16[512,1024]{1,0:T(8,128)(2,1)}, bf16[32,4,1024]{2,1,0:T(4,128)(2,1)}) custom-call(bf16[320,1024]{1,0:T(8,128)(2,1)S(1)} %collective-permute-done.5.refs_0_, bf16[320,1024]{1,0:T(8,128)(2,1)S(1)} %collective-permute-done.7.refs_1_, bf16[1024,1024]{1,0:T(8,128)(2,1)S(1)} %constant_dynamic-slice_fusion.refs_2_, ...), custom_call_target="tpu_custom_call" | custom-call | flops 1310720 | bytes 1024 | tf_op jit(solution)/shard_map/pallas_call | solution.py:86
  (10 shorter events, 0.1 us)
Async XLA Ops:
  0.6 45.6 %copy-start = (bf16[32,4,4,256]{3,2,1,0:T(4,128)(2,1)S(1)}, bf16[32,4,4,256]{3,2,1,0:T(4,128)(2,1)}, u32[]{:S(2)}) copy-start(bf16[32,4,4,256]{3,2,1,0:T(4,128)(2,1)} %param.16) | copy-start | bytes 786436
  0.6 4.3 %copy-start.8 = (bf16[512,4,256]{2,1,0:T(4,128)(2,1)S(1)}, bf16[512,4,256]{2,1,0:T(4,128)(2,1)}, u32[]{:S(2)}) copy-start(bf16[512,4,256]{2,1,0:T(4,128)(2,1)} %param.12) | copy-start | bytes 3145732
  4.9 0.7 copy-start.4
  6.9 5.9 %copy-start.5 = (bf16[512,4,256]{2,1,0:T(4,128)(2,1)S(1)}, bf16[512,4,256]{2,1,0:T(4,128)(2,1)}, u32[]{:S(2)}) copy-start(bf16[512,4,256]{2,1,0:T(4,128)(2,1)} %param.11) | copy-start | bytes 3145732
  6.9 5.9 %copy-start.6 = (bf16[512,4,256]{2,1,0:T(4,128)(2,1)S(1)}, bf16[512,4,256]{2,1,0:T(4,128)(2,1)}, u32[]{:S(2)}) copy-start(bf16[512,4,256]{2,1,0:T(4,128)(2,1)} %param.10) | copy-start | bytes 3145732
  6.9 29.5 %all-to-all-start = ((bf16[16,208,256]{2,1,0:T(8,128)(2,1)}), bf16[16,208,256]{2,1,0:T(8,128)(2,1)}, u32[]{:S(2)}, u32[]{:S(2)}) async-start(bf16[16,208,256]{2,1,0:T(8,128)(2,1)} %shard_map.113), calls=%async_computation | async-start | bytes 3407872 | tf_op jit(solution)/shard_map/all_to_all | solution.py:324
  36.5 9.6 %copy-start.7 = (f32[4,4,32]{2,1,0:T(4,128)S(1)}, f32[4,4,32]{2,1,0:T(4,128)}, u32[]{:S(2)}) copy-start(f32[4,4,32]{2,1,0:T(4,128)} %param.18) | copy-start | bytes 6148
  41.7 18.1 %all-to-all-start.1 = ((bf16[16,96,256]{2,1,0:T(8,128)(2,1)}), bf16[16,96,256]{2,1,0:T(8,128)(2,1)}, u32[]{:S(2)}, u32[]{:S(2)}) async-start(bf16[16,96,256]{2,1,0:T(8,128)(2,1)} %shard_map.114), calls=%async_computation.1 | async-start | bytes 1572864 | tf_op jit(solution)/shard_map/all_to_all | solution.py:339
  59.8 1.0 copy-start.3
  64.2 32.2 %collective-permute-start.4 = (bf16[640,1024]{1,0:T(8,128)(2,1)}, bf16[640,1024]{1,0:T(8,128)(2,1)}, u32[]{:S(2)}, u32[]{:S(2)}) collective-permute-start(bf16[640,1024]{1,0:T(8,128)(2,1)} %get-tuple-element.42.refs_1_), channel_id=1, source_target_pairs={{0,1},{1,0},{2,3},{3,2},{4,5},{5,4},{6,7},{7,6},{8,9},{9,8},{10,11... | collective-permute-start | bytes 3932168 | tf_op jit(solution)/shard_map/ppermute | solution.py:21
  67.1 36.4 %collective-permute-start.2 = (bf16[640,1024]{1,0:T(8,128)(2,1)}, bf16[640,1024]{1,0:T(8,128)(2,1)}, u32[]{:S(2)}, u32[]{:S(2)}) collective-permute-start(bf16[640,1024]{1,0:T(8,128)(2,1)} %get-tuple-element.42.refs_1_), channel_id=1, source_target_pairs={{0,2},{1,3},{2,4},{3,5},{4,6},{5,7},{6,0},{7,1},{8,10},{9,11},{10,... | collective-permute-start | bytes 3932168 | tf_op jit(solution)/shard_map/ppermute | solution.py:13
  68.9 17.9 %collective-permute-start.3 = (bf16[320,1024]{1,0:T(8,128)(2,1)}, bf16[320,1024]{1,0:T(8,128)(2,1)S(1)}, u32[]{:S(2)}, u32[]{:S(2)}) collective-permute-start(bf16[320,1024]{1,0:T(8,128)(2,1)} %get-tuple-element.44), channel_id=1, source_target_pairs={{0,6},{1,7},{2,0},{3,1},{4,2},{5,3},{6,4},{7,5},{8,14},{9,15},{10,... | collective-permute-start | bytes 1966088 | tf_op jit(solution)/shard_map/ppermute | solution.py:17
  71.1 28.1 %collective-permute-start = (bf16[320,1024]{1,0:T(8,128)(2,1)}, bf16[320,1024]{1,0:T(8,128)(2,1)}, u32[]{:S(2)}, u32[]{:S(2)}) collective-permute-start(bf16[320,1024]{1,0:T(8,128)(2,1)} %get-tuple-element.41), channel_id=1, source_target_pairs={{0,6},{1,7},{2,0},{3,1},{4,2},{5,3},{6,4},{7,5},{8,14},{9,15},{10,... | collective-permute-start | bytes 1966088 | tf_op jit(solution)/shard_map/ppermute | solution.py:17
  96.4 36.5 %collective-permute-start.8 = (bf16[640,1024]{1,0:T(8,128)(2,1)}, bf16[640,1024]{1,0:T(8,128)(2,1)}, u32[]{:S(2)}, u32[]{:S(2)}) collective-permute-start(bf16[640,1024]{1,0:T(8,128)(2,1)} %collective-permute-done.4.refs_4_), channel_id=1, source_target_pairs={{0,2},{1,3},{2,4},{3,5},{4,6},{5,7},{6,0},{7,1},{8,10},{9,11},{10,... | collective-permute-start | bytes 3932168 | tf_op jit(solution)/shard_map/ppermute | solution.py:13
  99.2 19.5 %collective-permute-start.1 = (bf16[320,1024]{1,0:T(8,128)(2,1)}, bf16[320,1024]{1,0:T(8,128)(2,1)}, u32[]{:S(2)}, u32[]{:S(2)}) collective-permute-start(bf16[320,1024]{1,0:T(8,128)(2,1)} %collective-permute-done.refs_2_), channel_id=1, source_target_pairs={{0,1},{1,0},{2,3},{3,2},{4,5},{5,4},{6,7},{7,6},{8,9},{9,8},{10,11... | collective-permute-start | bytes 1966088 | tf_op jit(solution)/shard_map/ppermute | solution.py:21
  101.1 21.0 %collective-permute-start.6 = (bf16[320,1024]{1,0:T(8,128)(2,1)S(1)}, bf16[320,1024]{1,0:T(8,128)(2,1)}, u32[]{:S(2)}, u32[]{:S(2)}) collective-permute-start(bf16[320,1024]{1,0:T(8,128)(2,1)S(1)} %collective-permute-done.3.refs_3_), channel_id=1, source_target_pairs={{0,6},{1,7},{2,0},{3,1},{4,2},{5,3},{6,4},{7,5},{8,14},{9,15},{10,... | collective-permute-start | bytes 1966088 | tf_op jit(solution)/shard_map/ppermute | solution.py:17
  103.5 29.4 %collective-permute-start.9 = (bf16[320,1024]{1,0:T(8,128)(2,1)}, bf16[320,1024]{1,0:T(8,128)(2,1)}, u32[]{:S(2)}, u32[]{:S(2)}) collective-permute-start(bf16[320,1024]{1,0:T(8,128)(2,1)} %collective-permute-done.refs_2_), channel_id=1, source_target_pairs={{0,6},{1,7},{2,0},{3,1},{4,2},{5,3},{6,4},{7,5},{8,14},{9,15},{10,... | collective-permute-start | bytes 1966088 | tf_op jit(solution)/shard_map/ppermute | solution.py:17
  105.3 27.6 %collective-permute-start.10 = (bf16[320,1024]{1,0:T(8,128)(2,1)S(1)}, bf16[320,1024]{1,0:T(8,128)(2,1)}, u32[]{:S(2)}, u32[]{:S(2)}) collective-permute-start(bf16[320,1024]{1,0:T(8,128)(2,1)S(1)} %collective-permute-done.3.refs_3_), channel_id=1, source_target_pairs={{0,1},{1,0},{2,3},{3,2},{4,5},{5,4},{6,7},{7,6},{8,9},{9,8},{10,11... | collective-permute-start | bytes 1966088 | tf_op jit(solution)/shard_map/ppermute | solution.py:21
  114.9 1.5 %copy-start.1 = (f32[640,1024]{1,0:T(8,128)}, f32[640,1024]{1,0:T(8,128)S(1)}, u32[]{:S(2)}) copy-start(f32[640,1024]{1,0:T(8,128)S(1)} %shard_map.117.refs_7_) | copy-start | bytes 7864324
  118.7 25.5 %collective-permute-start.5 = (bf16[320,1024]{1,0:T(8,128)(2,1)}, bf16[320,1024]{1,0:T(8,128)(2,1)S(1)}, u32[]{:S(2)}, u32[]{:S(2)}) collective-permute-start(bf16[320,1024]{1,0:T(8,128)(2,1)} %collective-permute-done.1.refs_4_), channel_id=1, source_target_pairs={{0,6},{1,7},{2,0},{3,1},{4,2},{5,3},{6,4},{7,5},{8,14},{9,15},{10,... | collective-permute-start | bytes 1966088 | tf_op jit(solution)/shard_map/ppermute | solution.py:17
  122.1 22.0 %collective-permute-start.7 = (bf16[320,1024]{1,0:T(8,128)(2,1)}, bf16[320,1024]{1,0:T(8,128)(2,1)S(1)}, u32[]{:S(2)}, u32[]{:S(2)}) collective-permute-start(bf16[320,1024]{1,0:T(8,128)(2,1)} %collective-permute-done.6.refs_3_), channel_id=1, source_target_pairs={{0,1},{1,0},{2,3},{3,2},{4,5},{5,4},{6,7},{7,6},{8,9},{9,8},{10,11... | collective-permute-start | bytes 1966088 | tf_op jit(solution)/shard_map/ppermute | solution.py:21
  123.0 9.9 %copy-start.2 = (f32[640,1024]{1,0:T(8,128)S(1)}, f32[640,1024]{1,0:T(8,128)}, u32[]{:S(2)}) copy-start(f32[640,1024]{1,0:T(8,128)} %copy-done.1) | copy-start | bytes 7864324

commit v8 on v7

--- a/solution.py
+++ b/solution.py
@@ -126,7 +126,7 @@
         sections = jnp.broadcast_to(n_ref[...].astype(F32), (8, rows)).astype(BF)
         sections = jnp.dot(sections, mine.astype(BF), preferred_element_type=F32)[:1]
         sections = jnp.concatenate([sections, jnp.zeros((1, dim - slots), F32)], axis=1)
-        line = lax.broadcasted_iota(jnp.int32, (16, dim), 0)
+        line = lax.broadcasted_iota(jnp.int32, (8, dim), 0)
         for h in range(heads):
             header = jnp.where(line == 3, sections, 0.0)
             for i in range(3):
@@ -135,14 +135,14 @@
             for k in range(per_head):
                 c = h * per_head + k
                 o_ref[c, :slice_rows, :] = s_ref[h, k * slice_rows : (k + 1) * slice_rows, :]
-                o_ref[c, slice_rows : slice_rows + 16, :] = header
-                o_ref[c, slice_rows + 16 :, :] = q_ref[h]
+                o_ref[c, slice_rows + slots :, :] = header
+                o_ref[c, slice_rows : slice_rows + slots, :] = q_ref[h]
 
     return pl.pallas_call(
         body,
         in_specs=[WHOLE] * 4,
         out_specs=WHOLE,
-        out_shape=jax.ShapeDtypeStruct((count, slice_rows + 16 + slots, dim), BF),
+        out_shape=jax.ShapeDtypeStruct((count, slice_rows + slots + 8, dim), BF),
         compiler_params=pltpu.CompilerParams(vmem_limit_bytes=12 << 20),
         cost_estimate=pl.CostEstimate(flops=0, bytes_accessed=3 << 20, transcendentals=0),
     )(own_state, parts, named, queries)
@@ -150,30 +150,41 @@
 
 def scan_and_read(got, slice_rows, slots):
     sections, _, dim = got.shape
-    head_rows, half = got.shape[1] - slice_rows - slots, slice_rows // 2
-
-    def body(got_ref, out_ref, ends):
+    half = slice_rows // 2
+
+    def body(got_ref, out_ref, states, asked_held, heads_held, ends, held, moved):
+        into = ((states, 0), (heads_held, slice_rows + slots), (asked_held, slice_rows))
+        arrive = [
+            pltpu.make_async_copy(
+                got_ref.at[:, pl.ds(first, to.shape[1]), :], to, moved.at[i]
+            )
+            for i, (to, first) in enumerate(into)
+        ]
+        for copy in arrive:
+            copy.start()
+        arrive[0].wait()
+        arrive[1].wait()
         state = jnp.zeros((slice_rows, dim), F32)
         for c in range(sections):
-            out_ref[c, :slice_rows, :] = state.astype(BF)
-            header = got_ref[c, slice_rows : slice_rows + 16, :].astype(F32)
+            held[c, :slice_rows, :] = state.astype(BF)
+            header = heads_held[c].astype(F32)
             factor = header[0:1] + header[1:2] + header[2:3]
-            state = factor * state + got_ref[c, :slice_rows, :].astype(F32)
+            state = factor * state + states[c].astype(F32)
             ends[c * slice_rows : (c + 1) * slice_rows, :] = state.astype(BF)
-
-        @pl.loop(0, sections // 2)
-        def _(p):
-            asked, named = [], []
-            for c in (2 * p, 2 * p + 1):
-                asked.append(got_ref[c, slice_rows + head_rows :, :])
-                header = got_ref[c, slice_rows : slice_rows + 16, :].astype(F32)
-                named.append(header[3:4, :slots])
-            asked, named = jnp.concatenate(asked, axis=0), jnp.concatenate(named, axis=1)
+        top = pl.ds(0, slice_rows)
+        leave = [pltpu.make_async_copy(held.at[:, top, :], out_ref.at[:, top, :], moved.at[3])]
+        leave[0].start()
+        arrive[2].wait()
+        for p in range(sections // 2):
+            pair = pl.ds(2 * p, 2)
+            rows = asked_held[2 * p : 2 * p + 2].reshape(2 * slots, dim)
+            named = [heads_held[2 * p + k].astype(F32)[3:4, :slots] for k in range(2)]
+            named = jnp.concatenate(named, axis=1)
             total = jnp.zeros((slice_rows, 2 * slots), F32)
             for j in range(0, sections, 4):
                 reads = lax.dot_general(
                     ends[j * slice_rows : (j + 4) * slice_rows, :],
-                    asked,
+                    rows,
                     NT,
                     preferred_element_type=F32,
                 )
@@ -183,15 +194,33 @@
             total = total.astype(BF)
             for k in range(2):
                 mine = total[:, k * slots : (k + 1) * slots]
-                out_ref[2 * p + k, slice_rows:, :slots] = mine[:half]
-                out_ref[2 * p + k, slice_rows:, slots:] = mine[half:]
-
+                held[2 * p + k, slice_rows:, :slots] = mine[:half]
+                held[2 * p + k, slice_rows:, slots:] = mine[half:]
+            below = pl.ds(slice_rows, half)
+            leave.append(
+                pltpu.make_async_copy(
+                    held.at[pair, below, :], out_ref.at[pair, below, :], moved.at[4 + p]
+                )
+            )
+            leave[-1].start()
+        for copy in leave:
+            copy.wait()
+
+    shape = (sections, slice_rows + half, dim)
+    head_rows = got.shape[1] - slice_rows - slots
     return pl.pallas_call(
         body,
-        in_specs=[WHOLE],
-        out_specs=WHOLE,
-        out_shape=jax.ShapeDtypeStruct((sections, slice_rows + half, dim), BF),
-        scratch_shapes=[pltpu.VMEM((sections * slice_rows, dim), BF)],
+        in_specs=[pl.BlockSpec(memory_space=pl.ANY)],
+        out_specs=pl.BlockSpec(memory_space=pl.ANY),
+        out_shape=jax.ShapeDtypeStruct(shape, BF),
+        scratch_shapes=[
+            pltpu.VMEM((sections, slice_rows, dim), BF),
+            pltpu.VMEM((sections, slots, dim), BF),
+            pltpu.VMEM((sections, head_rows, dim), BF),
+            pltpu.VMEM((sections * slice_rows, dim), BF),
+            pltpu.VMEM(shape, BF),
+            pltpu.SemaphoreType.DMA((4 + sections // 2,)),
+        ],
         compiler_params=pltpu.CompilerParams(vmem_limit_bytes=58 << 20),
         cost_estimate=pl.CostEstimate(
             flops=2 * sections * slots * sections * slice_rows * dim,

time: 147 us -> 145 us (0.986)
  Pallas kernels: 33.5 us -> 31.7 us
    pallas_call x1, Pallas kernels: 5.25 us -> 3.51 us  [scan_and_read(): pl.pallas_call(body, in_specs=[pl.BlockSpec(memory_space=pl.ANY)], out_sp...]
where the time goes in v8:
time: 145 us; the launch traced here: 144 us
  waiting for transfers between devices  56.8 us (39%)
  starting transfers between devices  32.6 us (22%)
  Pallas kernels  31.7 us (22%)
  local copies, waits for them, and re-layouts  11.3 us (8%)
  matrix products  8.64 us (6%)
  other arithmetic  2.39 us (2%)
    all_to_all x2, waiting for transfers between devices, shards(): got = lax.all_to_all(sent, 'ctx', 0, 0)  23.9 us
    ppermute x5, waiting for transfers between devices, down(): return lax.ppermute(a, 'head', [(h, (h - 2) % 8) for h in range(8)])  21 us
    pallas_call x3, Pallas kernels, project(): pl.pallas_call(body, in_specs=[pl.BlockSpec(memory_space=pltpu.SMEM)] + [...  20.9 us
    ppermute x4, waiting for transfers between devices, across(): return lax.ppermute(a, 'head', [(h, h ^ 1) for h in range(8)])  11.9 us
    ppermute x5, starting transfers between devices, down(): return lax.ppermute(a, 'head', [(h, (h - 2) % 8) for h in range(8)])  11.7 us
    all_to_all x2, starting transfers between devices, shards(): got = lax.all_to_all(sent, 'ctx', 0, 0)  10.1 us
    ppermute x4, starting transfers between devices, across(): return lax.ppermute(a, 'head', [(h, h ^ 1) for h in range(8)])  6.97 us
    unnamed x20, local copies, waits for them, and re-layouts  4.92 us
  transfers between devices with their start and end apart: 13, of which 8 were waited for; matrix products, arithmetic and copies ran while one was open for 10% of the time, Pallas kernels for 14%

profile of v8, /device:TPU:0, one launch (start us, length us, event | category | flops | bytes accessed | tf_op | source)
XLA Modules:
  0.0 144.3 jit_solution(4612889814680931218)
XLA Ops:
  0.6 0.0 copy-start
  0.6 0.0 copy-start.8
  0.7 1.1 fusion.9
  1.7 0.2 fusion.24
  1.9 0.1 subtract_exponential_fusion
  2.0 0.2 copy.24
  2.2 1.0 copy.66
  3.2 1.8 %multiply_convert_fusion.1 = bf16[512,4,256]{2,1,0:T(4,128)(2,1)S(1)} fusion(bf16[512,4,256]{2,1,0:T(4,128)(2,1)} %param.11, f32[512,4]{1,0:T(8,128)S(1)} %copy.24), kind=kLoop, calls=%fused_computation.1 | loop fusion | flops 1572864 | bytes 2105344 | tf_op jit(solution)/shard_map/convert_element_type | solution.py:344
  4.9 0.0 copy-done.8
  4.9 0.0 copy-start.4
  4.9 0.6 fusion.1.s_ref
  5.5 0.1 pad_maximum_fusion.1.p_ref
  5.6 0.0 copy-done.4
  5.6 1.3 shard_map.113
  6.9 5.8 %all-to-all-start = ((bf16[16,200,256]{2,1,0:T(8,128)(2,1)}), bf16[16,200,256]{2,1,0:T(8,128)(2,1)}, u32[]{:S(2)}, u32[]{:S(2)}) async-start(bf16[16,200,256]{2,1,0:T(8,128)(2,1)} %shard_map.113), calls=%async_computation | async-start | bytes 3276800 | tf_op jit(solution)/shard_map/all_to_all | solution.py:353
  12.7 0.1 iota_compare_fusion
  12.8 0.0 copy-done.5
  12.8 0.0 copy-done.6
  12.8 4.7 %fusion = f32[4,256,512]{2,1,0:T(8,128)} fusion(f32[4,512]{1,0:T(4,128)S(1)} %bitcast.35, pred[512,512]{1,0:T(8,128)(4,1)S(1)} %iota_compare_fusion, bf16[512,4,256]{2,1,0:T(4,128)(2,1)S(1)} %copy-done.5, bf16[512,4,256]{2,1,0:T(4,128)(2,1)S(1)} %copy-done.6, bf16[512,4,256]{2,1,0:T(4,128)(2,1)} %param.12), kind=kOutput, calls=%fused_computation.2 | convolution fusion | flops 1078984704 | bytes 5513216 | tf_op jit(solution)/shard_map/hnm,mhe->nhe/dot_general | solution.py:362
  17.5 1.9 %copy.42.in_ref = f32[512,1024]{1,0:T(8,128)S(1)} copy(f32[512,1024]{0,1:T(8,128)} %bitcast.38) | data formatting | bytes 4194304 | tf_op jit(solution)/shard_map/reshape | solution.py:363
  19.5 1.4 %copy.43 = bf16[64,8,4,256]{3,1,2,0:T(8,128)(2,1)S(1)} copy(bf16[64,8,4,256]{3,2,1,0:T(4,128)(2,1)} %bitcast.40) | data formatting | bytes 2097152
  20.9 14.8 %all-to-all-done.got_ref = bf16[16,200,256]{2,1,0:T(8,128)(2,1)} async-done(((bf16[16,200,256]{2,1,0:T(8,128)(2,1)}), bf16[16,200,256]{2,1,0:T(8,128)(2,1)}, u32[]{:S(2)}, u32[]{:S(2)}) %all-to-all-start) | async-done | bytes 1638432 | tf_op jit(solution)/shard_map/all_to_all | solution.py:353
  35.7 3.5 %shard_map.114 = bf16[16,96,256]{2,1,0:T(8,128)(2,1)} custom-call(bf16[16,200,256]{2,1,0:T(8,128)(2,1)} %all-to-all-done.got_ref), custom_call_target="tpu_custom_call" | custom-call | flops 1073741824 | bytes 6291456 | tf_op jit(solution)/shard_map/pallas_call | solution.py:211
  39.2 4.3 %all-to-all-start.1 = ((bf16[16,96,256]{2,1,0:T(8,128)(2,1)}), bf16[16,96,256]{2,1,0:T(8,128)(2,1)}, u32[]{:S(2)}, u32[]{:S(2)}) async-start(bf16[16,96,256]{2,1,0:T(8,128)(2,1)} %shard_map.114), calls=%async_computation.1 | async-start | bytes 1572864 | tf_op jit(solution)/shard_map/all_to_all | solution.py:368
  43.6 0.0 copy-done.7
  43.6 0.1 copy.31
  43.7 0.0 copy-done
  43.8 2.3 %convolution_bitcast_fusion = f32[32,4,4,256]{3,1,2,0:T(4,128)} fusion(bf16[32,4,4,256]{3,2,1,0:T(4,128)(2,1)S(1)} %copy-done, bf16[32,4,4,256]{3,2,1,0:T(4,128)(2,1)} %param.15, bf16[32,4,4,256]{3,2,1,0:T(4,128)(2,1)} %param.17, f32[32,4,4]{2,1,0:T(4,128)S(1)} %copy.31, pred[4,4]{1,0:T(4,128)(4,1)S(1)} %iota_compare_fusion.3), kind=kOutput, calls=%fused_computation.5 | convolution fusion | flops 2105344 | bytes 1312784 | tf_op jit(solution)/shard_map/rhtu,ruhe->rthe/dot_general | solution.py:382
  46.1 1.2 copy.34
  47.2 0.9 copy.44
  48.1 0.1 copy.35
  48.3 9.1 %all-to-all-done.1.got_ref = bf16[16,96,256]{2,1,0:T(8,128)(2,1)} async-done(((bf16[16,96,256]{2,1,0:T(8,128)(2,1)}), bf16[16,96,256]{2,1,0:T(8,128)(2,1)}, u32[]{:S(2)}, u32[]{:S(2)}) %all-to-all-start.1) | async-done | bytes 786464 | tf_op jit(solution)/shard_map/all_to_all | solution.py:368
  57.3 1.0 copy-done.3
  58.4 3.4 %shard_map.115 = (bf16[640,1024]{1,0:T(8,128)(2,1)}, bf16[320,1024]{1,0:T(8,128)(2,1)}, bf16[320,1024]{1,0:T(8,128)(2,1)}) custom-call(bf16[512,1024]{1,0:T(8,128)(2,1)S(1)} %bitcast.30, f32[512,1024]{1,0:T(8,128)S(1)} %copy.42.in_ref, f32[4,512]{1,0:T(4,128)S(1)} %bitcast.36, bf16[16,96,256]{2,1,0:T(8,128)(2,1)} %all-to-all-done.1.got_ref, ...), custom_call_target="tpu_custom_call" | custom-call | flops 268435456 | bytes 6291456 | tf_op jit(solution)/shard_map/pallas_call | solution.py:268
  61.8 2.8 %collective-permute-start.4 = (bf16[640,1024]{1,0:T(8,128)(2,1)}, bf16[640,1024]{1,0:T(8,128)(2,1)}, u32[]{:S(2)}, u32[]{:S(2)}) collective-permute-start(bf16[640,1024]{1,0:T(8,128)(2,1)} %get-tuple-element.42.refs_1_), channel_id=1, source_target_pairs={{0,1},{1,0},{2,3},{3,2},{4,5},{5,4},{6,7},{7,6},{8,9},{9,8},{10,11... | collective-permute-start | bytes 3932168 | tf_op jit(solution)/shard_map/ppermute | solution.py:21
  64.6 1.9 %collective-permute-start.2 = (bf16[640,1024]{1,0:T(8,128)(2,1)}, bf16[640,1024]{1,0:T(8,128)(2,1)}, u32[]{:S(2)}, u32[]{:S(2)}) collective-permute-start(bf16[640,1024]{1,0:T(8,128)(2,1)} %get-tuple-element.42.refs_1_), channel_id=1, source_target_pairs={{0,2},{1,3},{2,4},{3,5},{4,6},{5,7},{6,0},{7,1},{8,10},{9,11},{10,... | collective-permute-start | bytes 3932168 | tf_op jit(solution)/shard_map/ppermute | solution.py:13
  66.5 2.1 %collective-permute-start.3 = (bf16[320,1024]{1,0:T(8,128)(2,1)}, bf16[320,1024]{1,0:T(8,128)(2,1)S(1)}, u32[]{:S(2)}, u32[]{:S(2)}) collective-permute-start(bf16[320,1024]{1,0:T(8,128)(2,1)} %get-tuple-element.44), channel_id=1, source_target_pairs={{0,6},{1,7},{2,0},{3,1},{4,2},{5,3},{6,4},{7,5},{8,14},{9,15},{10,... | collective-permute-start | bytes 1966088 | tf_op jit(solution)/shard_map/ppermute | solution.py:17
  68.6 2.0 %collective-permute-start = (bf16[320,1024]{1,0:T(8,128)(2,1)}, bf16[320,1024]{1,0:T(8,128)(2,1)}, u32[]{:S(2)}, u32[]{:S(2)}) collective-permute-start(bf16[320,1024]{1,0:T(8,128)(2,1)} %get-tuple-element.41), channel_id=1, source_target_pairs={{0,6},{1,7},{2,0},{3,1},{4,2},{5,3},{6,4},{7,5},{8,14},{9,15},{10,... | collective-permute-start | bytes 1966088 | tf_op jit(solution)/shard_map/ppermute | solution.py:17
  70.6 4.4 %shard_map.116.refs_6_ = f32[640,1024]{1,0:T(8,128)S(1)} custom-call(s32[1]{0:T(128)} %bitcast.11.refs_0_, bf16[640,1024]{1,0:T(8,128)(2,1)} %get-tuple-element.42.refs_1_, bf16[8192,1024]{1,0:T(8,128)(2,1)} %refs_6_.1), custom_call_target="tpu_custom_call" | custom-call | flops 1310720 | bytes 1024 | tf_op jit(solution)/shard_map/pallas_call | solution.py:94
  75.1 9.3 %collective-permute-done.3.refs_3_ = bf16[320,1024]{1,0:T(8,128)(2,1)S(1)} collective-permute-done((bf16[320,1024]{1,0:T(8,128)(2,1)}, bf16[320,1024]{1,0:T(8,128)(2,1)S(1)}, u32[]{:S(2)}, u32[]{:S(2)}) %collective-permute-start.3) | collective-permute-done | bytes 655392 | tf_op jit(solution)/shard_map/ppermute | solution.py:17
  84.4 9.6 %collective-permute-done.4.refs_4_ = bf16[640,1024]{1,0:T(8,128)(2,1)} collective-permute-done((bf16[640,1024]{1,0:T(8,128)(2,1)}, bf16[640,1024]{1,0:T(8,128)(2,1)}, u32[]{:S(2)}, u32[]{:S(2)}) %collective-permute-start.4) | collective-permute-done | bytes 1310752 | tf_op jit(solution)/shard_map/ppermute | solution.py:21
  94.0 1.9 %collective-permute-start.8 = (bf16[640,1024]{1,0:T(8,128)(2,1)}, bf16[640,1024]{1,0:T(8,128)(2,1)}, u32[]{:S(2)}, u32[]{:S(2)}) collective-permute-start(bf16[640,1024]{1,0:T(8,128)(2,1)} %collective-permute-done.4.refs_4_), channel_id=1, source_target_pairs={{0,2},{1,3},{2,4},{3,5},{4,6},{5,7},{6,0},{7,1},{8,10},{9,11},{10,... | collective-permute-start | bytes 3932168 | tf_op jit(solution)/shard_map/ppermute | solution.py:13
  95.9 0.8 collective-permute-done.refs_2_
  96.8 1.9 %collective-permute-start.1 = (bf16[320,1024]{1,0:T(8,128)(2,1)}, bf16[320,1024]{1,0:T(8,128)(2,1)}, u32[]{:S(2)}, u32[]{:S(2)}) collective-permute-start(bf16[320,1024]{1,0:T(8,128)(2,1)} %collective-permute-done.refs_2_), channel_id=1, source_target_pairs={{0,1},{1,0},{2,3},{3,2},{4,5},{5,4},{6,7},{7,6},{8,9},{9,8},{10,11... | collective-permute-start | bytes 1966088 | tf_op jit(solution)/shard_map/ppermute | solution.py:21
  98.6 2.3 %collective-permute-start.6 = (bf16[320,1024]{1,0:T(8,128)(2,1)S(1)}, bf16[320,1024]{1,0:T(8,128)(2,1)}, u32[]{:S(2)}, u32[]{:S(2)}) collective-permute-start(bf16[320,1024]{1,0:T(8,128)(2,1)S(1)} %collective-permute-done.3.refs_3_), channel_id=1, source_target_pairs={{0,6},{1,7},{2,0},{3,1},{4,2},{5,3},{6,4},{7,5},{8,14},{9,15},{10,... | collective-permute-start | bytes 1966088 | tf_op jit(solution)/shard_map/ppermute | solution.py:17
  101.0 0.1 pad_add_fusion.refs_0_
  101.1 0.0 collective-permute-done.2.refs_1_
  101.1 1.8 %collective-permute-start.9 = (bf16[320,1024]{1,0:T(8,128)(2,1)}, bf16[320,1024]{1,0:T(8,128)(2,1)}, u32[]{:S(2)}, u32[]{:S(2)}) collective-permute-start(bf16[320,1024]{1,0:T(8,128)(2,1)} %collective-permute-done.refs_2_), channel_id=1, source_target_pairs={{0,6},{1,7},{2,0},{3,1},{4,2},{5,3},{6,4},{7,5},{8,14},{9,15},{10,... | collective-permute-start | bytes 1966088 | tf_op jit(solution)/shard_map/ppermute | solution.py:17
  102.9 1.5 %collective-permute-start.10 = (bf16[320,1024]{1,0:T(8,128)(2,1)S(1)}, bf16[320,1024]{1,0:T(8,128)(2,1)}, u32[]{:S(2)}, u32[]{:S(2)}) collective-permute-start(bf16[320,1024]{1,0:T(8,128)(2,1)S(1)} %collective-permute-done.3.refs_3_), channel_id=1, source_target_pairs={{0,1},{1,0},{2,3},{3,2},{4,5},{5,4},{6,7},{7,6},{8,9},{9,8},{10,11... | collective-permute-start | bytes 1966088 | tf_op jit(solution)/shard_map/ppermute | solution.py:21
  104.3 8.1 %shard_map.117.refs_7_ = f32[640,1024]{1,0:T(8,128)S(1)} custom-call(s32[3]{0:T(128)S(1)} %pad_add_fusion.refs_0_, bf16[640,1024]{1,0:T(8,128)(2,1)} %collective-permute-done.2.refs_1_, bf16[320,1024]{1,0:T(8,128)(2,1)} %collective-permute-done.refs_2_, bf16[320,1024]{1,0:T(8,128)(2,1)S(1)} %collective-permute-done.3.refs_3_, ...), custom_call_target="tpu_custom_call" | custom-call | flops 3932160 | bytes 1024 | tf_op jit(solution)/shard_map/pallas_call | solution.py:94
  112.5 1.5 %copy-done.1 = f32[640,1024]{1,0:T(8,128)} copy-done((f32[640,1024]{1,0:T(8,128)}, f32[640,1024]{1,0:T(8,128)S(1)}, u32[]{:S(2)}) %copy-start.1) | copy-done | bytes 2621464
  114.0 2.3 %collective-permute-done.1.refs_4_ = bf16[320,1024]{1,0:T(8,128)(2,1)} collective-permute-done((bf16[320,1024]{1,0:T(8,128)(2,1)}, bf16[320,1024]{1,0:T(8,128)(2,1)}, u32[]{:S(2)}, u32[]{:S(2)}) %collective-permute-start.1) | collective-permute-done | bytes 655392 | tf_op jit(solution)/shard_map/ppermute | solution.py:21
  116.2 3.4 %collective-permute-start.5 = (bf16[320,1024]{1,0:T(8,128)(2,1)}, bf16[320,1024]{1,0:T(8,128)(2,1)S(1)}, u32[]{:S(2)}, u32[]{:S(2)}) collective-permute-start(bf16[320,1024]{1,0:T(8,128)(2,1)} %collective-permute-done.1.refs_4_), channel_id=1, source_target_pairs={{0,6},{1,7},{2,0},{3,1},{4,2},{5,3},{6,4},{7,5},{8,14},{9,15},{10,... | collective-permute-start | bytes 1966088 | tf_op jit(solution)/shard_map/ppermute | solution.py:17
  119.7 0.0 collective-permute-done.6.refs_3_
  119.7 0.8 collective-permute-start.7
  120.5 0.1 pad_add_fusion.1.refs_0_
  120.6 1.9 %constant_dynamic-slice_fusion.refs_2_ = bf16[1024,1024]{1,0:T(8,128)(2,1)S(1)} fusion(bf16[8192,1024]{1,0:T(8,128)(2,1)} %refs_6_.1, s32[]{:T(128)S(6)} %select_n.52), kind=kLoop, calls=%fused_computation.44 | loop fusion | bytes 4194308 | tf_op jit(solution)/shard_map/dynamic_slice | solution.py:310
  122.5 8.0 %collective-permute-done.9.refs_2_ = bf16[320,1024]{1,0:T(8,128)(2,1)} collective-permute-done((bf16[320,1024]{1,0:T(8,128)(2,1)}, bf16[320,1024]{1,0:T(8,128)(2,1)}, u32[]{:S(2)}, u32[]{:S(2)}) %collective-permute-start.9) | collective-permute-done | bytes 655392 | tf_op jit(solution)/shard_map/ppermute | solution.py:17
  130.5 0.0 collective-permute-done.10.refs_5_
  130.5 0.0 collective-permute-done.8.refs_1_
  130.5 8.3 %shard_map.118.refs_3_ = f32[640,1024]{1,0:T(8,128)S(1)} custom-call(s32[3]{0:T(128)S(1)} %pad_add_fusion.1.refs_0_, bf16[640,1024]{1,0:T(8,128)(2,1)} %collective-permute-done.8.refs_1_, bf16[320,1024]{1,0:T(8,128)(2,1)} %collective-permute-done.9.refs_2_, bf16[320,1024]{1,0:T(8,128)(2,1)} %collective-permute-done.6.refs_3_, ...), custom_call_target="tpu_custom_call" | custom-call | flops 3932160 | bytes 1024 | tf_op jit(solution)/shard_map/pallas_call | solution.py:94
  138.8 2.9 %collective-permute-done.5.refs_0_ = bf16[320,1024]{1,0:T(8,128)(2,1)S(1)} collective-permute-done((bf16[320,1024]{1,0:T(8,128)(2,1)}, bf16[320,1024]{1,0:T(8,128)(2,1)S(1)}, u32[]{:S(2)}, u32[]{:S(2)}) %collective-permute-start.5) | collective-permute-done | bytes 655392 | tf_op jit(solution)/shard_map/ppermute | solution.py:17
  141.7 0.0 collective-permute-done.7.refs_1_
  141.7 2.6 %shard_map.119 = (bf16[512,1024]{1,0:T(8,128)(2,1)}, bf16[32,4,1024]{2,1,0:T(4,128)(2,1)}) custom-call(bf16[320,1024]{1,0:T(8,128)(2,1)S(1)} %collective-permute-done.5.refs_0_, bf16[320,1024]{1,0:T(8,128)(2,1)S(1)} %collective-permute-done.7.refs_1_, bf16[1024,1024]{1,0:T(8,128)(2,1)S(1)} %constant_dynamic-slice_fusion.refs_2_, ...), custom_call_target="tpu_custom_call" | custom-call | flops 1310720 | bytes 1024 | tf_op jit(solution)/shard_map/pallas_call | solution.py:86
  (10 shorter events, 0.1 us)
Async XLA Ops:
  0.6 43.1 %copy-start = (bf16[32,4,4,256]{3,2,1,0:T(4,128)(2,1)S(1)}, bf16[32,4,4,256]{3,2,1,0:T(4,128)(2,1)}, u32[]{:S(2)}) copy-start(bf16[32,4,4,256]{3,2,1,0:T(4,128)(2,1)} %param.16) | copy-start | bytes 786436
  0.6 4.3 %copy-start.8 = (bf16[512,4,256]{2,1,0:T(4,128)(2,1)S(1)}, bf16[512,4,256]{2,1,0:T(4,128)(2,1)}, u32[]{:S(2)}) copy-start(bf16[512,4,256]{2,1,0:T(4,128)(2,1)} %param.12) | copy-start | bytes 3145732
  4.9 0.7 copy-start.4
  6.9 5.9 %copy-start.5 = (bf16[512,4,256]{2,1,0:T(4,128)(2,1)S(1)}, bf16[512,4,256]{2,1,0:T(4,128)(2,1)}, u32[]{:S(2)}) copy-start(bf16[512,4,256]{2,1,0:T(4,128)(2,1)} %param.11) | copy-start | bytes 3145732
  6.9 5.9 %copy-start.6 = (bf16[512,4,256]{2,1,0:T(4,128)(2,1)S(1)}, bf16[512,4,256]{2,1,0:T(4,128)(2,1)}, u32[]{:S(2)}) copy-start(bf16[512,4,256]{2,1,0:T(4,128)(2,1)} %param.10) | copy-start | bytes 3145732
  6.9 28.8 %all-to-all-start = ((bf16[16,200,256]{2,1,0:T(8,128)(2,1)}), bf16[16,200,256]{2,1,0:T(8,128)(2,1)}, u32[]{:S(2)}, u32[]{:S(2)}) async-start(bf16[16,200,256]{2,1,0:T(8,128)(2,1)} %shard_map.113), calls=%async_computation | async-start | bytes 3276800 | tf_op jit(solution)/shard_map/all_to_all | solution.py:353
  35.7 7.8 %copy-start.7 = (f32[4,4,32]{2,1,0:T(4,128)S(1)}, f32[4,4,32]{2,1,0:T(4,128)}, u32[]{:S(2)}) copy-start(f32[4,4,32]{2,1,0:T(4,128)} %param.18) | copy-start | bytes 6148
  39.2 18.1 %all-to-all-start.1 = ((bf16[16,96,256]{2,1,0:T(8,128)(2,1)}), bf16[16,96,256]{2,1,0:T(8,128)(2,1)}, u32[]{:S(2)}, u32[]{:S(2)}) async-start(bf16[16,96,256]{2,1,0:T(8,128)(2,1)} %shard_map.114), calls=%async_computation.1 | async-start | bytes 1572864 | tf_op jit(solution)/shard_map/all_to_all | solution.py:368
  57.3 1.0 copy-start.3
  61.8 32.2 %collective-permute-start.4 = (bf16[640,1024]{1,0:T(8,128)(2,1)}, bf16[640,1024]{1,0:T(8,128)(2,1)}, u32[]{:S(2)}, u32[]{:S(2)}) collective-permute-start(bf16[640,1024]{1,0:T(8,128)(2,1)} %get-tuple-element.42.refs_1_), channel_id=1, source_target_pairs={{0,1},{1,0},{2,3},{3,2},{4,5},{5,4},{6,7},{7,6},{8,9},{9,8},{10,11... | collective-permute-start | bytes 3932168 | tf_op jit(solution)/shard_map/ppermute | solution.py:21
  64.6 36.5 %collective-permute-start.2 = (bf16[640,1024]{1,0:T(8,128)(2,1)}, bf16[640,1024]{1,0:T(8,128)(2,1)}, u32[]{:S(2)}, u32[]{:S(2)}) collective-permute-start(bf16[640,1024]{1,0:T(8,128)(2,1)} %get-tuple-element.42.refs_1_), channel_id=1, source_target_pairs={{0,2},{1,3},{2,4},{3,5},{4,6},{5,7},{6,0},{7,1},{8,10},{9,11},{10,... | collective-permute-start | bytes 3932168 | tf_op jit(solution)/shard_map/ppermute | solution.py:13
  66.5 17.9 %collective-permute-start.3 = (bf16[320,1024]{1,0:T(8,128)(2,1)}, bf16[320,1024]{1,0:T(8,128)(2,1)S(1)}, u32[]{:S(2)}, u32[]{:S(2)}) collective-permute-start(bf16[320,1024]{1,0:T(8,128)(2,1)} %get-tuple-element.44), channel_id=1, source_target_pairs={{0,6},{1,7},{2,0},{3,1},{4,2},{5,3},{6,4},{7,5},{8,14},{9,15},{10,... | collective-permute-start | bytes 1966088 | tf_op jit(solution)/shard_map/ppermute | solution.py:17
  68.6 28.1 %collective-permute-start = (bf16[320,1024]{1,0:T(8,128)(2,1)}, bf16[320,1024]{1,0:T(8,128)(2,1)}, u32[]{:S(2)}, u32[]{:S(2)}) collective-permute-start(bf16[320,1024]{1,0:T(8,128)(2,1)} %get-tuple-element.41), channel_id=1, source_target_pairs={{0,6},{1,7},{2,0},{3,1},{4,2},{5,3},{6,4},{7,5},{8,14},{9,15},{10,... | collective-permute-start | bytes 1966088 | tf_op jit(solution)/shard_map/ppermute | solution.py:17
  94.0 36.5 %collective-permute-start.8 = (bf16[640,1024]{1,0:T(8,128)(2,1)}, bf16[640,1024]{1,0:T(8,128)(2,1)}, u32[]{:S(2)}, u32[]{:S(2)}) collective-permute-start(bf16[640,1024]{1,0:T(8,128)(2,1)} %collective-permute-done.4.refs_4_), channel_id=1, source_target_pairs={{0,2},{1,3},{2,4},{3,5},{4,6},{5,7},{6,0},{7,1},{8,10},{9,11},{10,... | collective-permute-start | bytes 3932168 | tf_op jit(solution)/shard_map/ppermute | solution.py:13
  96.8 19.5 %collective-permute-start.1 = (bf16[320,1024]{1,0:T(8,128)(2,1)}, bf16[320,1024]{1,0:T(8,128)(2,1)}, u32[]{:S(2)}, u32[]{:S(2)}) collective-permute-start(bf16[320,1024]{1,0:T(8,128)(2,1)} %collective-permute-done.refs_2_), channel_id=1, source_target_pairs={{0,1},{1,0},{2,3},{3,2},{4,5},{5,4},{6,7},{7,6},{8,9},{9,8},{10,11... | collective-permute-start | bytes 1966088 | tf_op jit(solution)/shard_map/ppermute | solution.py:21
  98.6 21.0 %collective-permute-start.6 = (bf16[320,1024]{1,0:T(8,128)(2,1)S(1)}, bf16[320,1024]{1,0:T(8,128)(2,1)}, u32[]{:S(2)}, u32[]{:S(2)}) collective-permute-start(bf16[320,1024]{1,0:T(8,128)(2,1)S(1)} %collective-permute-done.3.refs_3_), channel_id=1, source_target_pairs={{0,6},{1,7},{2,0},{3,1},{4,2},{5,3},{6,4},{7,5},{8,14},{9,15},{10,... | collective-permute-start | bytes 1966088 | tf_op jit(solution)/shard_map/ppermute | solution.py:17
  101.1 29.4 %collective-permute-start.9 = (bf16[320,1024]{1,0:T(8,128)(2,1)}, bf16[320,1024]{1,0:T(8,128)(2,1)}, u32[]{:S(2)}, u32[]{:S(2)}) collective-permute-start(bf16[320,1024]{1,0:T(8,128)(2,1)} %collective-permute-done.refs_2_), channel_id=1, source_target_pairs={{0,6},{1,7},{2,0},{3,1},{4,2},{5,3},{6,4},{7,5},{8,14},{9,15},{10,... | collective-permute-start | bytes 1966088 | tf_op jit(solution)/shard_map/ppermute | solution.py:17
  102.9 27.6 %collective-permute-start.10 = (bf16[320,1024]{1,0:T(8,128)(2,1)S(1)}, bf16[320,1024]{1,0:T(8,128)(2,1)}, u32[]{:S(2)}, u32[]{:S(2)}) collective-permute-start(bf16[320,1024]{1,0:T(8,128)(2,1)S(1)} %collective-permute-done.3.refs_3_), channel_id=1, source_target_pairs={{0,1},{1,0},{2,3},{3,2},{4,5},{5,4},{6,7},{7,6},{8,9},{9,8},{10,11... | collective-permute-start | bytes 1966088 | tf_op jit(solution)/shard_map/ppermute | solution.py:21
  112.5 1.5 %copy-start.1 = (f32[640,1024]{1,0:T(8,128)}, f32[640,1024]{1,0:T(8,128)S(1)}, u32[]{:S(2)}) copy-start(f32[640,1024]{1,0:T(8,128)S(1)} %shard_map.117.refs_7_) | copy-start | bytes 7864324
  116.2 25.5 %collective-permute-start.5 = (bf16[320,1024]{1,0:T(8,128)(2,1)}, bf16[320,1024]{1,0:T(8,128)(2,1)S(1)}, u32[]{:S(2)}, u32[]{:S(2)}) collective-permute-start(bf16[320,1024]{1,0:T(8,128)(2,1)} %collective-permute-done.1.refs_4_), channel_id=1, source_target_pairs={{0,6},{1,7},{2,0},{3,1},{4,2},{5,3},{6,4},{7,5},{8,14},{9,15},{10,... | collective-permute-start | bytes 1966088 | tf_op jit(solution)/shard_map/ppermute | solution.py:17
  119.7 22.0 %collective-permute-start.7 = (bf16[320,1024]{1,0:T(8,128)(2,1)}, bf16[320,1024]{1,0:T(8,128)(2,1)S(1)}, u32[]{:S(2)}, u32[]{:S(2)}) collective-permute-start(bf16[320,1024]{1,0:T(8,128)(2,1)} %collective-permute-done.6.refs_3_), channel_id=1, source_target_pairs={{0,1},{1,0},{2,3},{3,2},{4,5},{5,4},{6,7},{7,6},{8,9},{9,8},{10,11... | collective-permute-start | bytes 1966088 | tf_op jit(solution)/shard_map/ppermute | solution.py:21
  120.6 9.9 %copy-start.2 = (f32[640,1024]{1,0:T(8,128)S(1)}, f32[640,1024]{1,0:T(8,128)}, u32[]{:S(2)}) copy-start(f32[640,1024]{1,0:T(8,128)} %copy-done.1) | copy-start | bytes 7864324

commit v9 on v8

--- a/solution.py
+++ b/solution.py
@@ -113,7 +113,7 @@
 
 def first_parcels(own_state, parts, named, queries):
     heads, dim, _ = own_state.shape
-    slots, rows = queries.shape[1], named.shape[1]
+    slots, rows = queries.shape[0], named.shape[1]
     count = lax.axis_size("ctx")
     per_head = count // heads
     slice_rows = heads * dim // count
@@ -128,6 +128,7 @@
         sections = jnp.concatenate([sections, jnp.zeros((1, dim - slots), F32)], axis=1)
         line = lax.broadcasted_iota(jnp.int32, (8, dim), 0)
         for h in range(heads):
+            asked = q_ref[:, h, :]
             header = jnp.where(line == 3, sections, 0.0)
             for i in range(3):
                 header = jnp.where(line == i, p_ref[h : h + 1, i : i + 1], header)
@@ -136,7 +137,7 @@
                 c = h * per_head + k
                 o_ref[c, :slice_rows, :] = s_ref[h, k * slice_rows : (k + 1) * slice_rows, :]
                 o_ref[c, slice_rows + slots :, :] = header
-                o_ref[c, slice_rows : slice_rows + slots, :] = q_ref[h]
+                o_ref[c, slice_rows : slice_rows + slots, :] = asked
 
     return pl.pallas_call(
         body,
@@ -348,7 +349,7 @@
     high = lax.reduce_precision(total_decay, 8, 7)
     middle = lax.reduce_precision(total_decay - high, 8, 7)
     parts = jnp.stack([high, middle, total_decay - high - middle], axis=1)
-    asked = q_step.reshape(slots, heads, dim).transpose(1, 0, 2)
+    asked = q_step.reshape(slots, heads, dim)
     sent = first_parcels(own_state.astype(BF), parts, prompt_section.reshape(1, rows), asked)
     got = lax.all_to_all(sent, "ctx", 0, 0)
 

time: 145 us -> 145 us (level)
    unnamed x20 -> x22, local copies, waits for them, and re-layouts: 4.92 us -> 5.2 us
where the time goes in v9:
time: 145 us; the launch traced here: 144 us
  waiting for transfers between devices  56.6 us (39%)
  starting transfers between devices  32.8 us (23%)
  Pallas kernels  32.3 us (22%)
  local copies, waits for them, and re-layouts  10.6 us (7%)
  matrix products  8.63 us (6%)
  other arithmetic  2.39 us (2%)
    all_to_all x2, waiting for transfers between devices, shards(): got = lax.all_to_all(sent, 'ctx', 0, 0)  23.9 us
    ppermute x5, waiting for transfers between devices, down(): return lax.ppermute(a, 'head', [(h, (h - 2) % 8) for h in range(8)])  21 us
    pallas_call x3, Pallas kernels, project(): pl.pallas_call(body, in_specs=[pl.BlockSpec(memory_space=pltpu.SMEM)] + [...  20.9 us
    ppermute x5, starting transfers between devices, down(): return lax.ppermute(a, 'head', [(h, (h - 2) % 8) for h in range(8)])  11.9 us
    ppermute x4, waiting for transfers between devices, across(): return lax.ppermute(a, 'head', [(h, h ^ 1) for h in range(8)])  11.7 us
    all_to_all x2, starting transfers between devices, shards(): got = lax.all_to_all(sent, 'ctx', 0, 0)  10.1 us
    ppermute x4, starting transfers between devices, across(): return lax.ppermute(a, 'head', [(h, h ^ 1) for h in range(8)])  6.97 us
    unnamed x22, local copies, waits for them, and re-layouts  5.2 us
  transfers between devices with their start and end apart: 13, of which 8 were waited for; matrix products, arithmetic and copies ran while one was open for 10% of the time, Pallas kernels for 14%

profile of v9, /device:TPU:0, one launch (start us, length us, event | category | flops | bytes accessed | tf_op | source)
XLA Modules:
  0.0 144.2 jit_solution(1245238423630464578)
XLA Ops:
  0.6 0.0 copy-start
  0.6 0.0 copy-start.9
  0.7 1.1 fusion.9
  1.7 0.2 fusion.24
  1.9 0.1 subtract_exponential_fusion
  2.0 0.2 copy.23
  2.2 1.8 %multiply_convert_fusion.1 = bf16[512,4,256]{2,1,0:T(4,128)(2,1)S(1)} fusion(bf16[512,4,256]{2,1,0:T(4,128)(2,1)} %param.11, f32[512,4]{1,0:T(8,128)S(1)} %copy.23), kind=kLoop, calls=%fused_computation.1 | loop fusion | flops 1572864 | bytes 2105344 | tf_op jit(solution)/shard_map/convert_element_type | solution.py:345
  3.9 0.0 copy-done.9
  3.9 0.0 copy-start.4
  4.0 0.0 copy-start.5
  4.0 0.6 fusion.1.s_ref
  4.5 0.1 pad_maximum_fusion.1.p_ref
  4.6 0.3 copy-done.4
  4.9 0.0 copy-done.5
  4.9 1.9 %shard_map.113 = bf16[16,200,256]{2,1,0:T(8,128)(2,1)} custom-call(bf16[4,256,256]{2,1,0:T(8,128)(2,1)S(1)} %fusion.1.s_ref, f32[4,3]{1,0:T(4,128)S(1)} %pad_maximum_fusion.1.p_ref, s32[1,32]{1,0:T(1,128)S(1)} %bitcast.34, bf16[128,4,256]{2,1,0:T(4,128)(2,1)S(1)} %bitcast.30), custom_call_target="tpu_custom_call" | custom-call | bytes 3145728 | tf_op jit(solution)/shard_map/pallas_call | solution.py:142
  6.8 5.8 %all-to-all-start = ((bf16[16,200,256]{2,1,0:T(8,128)(2,1)}), bf16[16,200,256]{2,1,0:T(8,128)(2,1)}, u32[]{:S(2)}, u32[]{:S(2)}) async-start(bf16[16,200,256]{2,1,0:T(8,128)(2,1)} %shard_map.113), calls=%async_computation | async-start | bytes 3276800 | tf_op jit(solution)/shard_map/all_to_all | solution.py:354
  12.6 0.1 iota_compare_fusion
  12.7 0.0 copy-done.6
  12.7 0.0 copy-done.7
  12.7 4.7 %fusion = f32[4,256,512]{2,1,0:T(8,128)} fusion(f32[4,512]{1,0:T(4,128)S(1)} %bitcast.32, pred[512,512]{1,0:T(8,128)(4,1)S(1)} %iota_compare_fusion, bf16[512,4,256]{2,1,0:T(4,128)(2,1)S(1)} %copy-done.6, bf16[512,4,256]{2,1,0:T(4,128)(2,1)S(1)} %copy-done.7, bf16[512,4,256]{2,1,0:T(4,128)(2,1)} %param.12), kind=kOutput, calls=%fused_computation.2 | convolution fusion | flops 1078984704 | bytes 5513216 | tf_op jit(solution)/shard_map/hnm,mhe->nhe/dot_general | solution.py:363
  17.4 1.9 %copy.39.in_ref = f32[512,1024]{1,0:T(8,128)S(1)} copy(f32[512,1024]{0,1:T(8,128)} %bitcast.35) | data formatting | bytes 4194304 | tf_op jit(solution)/shard_map/reshape | solution.py:364
  19.3 1.4 %copy.40 = bf16[64,8,4,256]{3,1,2,0:T(8,128)(2,1)S(1)} copy(bf16[64,8,4,256]{3,2,1,0:T(4,128)(2,1)} %bitcast.37) | data formatting | bytes 2097152
  20.8 14.8 %all-to-all-done.got_ref = bf16[16,200,256]{2,1,0:T(8,128)(2,1)} async-done(((bf16[16,200,256]{2,1,0:T(8,128)(2,1)}), bf16[16,200,256]{2,1,0:T(8,128)(2,1)}, u32[]{:S(2)}, u32[]{:S(2)}) %all-to-all-start) | async-done | bytes 1638432 | tf_op jit(solution)/shard_map/all_to_all | solution.py:354
  35.6 3.5 %shard_map.114 = bf16[16,96,256]{2,1,0:T(8,128)(2,1)} custom-call(bf16[16,200,256]{2,1,0:T(8,128)(2,1)} %all-to-all-done.got_ref), custom_call_target="tpu_custom_call" | custom-call | flops 1073741824 | bytes 6291456 | tf_op jit(solution)/shard_map/pallas_call | solution.py:212
  39.1 4.3 %all-to-all-start.1 = ((bf16[16,96,256]{2,1,0:T(8,128)(2,1)}), bf16[16,96,256]{2,1,0:T(8,128)(2,1)}, u32[]{:S(2)}, u32[]{:S(2)}) async-start(bf16[16,96,256]{2,1,0:T(8,128)(2,1)} %shard_map.114), calls=%async_computation.1 | async-start | bytes 1572864 | tf_op jit(solution)/shard_map/all_to_all | solution.py:369
  43.5 0.0 copy-done.8
  43.5 0.1 copy.29
  43.6 2.3 %convolution_bitcast_fusion = f32[32,4,4,256]{3,1,2,0:T(4,128)} fusion(bf16[32,4,4,256]{3,2,1,0:T(4,128)(2,1)S(1)} %copy-done, bf16[32,4,4,256]{3,2,1,0:T(4,128)(2,1)} %param.15, bf16[32,4,4,256]{3,2,1,0:T(4,128)(2,1)} %param.17, f32[32,4,4]{2,1,0:T(4,128)S(1)} %copy.29, pred[4,4]{1,0:T(4,128)(4,1)S(1)} %iota_compare_fusion.3), kind=kOutput, calls=%fused_computation.5 | convolution fusion | flops 2105344 | bytes 1312784 | tf_op jit(solution)/shard_map/rhtu,ruhe->rthe/dot_general | solution.py:383
  45.9 1.2 copy.32
  47.1 0.9 copy.41
  48.0 0.1 copy.33
  48.1 9.1 %all-to-all-done.1.got_ref = bf16[16,96,256]{2,1,0:T(8,128)(2,1)} async-done(((bf16[16,96,256]{2,1,0:T(8,128)(2,1)}), bf16[16,96,256]{2,1,0:T(8,128)(2,1)}, u32[]{:S(2)}, u32[]{:S(2)}) %all-to-all-start.1) | async-done | bytes 786464 | tf_op jit(solution)/shard_map/all_to_all | solution.py:369
  57.2 1.0 copy-done.3
  58.3 3.4 %shard_map.115 = (bf16[640,1024]{1,0:T(8,128)(2,1)}, bf16[320,1024]{1,0:T(8,128)(2,1)}, bf16[320,1024]{1,0:T(8,128)(2,1)}) custom-call(bf16[512,1024]{1,0:T(8,128)(2,1)S(1)} %bitcast.27, f32[512,1024]{1,0:T(8,128)S(1)} %copy.39.in_ref, f32[4,512]{1,0:T(4,128)S(1)} %bitcast.33, bf16[16,96,256]{2,1,0:T(8,128)(2,1)} %all-to-all-done.1.got_ref, ...), custom_call_target="tpu_custom_call" | custom-call | flops 268435456 | bytes 6291456 | tf_op jit(solution)/shard_map/pallas_call | solution.py:269
  61.7 2.8 %collective-permute-start.4 = (bf16[640,1024]{1,0:T(8,128)(2,1)}, bf16[640,1024]{1,0:T(8,128)(2,1)}, u32[]{:S(2)}, u32[]{:S(2)}) collective-permute-start(bf16[640,1024]{1,0:T(8,128)(2,1)} %get-tuple-element.42.refs_1_), channel_id=1, source_target_pairs={{0,1},{1,0},{2,3},{3,2},{4,5},{5,4},{6,7},{7,6},{8,9},{9,8},{10,11... | collective-permute-start | bytes 3932168 | tf_op jit(solution)/shard_map/ppermute | solution.py:21
  64.5 1.9 %collective-permute-start.2 = (bf16[640,1024]{1,0:T(8,128)(2,1)}, bf16[640,1024]{1,0:T(8,128)(2,1)}, u32[]{:S(2)}, u32[]{:S(2)}) collective-permute-start(bf16[640,1024]{1,0:T(8,128)(2,1)} %get-tuple-element.42.refs_1_), channel_id=1, source_target_pairs={{0,2},{1,3},{2,4},{3,5},{4,6},{5,7},{6,0},{7,1},{8,10},{9,11},{10,... | collective-permute-start | bytes 3932168 | tf_op jit(solution)/shard_map/ppermute | solution.py:13
  66.4 2.1 %collective-permute-start.3 = (bf16[320,1024]{1,0:T(8,128)(2,1)}, bf16[320,1024]{1,0:T(8,128)(2,1)S(1)}, u32[]{:S(2)}, u32[]{:S(2)}) collective-permute-start(bf16[320,1024]{1,0:T(8,128)(2,1)} %get-tuple-element.44), channel_id=1, source_target_pairs={{0,6},{1,7},{2,0},{3,1},{4,2},{5,3},{6,4},{7,5},{8,14},{9,15},{10,... | collective-permute-start | bytes 1966088 | tf_op jit(solution)/shard_map/ppermute | solution.py:17
  68.5 2.0 %collective-permute-start = (bf16[320,1024]{1,0:T(8,128)(2,1)}, bf16[320,1024]{1,0:T(8,128)(2,1)}, u32[]{:S(2)}, u32[]{:S(2)}) collective-permute-start(bf16[320,1024]{1,0:T(8,128)(2,1)} %get-tuple-element.41), channel_id=1, source_target_pairs={{0,6},{1,7},{2,0},{3,1},{4,2},{5,3},{6,4},{7,5},{8,14},{9,15},{10,... | collective-permute-start | bytes 1966088 | tf_op jit(solution)/shard_map/ppermute | solution.py:17
  70.5 4.4 %shard_map.116.refs_6_ = f32[640,1024]{1,0:T(8,128)S(1)} custom-call(s32[1]{0:T(128)} %bitcast.10.refs_0_, bf16[640,1024]{1,0:T(8,128)(2,1)} %get-tuple-element.42.refs_1_, bf16[8192,1024]{1,0:T(8,128)(2,1)} %refs_6_.1), custom_call_target="tpu_custom_call" | custom-call | flops 1310720 | bytes 1024 | tf_op jit(solution)/shard_map/pallas_call | solution.py:94
  75.0 9.3 %collective-permute-done.3.refs_3_ = bf16[320,1024]{1,0:T(8,128)(2,1)S(1)} collective-permute-done((bf16[320,1024]{1,0:T(8,128)(2,1)}, bf16[320,1024]{1,0:T(8,128)(2,1)S(1)}, u32[]{:S(2)}, u32[]{:S(2)}) %collective-permute-start.3) | collective-permute-done | bytes 655392 | tf_op jit(solution)/shard_map/ppermute | solution.py:17
  84.3 9.6 %collective-permute-done.4.refs_4_ = bf16[640,1024]{1,0:T(8,128)(2,1)} collective-permute-done((bf16[640,1024]{1,0:T(8,128)(2,1)}, bf16[640,1024]{1,0:T(8,128)(2,1)}, u32[]{:S(2)}, u32[]{:S(2)}) %collective-permute-start.4) | collective-permute-done | bytes 1310752 | tf_op jit(solution)/shard_map/ppermute | solution.py:21
  93.9 1.9 %collective-permute-start.8 = (bf16[640,1024]{1,0:T(8,128)(2,1)}, bf16[640,1024]{1,0:T(8,128)(2,1)}, u32[]{:S(2)}, u32[]{:S(2)}) collective-permute-start(bf16[640,1024]{1,0:T(8,128)(2,1)} %collective-permute-done.4.refs_4_), channel_id=1, source_target_pairs={{0,2},{1,3},{2,4},{3,5},{4,6},{5,7},{6,0},{7,1},{8,10},{9,11},{10,... | collective-permute-start | bytes 3932168 | tf_op jit(solution)/shard_map/ppermute | solution.py:13
  95.8 0.8 collective-permute-done.refs_2_
  96.6 1.9 %collective-permute-start.1 = (bf16[320,1024]{1,0:T(8,128)(2,1)}, bf16[320,1024]{1,0:T(8,128)(2,1)}, u32[]{:S(2)}, u32[]{:S(2)}) collective-permute-start(bf16[320,1024]{1,0:T(8,128)(2,1)} %collective-permute-done.refs_2_), channel_id=1, source_target_pairs={{0,1},{1,0},{2,3},{3,2},{4,5},{5,4},{6,7},{7,6},{8,9},{9,8},{10,11... | collective-permute-start | bytes 1966088 | tf_op jit(solution)/shard_map/ppermute | solution.py:21
  98.5 2.3 %collective-permute-start.6 = (bf16[320,1024]{1,0:T(8,128)(2,1)S(1)}, bf16[320,1024]{1,0:T(8,128)(2,1)}, u32[]{:S(2)}, u32[]{:S(2)}) collective-permute-start(bf16[320,1024]{1,0:T(8,128)(2,1)S(1)} %collective-permute-done.3.refs_3_), channel_id=1, source_target_pairs={{0,6},{1,7},{2,0},{3,1},{4,2},{5,3},{6,4},{7,5},{8,14},{9,15},{10,... | collective-permute-start | bytes 1966088 | tf_op jit(solution)/shard_map/ppermute | solution.py:17
  100.9 0.1 pad_add_fusion.refs_0_
  101.0 0.0 collective-permute-done.2.refs_1_
  101.0 2.0 %collective-permute-start.9 = (bf16[320,1024]{1,0:T(8,128)(2,1)}, bf16[320,1024]{1,0:T(8,128)(2,1)}, u32[]{:S(2)}, u32[]{:S(2)}) collective-permute-start(bf16[320,1024]{1,0:T(8,128)(2,1)} %collective-permute-done.refs_2_), channel_id=1, source_target_pairs={{0,6},{1,7},{2,0},{3,1},{4,2},{5,3},{6,4},{7,5},{8,14},{9,15},{10,... | collective-permute-start | bytes 1966088 | tf_op jit(solution)/shard_map/ppermute | solution.py:17
  103.0 1.5 %collective-permute-start.10 = (bf16[320,1024]{1,0:T(8,128)(2,1)S(1)}, bf16[320,1024]{1,0:T(8,128)(2,1)}, u32[]{:S(2)}, u32[]{:S(2)}) collective-permute-start(bf16[320,1024]{1,0:T(8,128)(2,1)S(1)} %collective-permute-done.3.refs_3_), channel_id=1, source_target_pairs={{0,1},{1,0},{2,3},{3,2},{4,5},{5,4},{6,7},{7,6},{8,9},{9,8},{10,11... | collective-permute-start | bytes 1966088 | tf_op jit(solution)/shard_map/ppermute | solution.py:21
  104.4 8.1 %shard_map.117.refs_7_ = f32[640,1024]{1,0:T(8,128)S(1)} custom-call(s32[3]{0:T(128)S(1)} %pad_add_fusion.refs_0_, bf16[640,1024]{1,0:T(8,128)(2,1)} %collective-permute-done.2.refs_1_, bf16[320,1024]{1,0:T(8,128)(2,1)} %collective-permute-done.refs_2_, bf16[320,1024]{1,0:T(8,128)(2,1)S(1)} %collective-permute-done.3.refs_3_, ...), custom_call_target="tpu_custom_call" | custom-call | flops 3932160 | bytes 1024 | tf_op jit(solution)/shard_map/pallas_call | solution.py:94
  112.6 1.5 %copy-done.1 = f32[640,1024]{1,0:T(8,128)} copy-done((f32[640,1024]{1,0:T(8,128)}, f32[640,1024]{1,0:T(8,128)S(1)}, u32[]{:S(2)}) %copy-start.1) | copy-done | bytes 2621464
  114.1 2.1 %collective-permute-done.1.refs_4_ = bf16[320,1024]{1,0:T(8,128)(2,1)} collective-permute-done((bf16[320,1024]{1,0:T(8,128)(2,1)}, bf16[320,1024]{1,0:T(8,128)(2,1)}, u32[]{:S(2)}, u32[]{:S(2)}) %collective-permute-start.1) | collective-permute-done | bytes 655392 | tf_op jit(solution)/shard_map/ppermute | solution.py:21
  116.1 3.4 %collective-permute-start.5 = (bf16[320,1024]{1,0:T(8,128)(2,1)}, bf16[320,1024]{1,0:T(8,128)(2,1)S(1)}, u32[]{:S(2)}, u32[]{:S(2)}) collective-permute-start(bf16[320,1024]{1,0:T(8,128)(2,1)} %collective-permute-done.1.refs_4_), channel_id=1, source_target_pairs={{0,6},{1,7},{2,0},{3,1},{4,2},{5,3},{6,4},{7,5},{8,14},{9,15},{10,... | collective-permute-start | bytes 1966088 | tf_op jit(solution)/shard_map/ppermute | solution.py:17
  119.6 0.0 collective-permute-done.6.refs_3_
  119.6 0.8 collective-permute-start.7
  120.4 0.1 pad_add_fusion.1.refs_0_
  120.5 1.9 %constant_dynamic-slice_fusion.refs_2_ = bf16[1024,1024]{1,0:T(8,128)(2,1)S(1)} fusion(bf16[8192,1024]{1,0:T(8,128)(2,1)} %refs_6_.1, s32[]{:T(128)S(6)} %select_n.52), kind=kLoop, calls=%fused_computation.43 | loop fusion | bytes 4194308 | tf_op jit(solution)/shard_map/dynamic_slice | solution.py:311
  122.4 8.0 %collective-permute-done.9.refs_2_ = bf16[320,1024]{1,0:T(8,128)(2,1)} collective-permute-done((bf16[320,1024]{1,0:T(8,128)(2,1)}, bf16[320,1024]{1,0:T(8,128)(2,1)}, u32[]{:S(2)}, u32[]{:S(2)}) %collective-permute-start.9) | collective-permute-done | bytes 655392 | tf_op jit(solution)/shard_map/ppermute | solution.py:17
  130.4 0.0 collective-permute-done.10.refs_5_
  130.4 0.0 collective-permute-done.8.refs_1_
  130.4 8.3 %shard_map.118.refs_3_ = f32[640,1024]{1,0:T(8,128)S(1)} custom-call(s32[3]{0:T(128)S(1)} %pad_add_fusion.1.refs_0_, bf16[640,1024]{1,0:T(8,128)(2,1)} %collective-permute-done.8.refs_1_, bf16[320,1024]{1,0:T(8,128)(2,1)} %collective-permute-done.9.refs_2_, bf16[320,1024]{1,0:T(8,128)(2,1)} %collective-permute-done.6.refs_3_, ...), custom_call_target="tpu_custom_call" | custom-call | flops 3932160 | bytes 1024 | tf_op jit(solution)/shard_map/pallas_call | solution.py:94
  138.7 2.9 %collective-permute-done.5.refs_0_ = bf16[320,1024]{1,0:T(8,128)(2,1)S(1)} collective-permute-done((bf16[320,1024]{1,0:T(8,128)(2,1)}, bf16[320,1024]{1,0:T(8,128)(2,1)S(1)}, u32[]{:S(2)}, u32[]{:S(2)}) %collective-permute-start.5) | collective-permute-done | bytes 655392 | tf_op jit(solution)/shard_map/ppermute | solution.py:17
  141.6 0.0 collective-permute-done.7.refs_1_
  141.6 2.6 %shard_map.119 = (bf16[512,1024]{1,0:T(8,128)(2,1)}, bf16[32,4,1024]{2,1,0:T(4,128)(2,1)}) custom-call(bf16[320,1024]{1,0:T(8,128)(2,1)S(1)} %collective-permute-done.5.refs_0_, bf16[320,1024]{1,0:T(8,128)(2,1)S(1)} %collective-permute-done.7.refs_1_, bf16[1024,1024]{1,0:T(8,128)(2,1)S(1)} %constant_dynamic-slice_fusion.refs_2_, ...), custom_call_target="tpu_custom_call" | custom-call | flops 1310720 | bytes 1024 | tf_op jit(solution)/shard_map/pallas_call | solution.py:86
  (11 shorter events, 0.1 us)
Async XLA Ops:
  0.6 43.0 %copy-start = (bf16[32,4,4,256]{3,2,1,0:T(4,128)(2,1)S(1)}, bf16[32,4,4,256]{3,2,1,0:T(4,128)(2,1)}, u32[]{:S(2)}) copy-start(bf16[32,4,4,256]{3,2,1,0:T(4,128)(2,1)} %param.16) | copy-start | bytes 786436
  0.6 3.3 %copy-start.9 = (bf16[512,4,256]{2,1,0:T(4,128)(2,1)S(1)}, bf16[512,4,256]{2,1,0:T(4,128)(2,1)}, u32[]{:S(2)}) copy-start(bf16[512,4,256]{2,1,0:T(4,128)(2,1)} %param.12) | copy-start | bytes 3145732
  3.9 1.0 copy-start.4
  4.0 0.9 copy-start.5
  6.8 5.9 %copy-start.6 = (bf16[512,4,256]{2,1,0:T(4,128)(2,1)S(1)}, bf16[512,4,256]{2,1,0:T(4,128)(2,1)}, u32[]{:S(2)}) copy-start(bf16[512,4,256]{2,1,0:T(4,128)(2,1)} %param.11) | copy-start | bytes 3145732
  6.8 5.9 %copy-start.7 = (bf16[512,4,256]{2,1,0:T(4,128)(2,1)S(1)}, bf16[512,4,256]{2,1,0:T(4,128)(2,1)}, u32[]{:S(2)}) copy-start(bf16[512,4,256]{2,1,0:T(4,128)(2,1)} %param.10) | copy-start | bytes 3145732
  6.8 28.8 %all-to-all-start = ((bf16[16,200,256]{2,1,0:T(8,128)(2,1)}), bf16[16,200,256]{2,1,0:T(8,128)(2,1)}, u32[]{:S(2)}, u32[]{:S(2)}) async-start(bf16[16,200,256]{2,1,0:T(8,128)(2,1)} %shard_map.113), calls=%async_computation | async-start | bytes 3276800 | tf_op jit(solution)/shard_map/all_to_all | solution.py:354
  35.6 7.8 %copy-start.8 = (f32[4,4,32]{2,1,0:T(4,128)S(1)}, f32[4,4,32]{2,1,0:T(4,128)}, u32[]{:S(2)}) copy-start(f32[4,4,32]{2,1,0:T(4,128)} %param.18) | copy-start | bytes 6148
  39.1 18.1 %all-to-all-start.1 = ((bf16[16,96,256]{2,1,0:T(8,128)(2,1)}), bf16[16,96,256]{2,1,0:T(8,128)(2,1)}, u32[]{:S(2)}, u32[]{:S(2)}) async-start(bf16[16,96,256]{2,1,0:T(8,128)(2,1)} %shard_map.114), calls=%async_computation.1 | async-start | bytes 1572864 | tf_op jit(solution)/shard_map/all_to_all | solution.py:369
  57.2 1.0 copy-start.3
  61.7 32.2 %collective-permute-start.4 = (bf16[640,1024]{1,0:T(8,128)(2,1)}, bf16[640,1024]{1,0:T(8,128)(2,1)}, u32[]{:S(2)}, u32[]{:S(2)}) collective-permute-start(bf16[640,1024]{1,0:T(8,128)(2,1)} %get-tuple-element.42.refs_1_), channel_id=1, source_target_pairs={{0,1},{1,0},{2,3},{3,2},{4,5},{5,4},{6,7},{7,6},{8,9},{9,8},{10,11... | collective-permute-start | bytes 3932168 | tf_op jit(solution)/shard_map/ppermute | solution.py:21
  64.5 36.5 %collective-permute-start.2 = (bf16[640,1024]{1,0:T(8,128)(2,1)}, bf16[640,1024]{1,0:T(8,128)(2,1)}, u32[]{:S(2)}, u32[]{:S(2)}) collective-permute-start(bf16[640,1024]{1,0:T(8,128)(2,1)} %get-tuple-element.42.refs_1_), channel_id=1, source_target_pairs={{0,2},{1,3},{2,4},{3,5},{4,6},{5,7},{6,0},{7,1},{8,10},{9,11},{10,... | collective-permute-start | bytes 3932168 | tf_op jit(solution)/shard_map/ppermute | solution.py:13
  66.4 17.9 %collective-permute-start.3 = (bf16[320,1024]{1,0:T(8,128)(2,1)}, bf16[320,1024]{1,0:T(8,128)(2,1)S(1)}, u32[]{:S(2)}, u32[]{:S(2)}) collective-permute-start(bf16[320,1024]{1,0:T(8,128)(2,1)} %get-tuple-element.44), channel_id=1, source_target_pairs={{0,6},{1,7},{2,0},{3,1},{4,2},{5,3},{6,4},{7,5},{8,14},{9,15},{10,... | collective-permute-start | bytes 1966088 | tf_op jit(solution)/shard_map/ppermute | solution.py:17
  68.5 28.1 %collective-permute-start = (bf16[320,1024]{1,0:T(8,128)(2,1)}, bf16[320,1024]{1,0:T(8,128)(2,1)}, u32[]{:S(2)}, u32[]{:S(2)}) collective-permute-start(bf16[320,1024]{1,0:T(8,128)(2,1)} %get-tuple-element.41), channel_id=1, source_target_pairs={{0,6},{1,7},{2,0},{3,1},{4,2},{5,3},{6,4},{7,5},{8,14},{9,15},{10,... | collective-permute-start | bytes 1966088 | tf_op jit(solution)/shard_map/ppermute | solution.py:17
  93.9 36.5 %collective-permute-start.8 = (bf16[640,1024]{1,0:T(8,128)(2,1)}, bf16[640,1024]{1,0:T(8,128)(2,1)}, u32[]{:S(2)}, u32[]{:S(2)}) collective-permute-start(bf16[640,1024]{1,0:T(8,128)(2,1)} %collective-permute-done.4.refs_4_), channel_id=1, source_target_pairs={{0,2},{1,3},{2,4},{3,5},{4,6},{5,7},{6,0},{7,1},{8,10},{9,11},{10,... | collective-permute-start | bytes 3932168 | tf_op jit(solution)/shard_map/ppermute | solution.py:13
  96.6 19.5 %collective-permute-start.1 = (bf16[320,1024]{1,0:T(8,128)(2,1)}, bf16[320,1024]{1,0:T(8,128)(2,1)}, u32[]{:S(2)}, u32[]{:S(2)}) collective-permute-start(bf16[320,1024]{1,0:T(8,128)(2,1)} %collective-permute-done.refs_2_), channel_id=1, source_target_pairs={{0,1},{1,0},{2,3},{3,2},{4,5},{5,4},{6,7},{7,6},{8,9},{9,8},{10,11... | collective-permute-start | bytes 1966088 | tf_op jit(solution)/shard_map/ppermute | solution.py:21
  98.5 21.0 %collective-permute-start.6 = (bf16[320,1024]{1,0:T(8,128)(2,1)S(1)}, bf16[320,1024]{1,0:T(8,128)(2,1)}, u32[]{:S(2)}, u32[]{:S(2)}) collective-permute-start(bf16[320,1024]{1,0:T(8,128)(2,1)S(1)} %collective-permute-done.3.refs_3_), channel_id=1, source_target_pairs={{0,6},{1,7},{2,0},{3,1},{4,2},{5,3},{6,4},{7,5},{8,14},{9,15},{10,... | collective-permute-start | bytes 1966088 | tf_op jit(solution)/shard_map/ppermute | solution.py:17
  101.0 29.4 %collective-permute-start.9 = (bf16[320,1024]{1,0:T(8,128)(2,1)}, bf16[320,1024]{1,0:T(8,128)(2,1)}, u32[]{:S(2)}, u32[]{:S(2)}) collective-permute-start(bf16[320,1024]{1,0:T(8,128)(2,1)} %collective-permute-done.refs_2_), channel_id=1, source_target_pairs={{0,6},{1,7},{2,0},{3,1},{4,2},{5,3},{6,4},{7,5},{8,14},{9,15},{10,... | collective-permute-start | bytes 1966088 | tf_op jit(solution)/shard_map/ppermute | solution.py:17
  103.0 27.4 %collective-permute-start.10 = (bf16[320,1024]{1,0:T(8,128)(2,1)S(1)}, bf16[320,1024]{1,0:T(8,128)(2,1)}, u32[]{:S(2)}, u32[]{:S(2)}) collective-permute-start(bf16[320,1024]{1,0:T(8,128)(2,1)S(1)} %collective-permute-done.3.refs_3_), channel_id=1, source_target_pairs={{0,1},{1,0},{2,3},{3,2},{4,5},{5,4},{6,7},{7,6},{8,9},{9,8},{10,11... | collective-permute-start | bytes 1966088 | tf_op jit(solution)/shard_map/ppermute | solution.py:21
  112.6 1.5 %copy-start.1 = (f32[640,1024]{1,0:T(8,128)}, f32[640,1024]{1,0:T(8,128)S(1)}, u32[]{:S(2)}) copy-start(f32[640,1024]{1,0:T(8,128)S(1)} %shard_map.117.refs_7_) | copy-start | bytes 7864324
  116.1 25.5 %collective-permute-start.5 = (bf16[320,1024]{1,0:T(8,128)(2,1)}, bf16[320,1024]{1,0:T(8,128)(2,1)S(1)}, u32[]{:S(2)}, u32[]{:S(2)}) collective-permute-start(bf16[320,1024]{1,0:T(8,128)(2,1)} %collective-permute-done.1.refs_4_), channel_id=1, source_target_pairs={{0,6},{1,7},{2,0},{3,1},{4,2},{5,3},{6,4},{7,5},{8,14},{9,15},{10,... | collective-permute-start | bytes 1966088 | tf_op jit(solution)/shard_map/ppermute | solution.py:17
  119.6 22.0 %collective-permute-start.7 = (bf16[320,1024]{1,0:T(8,128)(2,1)}, bf16[320,1024]{1,0:T(8,128)(2,1)S(1)}, u32[]{:S(2)}, u32[]{:S(2)}) collective-permute-start(bf16[320,1024]{1,0:T(8,128)(2,1)} %collective-permute-done.6.refs_3_), channel_id=1, source_target_pairs={{0,1},{1,0},{2,3},{3,2},{4,5},{5,4},{6,7},{7,6},{8,9},{9,8},{10,11... | collective-permute-start | bytes 1966088 | tf_op jit(solution)/shard_map/ppermute | solution.py:21
  120.5 9.9 %copy-start.2 = (f32[640,1024]{1,0:T(8,128)S(1)}, f32[640,1024]{1,0:T(8,128)}, u32[]{:S(2)}) copy-start(f32[640,1024]{1,0:T(8,128)} %copy-done.1) | copy-start | bytes 7864324
